TPU v7x, 32 devices: a whole 2x2x4 slice. The times are simulated.
32 devices in a mesh: dp: 2 (over y), wide: 16 (over z, x, core).
Axes of the slice: x: 2, y: 2, z: 4, core: 2. Of those that a mesh axis runs over, the one named last changes fastest.
Arguments:
- inputs: bfloat16 [16384, 1024], P(('dp', 'wide')), may hold values from -6 to 6
- out_grad: bfloat16 [16384, 1024], P(('dp', 'wide')), may hold values from -6 to 6
- doc_lengths: int32 [2, 16], replicated, may hold values from 1 to 1024, 8192 in all within a row
- step_count: int32 [1], replicated, may hold values from 2 to 20
- qkv_weight: float32 [1024, 3072], P('wide'), may hold values from -0.1875 to 0.1875
- qkv_first: float32 [1024, 3072], P('wide'), may hold values from -0.00018310547 to 0.00018310547
- qkv_second: float32 [1024, 3072], P('wide'), may hold values from 8.0917345e-10 to 1.2930909e-08
- out_weight: float32 [1024, 1024], P('wide'), may hold values from -0.375 to 0.375
- out_first: float32 [1024, 1024], P('wide'), may hold values from -0.00018310547 to 0.00018310547
- out_second: float32 [1024, 1024], P('wide'), may hold values from 8.0917345e-10 to 1.2930909e-08
- fc1_weight: float32 [1024, 4096], P(None, 'wide'), may hold values from -0.1875 to 0.1875
- fc1_first: float32 [1024, 4096], P(None, 'wide'), may hold values from -0.00018310547 to 0.00018310547
- fc1_second: float32 [1024, 4096], P(None, 'wide'), may hold values from 8.0917345e-10 to 1.2930909e-08
- fc2_weight: float32 [4096, 1024], P('wide'), may hold values from -0.09375 to 0.09375
- fc2_first: float32 [4096, 1024], P('wide'), may hold values from -0.00018310547 to 0.00018310547
- fc2_second: float32 [4096, 1024], P('wide'), may hold values from 8.0917345e-10 to 1.2930909e-08
- model_vectors: float32 [10, 1024], P(None, 'wide'), may hold values from -0.4 to 1.3
- vectors_first: float32 [10, 1024], P(None, 'wide'), may hold values from -0.00018310547 to 0.00018310547
- vectors_second: float32 [10, 1024], P(None, 'wide'), may hold values from 8.0917345e-10 to 1.2930909e-08
- hidden_vectors: float32 [3, 4096], P(None, 'wide'), may hold values from -0.4 to 1.3
- hidden_first: float32 [3, 4096], P(None, 'wide'), may hold values from -0.00018310547 to 0.00018310547
- hidden_second: float32 [3, 4096], P(None, 'wide'), may hold values from 8.0917345e-10 to 1.2930909e-08
- head_scale: float32 [16], replicated, may hold values from 0.5 to 1.5
- head_first: float32 [16], replicated, may hold values from -0.00018310547 to 0.00018310547
- head_second: float32 [16], replicated, may hold values from 8.0917345e-10 to 1.2930909e-08
Outputs:
- output: bfloat16 [16384, 1024], P(('dp', 'wide'))
- input_grad: float32 [16384, 1024], P(('dp', 'wide'))
- grad_norm: float32 [1], replicated
- qkv_first_new: float32 [1024, 3072], P('wide')
- qkv_second_new: float32 [1024, 3072], P('wide')
- qkv_weight_new: float32 [1024, 3072], P('wide')
- out_first_new: float32 [1024, 1024], P('wide')
- out_second_new: float32 [1024, 1024], P('wide')
- out_weight_new: float32 [1024, 1024], P('wide')
- fc1_first_new: float32 [1024, 4096], P(None, 'wide')
- fc1_second_new: float32 [1024, 4096], P(None, 'wide')
- fc1_weight_new: float32 [1024, 4096], P(None, 'wide')
- fc2_first_new: float32 [4096, 1024], P('wide')
- fc2_second_new: float32 [4096, 1024], P('wide')
- fc2_weight_new: float32 [4096, 1024], P('wide')
- vectors_first_new: float32 [10, 1024], P(None, 'wide')
- vectors_second_new: float32 [10, 1024], P(None, 'wide')
- vectors_new: float32 [10, 1024], P(None, 'wide')
- hidden_first_new: float32 [3, 4096], P(None, 'wide')
- hidden_second_new: float32 [3, 4096], P(None, 'wide')
- hidden_new: float32 [3, 4096], P(None, 'wide')
- head_first_new: float32 [16], replicated
- head_second_new: float32 [16], replicated
- head_new: float32 [16], replicated
Inputs may be any that keep to these rules, and one draw needn't show every extreme that they name: `doc_lengths`: each row's 16 lengths sum to 8192, and the longest of each row is 1024.
All inputs are finite; a program needn't handle non-finite values.
Results may differ from a plain program's by a relative error of at most 0.0095.
The roundings to bfloat16 on the way count: a program that leaves them out, or rounds other values in their place, can miss the bound.
Values may be sent and summed in bfloat16 or wider, within the bound.
A program may use at most 256 MiB of HBM per device.

v0:
```python
import jax
import jax.numpy as jnp
from jax import lax
from jax.sharding import PartitionSpec as P

DOC_MOST = 1024


norm_epsilon = 1e-05
clip_limit = 1.0
first_decay = 0.9
second_decay = 0.98
adam_epsilon = 1e-08
matrix_rate = 0.1
vector_rate = 0.4
weight_decay = 0.1
masked_score = -1e30


def from_behind(shard, axis, by):
    count = lax.axis_size(axis)
    pairs = [(i, i + by) for i in range(count) if 0 <= i + by < count]
    return lax.ppermute(shard, axis, pairs)


def layer_norm(values_in, gain, shift):
    center = values_in - jnp.mean(values_in, axis=-1, keepdims=True)
    variance = jnp.mean(center * center, axis=-1, keepdims=True)
    scale = lax.rsqrt(variance + norm_epsilon)
    normed = center * scale
    return (normed * gain + shift, normed, scale)


def norm_back(grad, normed, scale, gain):
    scaled = grad * gain
    mean_plain = jnp.mean(scaled, axis=-1, keepdims=True)
    mean_cross = jnp.mean(scaled * normed, axis=-1, keepdims=True)
    return scale * (scaled - mean_plain - normed * mean_cross)


def middle_forward(activated, first_mean, second_mean, gain, shift):
    scale = lax.rsqrt(second_mean - first_mean * first_mean + norm_epsilon)
    normed = (activated - first_mean) * scale
    return (normed * gain + shift, normed, scale)


def exact_gelu(values_in):
    return jax.nn.gelu(values_in, approximate=False)


def doc_labels(doc_lengths, start, count, row_length):
    doc_count = doc_lengths.shape[1]
    places = start + jnp.arange(count, dtype=jnp.int32)
    row_number = start // row_length
    ends = jnp.cumsum(doc_lengths, axis=1)
    row_ends = lax.dynamic_slice_in_dim(ends, jnp.maximum(row_number, 0), 1, 0)[0]
    within = places - row_number * row_length
    document = jnp.sum((within[:, None] >= row_ends[None, :]).astype(jnp.int32), axis=1)
    return (row_number * doc_count + document, places)


def adam_step(grad, weight, first, second, step, rate, decay):
    first_new = first_decay * first + (1.0 - first_decay) * grad
    second_new = second_decay * second + (1.0 - second_decay) * grad * grad
    fix_one = 1.0 - jnp.power(jnp.float32(first_decay), step)
    fix_two = 1.0 - jnp.power(jnp.float32(second_decay), step)
    direction = first_new / fix_one / (jnp.sqrt(second_new / fix_two) + adam_epsilon)
    weight_new = weight - rate * (direction + decay * weight)
    return (first_new, second_new, weight_new)


def body(
    inputs,
    out_grad,
    doc_lengths,
    step_count,
    qkv_weight,
    qkv_first,
    qkv_second,
    out_weight,
    out_first,
    out_second,
    fc1_weight,
    fc1_first,
    fc1_second,
    fc2_weight,
    fc2_first,
    fc2_second,
    model_vectors,
    vectors_first,
    vectors_second,
    hidden_vectors,
    hidden_first,
    hidden_second,
    head_scale,
    head_first,
    head_second,
):
    tokens_dev = inputs.shape[0]
    width = inputs.shape[1]
    heads_count = head_scale.shape[0]
    head_size = width // heads_count
    row_length = tokens_dev * lax.axis_size("wide")
    key_span = (DOC_MOST + tokens_dev - 2) // tokens_dev
    score_scale = head_size ** (-0.5)
    block_index = lax.axis_index("dp") * lax.axis_size("wide") + lax.axis_index("wide")
    first_token = block_index * tokens_dev
    qkv_full, out_full, vector_full = (
        lax.all_gather(qkv_weight.astype(jnp.bfloat16), "wide", axis=0, tiled=True),
        lax.all_gather(out_weight.astype(jnp.bfloat16), "wide", axis=0, tiled=True),
        lax.all_gather(model_vectors.astype(jnp.bfloat16), "wide", axis=1, tiled=True),
    )
    vectors = vector_full.astype(jnp.float32)
    heads_low = lax.optimization_barrier(head_scale.astype(jnp.bfloat16)).astype(jnp.float32)
    tokens_in = inputs.astype(jnp.float32)
    normed_in, hat_in, scale_in = layer_norm(tokens_in, vectors[0], vectors[3])
    normed_low = normed_in.astype(jnp.bfloat16)
    projected = jnp.dot(normed_low, qkv_full, preferred_element_type=jnp.float32)
    queries = (projected[:, :width] + vectors[4]).astype(jnp.bfloat16)
    keys_local = projected[:, width : 2 * width].astype(jnp.bfloat16)
    values_local = (projected[:, 2 * width :] + vectors[5]).astype(jnp.bfloat16)
    local_pair = jnp.stack([keys_local, values_local])
    pair_list = [local_pair]
    label_list = []
    place_list = []
    for shift_step in range(key_span + 1):
        labels_here, places_here = doc_labels(
            doc_lengths, first_token - shift_step * tokens_dev, tokens_dev, row_length
        )
        label_list.append(labels_here)
        place_list.append(places_here)
        if shift_step > 0:
            pair_list.append(from_behind(local_pair, "wide", shift_step))
    query_labels = label_list[0]
    query_places = place_list[0]
    key_labels = jnp.concatenate(label_list, axis=0)
    key_places = jnp.concatenate(place_list, axis=0)
    pairs_all = jnp.concatenate(pair_list, axis=1)
    keys_all = pairs_all[0].reshape(-1, heads_count, head_size)
    values_all = pairs_all[1].reshape(-1, heads_count, head_size)
    allowed = (query_labels[:, None] == key_labels[None, :]) & (
        key_places[None, :] <= query_places[:, None]
    )
    queries_split = queries.reshape(tokens_dev, heads_count, head_size)

    def masked_scores():
        raw = (
            jnp.einsum("qhd,khd->hqk", queries_split, keys_all, preferred_element_type=jnp.float32)
            * score_scale
        )
        return jnp.where(allowed[None], raw, masked_score)

    scores = masked_scores()
    highest = jnp.max(scores, axis=-1, keepdims=True)
    weights_exp = jnp.exp(scores - highest)
    totals = jnp.sum(weights_exp, axis=-1, keepdims=True)
    log_totals = highest + jnp.log(totals)
    probs_low = (weights_exp / totals).astype(jnp.bfloat16)
    attended = jnp.einsum("hqk,khd->qhd", probs_low, values_all, preferred_element_type=jnp.float32)
    mixed_low = (
        (attended * heads_low[None, :, None]).astype(jnp.bfloat16).reshape(tokens_dev, width)
    )
    proj_out = jnp.dot(mixed_low, out_full, preferred_element_type=jnp.float32) + vectors[6]
    normed_post, hat_post, scale_post = layer_norm(proj_out, vectors[1], vectors[7])
    residual = tokens_in + normed_post
    normed_two, hat_two, scale_two = layer_norm(residual, vectors[2], vectors[8])
    rows_low = normed_two.astype(jnp.bfloat16)
    grad_in = out_grad.astype(jnp.float32)
    fc1_full, fc2_full, hidden_full = (
        lax.all_gather(fc1_weight.astype(jnp.bfloat16), "wide", axis=1, tiled=True),
        lax.all_gather(fc2_weight.astype(jnp.bfloat16), "wide", axis=0, tiled=True),
        lax.all_gather(hidden_vectors.astype(jnp.bfloat16), "wide", axis=1, tiled=True),
    )
    hidden_par = hidden_full.astype(jnp.float32)
    pre_act = jnp.dot(rows_low, fc1_full, preferred_element_type=jnp.float32) + hidden_par[2]
    activated, gelu_back = jax.vjp(exact_gelu, pre_act)
    first_mean = jnp.mean(activated, axis=-1, keepdims=True)
    second_mean = jnp.mean(activated * activated, axis=-1, keepdims=True)
    middle, hat_mid, scale_mid = middle_forward(
        activated, first_mean, second_mean, hidden_par[0], hidden_par[1]
    )
    middle_low = middle.astype(jnp.bfloat16)
    ffn_out = jnp.dot(middle_low, fc2_full, preferred_element_type=jnp.float32)
    output = (residual + (ffn_out + vectors[9])).astype(jnp.bfloat16)
    fc2_grad = jnp.einsum("tf,td->fd", middle_low, out_grad, preferred_element_type=jnp.float32)
    middle_grad = jnp.einsum("td,fd->tf", out_grad, fc2_full, preferred_element_type=jnp.float32)
    mid_gain_grad = jnp.sum(middle_grad * hat_mid, axis=0)
    mid_bias_grad = jnp.sum(middle_grad, axis=0)
    scaled_mid = middle_grad * hidden_par[0]
    plain_mean = jnp.mean(scaled_mid, axis=-1, keepdims=True)
    cross_mean = jnp.mean(scaled_mid * hat_mid, axis=-1, keepdims=True)
    act_grad = scale_mid * (scaled_mid - plain_mean - hat_mid * cross_mean)
    pre_low = gelu_back(act_grad)[0].astype(jnp.bfloat16)
    fc1_bias_grad = jnp.sum(pre_low.astype(jnp.float32), axis=0)
    fc1_grad = jnp.einsum("td,tf->df", rows_low, pre_low, preferred_element_type=jnp.float32)
    rows_grad = jnp.einsum("tf,df->td", pre_low, fc1_full, preferred_element_type=jnp.float32)
    hidden_grad = jnp.stack([mid_gain_grad, mid_bias_grad, fc1_bias_grad])
    out_bias_total = jnp.sum(grad_in, axis=0)
    residual_grad = grad_in + norm_back(rows_grad, hat_two, scale_two, vectors[2])
    gain_two_grad = jnp.sum(rows_grad * hat_two, axis=0)
    bias_two_grad = jnp.sum(rows_grad, axis=0)
    gain_post_grad = jnp.sum(residual_grad * hat_post, axis=0)
    bias_post_grad = jnp.sum(residual_grad, axis=0)
    proj_low = norm_back(residual_grad, hat_post, scale_post, vectors[1]).astype(jnp.bfloat16)
    proj_bias_grad = jnp.sum(proj_low.astype(jnp.float32), axis=0)
    out_weight_grad = jnp.einsum(
        "td,te->de", mixed_low, proj_low, preferred_element_type=jnp.float32
    )
    mixed_grad = jnp.einsum(
        "te,de->td", proj_low, out_full, preferred_element_type=jnp.float32
    ).reshape(tokens_dev, heads_count, head_size)
    head_grad = jnp.sum(mixed_grad * attended, axis=(0, 2))
    attended_low = (mixed_grad * heads_low[None, :, None]).astype(jnp.bfloat16)
    probs = jnp.exp(masked_scores() - log_totals)
    probs_grad = jnp.einsum(
        "qhd,khd->hqk", attended_low, values_all, preferred_element_type=jnp.float32
    )
    delta = jnp.transpose(jnp.sum(attended_low.astype(jnp.float32) * attended, axis=-1))[:, :, None]
    scores_low = (probs * (probs_grad - delta)).astype(jnp.bfloat16)
    query_grad = (
        (
            jnp.einsum("hqk,khd->qhd", scores_low, keys_all, preferred_element_type=jnp.float32)
            * score_scale
        )
        .astype(jnp.bfloat16)
        .reshape(tokens_dev, width)
    )
    key_grad = (
        jnp.einsum("hqk,qhd->khd", scores_low, queries_split, preferred_element_type=jnp.float32)
        * score_scale
    )
    value_grad = jnp.einsum(
        "hqk,qhd->khd", probs.astype(jnp.bfloat16), attended_low, preferred_element_type=jnp.float32
    )
    pair_grad = jnp.stack([key_grad.reshape(-1, width), value_grad.reshape(-1, width)])
    pair_back = pair_grad[:, :tokens_dev]
    for shift_step in range(1, key_span + 1):
        piece = pair_grad[:, shift_step * tokens_dev : (shift_step + 1) * tokens_dev]
        pair_back = pair_back + from_behind(piece, "wide", -shift_step)
    pair_low = pair_back.astype(jnp.bfloat16)
    qkv_cat = jnp.concatenate([query_grad, pair_low[0], pair_low[1]], axis=1)
    query_bias_grad = jnp.sum(query_grad.astype(jnp.float32), axis=0)
    value_bias_grad = jnp.sum(pair_low[1].astype(jnp.float32), axis=0)
    qkv_grad = jnp.einsum("td,te->de", normed_low, qkv_cat, preferred_element_type=jnp.float32)
    normed_grad = jnp.einsum("te,de->td", qkv_cat, qkv_full, preferred_element_type=jnp.float32)
    input_grad = residual_grad + norm_back(normed_grad, hat_in, scale_in, vectors[0])
    gain_in_grad = jnp.sum(normed_grad * hat_in, axis=0)
    bias_in_grad = jnp.sum(normed_grad, axis=0)
    vector_grad = jnp.stack(
        [
            gain_in_grad,
            gain_post_grad,
            gain_two_grad,
            bias_in_grad,
            query_bias_grad,
            value_bias_grad,
            proj_bias_grad,
            bias_post_grad,
            bias_two_grad,
            out_bias_total,
        ]
    )
    qkv_part, out_part, vector_part = (
        lax.psum_scatter(qkv_grad, "wide", scatter_dimension=0, tiled=True),
        lax.psum_scatter(out_weight_grad, "wide", scatter_dimension=0, tiled=True),
        lax.psum_scatter(vector_grad, "wide", scatter_dimension=1, tiled=True),
    )
    fc1_part, fc2_part, hidden_part = (
        lax.psum_scatter(fc1_grad, "wide", scatter_dimension=1, tiled=True),
        lax.psum_scatter(fc2_grad, "wide", scatter_dimension=0, tiled=True),
        lax.psum_scatter(hidden_grad, "wide", scatter_dimension=1, tiled=True),
    )
    summed = lax.psum(
        (qkv_part, out_part, fc1_part, fc2_part, vector_part, hidden_part, head_grad), "dp"
    )
    local_squares = sum((jnp.sum(member * member) for member in summed[:6]))
    norm_terms = lax.psum((local_squares, summed[6]), "wide")
    shard_grads = summed[:6]
    head_total = norm_terms[1]
    grad_norm = jnp.sqrt(norm_terms[0] + jnp.sum(head_total * head_total))
    factor = jnp.minimum(1.0, clip_limit / (grad_norm + 1e-06))
    step = step_count[0].astype(jnp.float32)
    grads = (
        shard_grads[0],
        shard_grads[1],
        shard_grads[2],
        shard_grads[3],
        shard_grads[4],
        shard_grads[5],
        head_total,
    )
    params = (
        qkv_weight,
        out_weight,
        fc1_weight,
        fc2_weight,
        model_vectors,
        hidden_vectors,
        head_scale,
    )
    firsts = (qkv_first, out_first, fc1_first, fc2_first, vectors_first, hidden_first, head_first)
    seconds = (
        qkv_second,
        out_second,
        fc1_second,
        fc2_second,
        vectors_second,
        hidden_second,
        head_second,
    )
    rates = (
        matrix_rate,
        matrix_rate,
        matrix_rate,
        matrix_rate,
        vector_rate,
        vector_rate,
        vector_rate,
    )
    decays = (weight_decay, weight_decay, weight_decay, weight_decay, 0.0, 0.0, 0.0)
    updated = []
    for number in range(7):
        updated.extend(
            adam_step(
                grads[number] * factor,
                params[number],
                firsts[number],
                seconds[number],
                step,
                rates[number],
                decays[number],
            )
        )
    return (
        output,
        input_grad,
        grad_norm.reshape(1),
        updated[0],
        updated[1],
        updated[2],
        updated[3],
        updated[4],
        updated[5],
        updated[6],
        updated[7],
        updated[8],
        updated[9],
        updated[10],
        updated[11],
        updated[12],
        updated[13],
        updated[14],
        updated[15],
        updated[16],
        updated[17],
        updated[18],
        updated[19],
        updated[20],
    )


def solution(mesh):
    placed = (
        P(("dp", "wide"), None),
        P(("dp", "wide"), None),
        P(),
        P(),
        P("wide", None),
        P("wide", None),
        P("wide", None),
        P("wide", None),
        P("wide", None),
        P("wide", None),
        P(None, "wide"),
        P(None, "wide"),
        P(None, "wide"),
        P("wide", None),
        P("wide", None),
        P("wide", None),
        P(None, "wide"),
        P(None, "wide"),
        P(None, "wide"),
        P(None, "wide"),
        P(None, "wide"),
        P(None, "wide"),
        P(),
        P(),
        P(),
    )
    return jax.shard_map(
        body,
        mesh=mesh,
        in_specs=placed,
        out_specs=(
            P(("dp", "wide"), None),
            P(("dp", "wide"), None),
            P(),
            P("wide", None),
            P("wide", None),
            P("wide", None),
            P("wide", None),
            P("wide", None),
            P("wide", None),
            P(None, "wide"),
            P(None, "wide"),
            P(None, "wide"),
            P("wide", None),
            P("wide", None),
            P("wide", None),
            P(None, "wide"),
            P(None, "wide"),
            P(None, "wide"),
            P(None, "wide"),
            P(None, "wide"),
            P(None, "wide"),
            P(),
            P(),
            P(),
        ),
        check_vma=False,
    )
```

profile of v0, /device:TPU:0, one launch (start us, length us, event | category | flops | bytes accessed | tf_op | source)
XLA Modules:
  0.0 1402.8 jit_solution(9525445198860748381)
XLA Ops:
  16.4 23.5 %all-gather = bf16[16,64,10]{1,2,0:T(8,128)(2,1)S(1)} all-gather(bf16[1,64,10]{1,2,0:T(8,128)(2,1)S(1)} %convert_bitcast_fusion), channel_id=1, replica_groups=mesh['dp'=2,'wide'=16] {'wide'}, dimensions={0}, use_global_device_ids=true | all-gather | bytes 21760 | tf_op jit(solution)/shard_map/all_gather | solution.py:111
  40.8 34.8 %all-gather.6.cloned.1.call-done = bf16[1024,3072]{1,0:T(8,128)(2,1)} async-done(((bf16[64,3072]{1,0:T(8,128)(2,1)}), bf16[1024,3072]{1,0:T(8,128)(2,1)}) %all-gather.6.cloned.1.call-update) | async-done | bytes 6291472 | tf_op jit(solution)/shard_map/all_gather | solution.py:109
  75.6 5.7 fusion.58
  90.8 130.6 %all_gather.22 = bf16[3,4096]{1,0:T(4,128)(2,1)S(1)} all-gather(bf16[3,256]{1,0:T(4,128)(2,1)S(1)} %convert_element_type.131), channel_id=1, replica_groups=mesh['dp'=2,'wide'=16] {'wide'}, dimensions={1}, use_global_device_ids=true | all-gather | bytes 26112 | tf_op jit(solution)/shard_map/all_gather | solution.py:172
  234.9 5.5 copy.72
  240.3 21.4 %fusion.2 = (f32[16,512]{1,0:T(8,128)S(1)}, f32[16,512,1536]{2,1,0:T(8,128)}) fusion(pred[512,1536]{1,0:T(8,128)(4,1)} %compare_and_fusion, bf16[512,16,64]{0,2,1:T(8,128)(2,1)} %bitcast.115, bf16[1536,16,64]{0,2,1:T(8,128)(2,1)S(1)} %bitcast.111), kind=kOutput, calls=%fused_computation.7 | convolution fusion | flops 1648353280 | bytes 55345152 | tf_op jit(solution)/shard_map/qhd,khd->hqk/dot_general | solution.py:148
  261.7 22.3 %fusion = f32[16,512]{1,0:T(8,128)S(1)} fusion(f32[16,512,1536]{2,1,0:T(8,128)} %get-tuple-element.112, f32[16,512]{1,0:T(8,128)S(1)} %get-tuple-element.111, pred[512,1536]{1,0:T(8,128)(4,1)} %compare_and_fusion), kind=kLoop, calls=%fused_computation.5 | loop fusion | flops 50323456 | bytes 51183616 | tf_op jit(solution)/shard_map/reduce_sum | solution.py:156
  284.0 23.7 %fusion.34 = (bf16[512,16,64]{0,2,1:T(8,128)(2,1)}, f32[16,64,512]{2,1,0:T(8,128)}) fusion(f32[16]{0:T(128)S(1)} %convert_element_type.126, bf16[1536,16,64]{0,2,1:T(8,128)(2,1)} %bitcast.119, f32[16,512,1536]{2,1,0:T(8,128)} %get-tuple-element.112, f32[16,512]{1,0:T(8,128)S(1)} %fusion, f32[16,512]{1,0:T(8,128)S(1)} %get-tuple-element.111, ...), kind=kOutput, calls=%fused_computation.77 | convolution fusion | flops 1674575872 | bytes 57475136 | tf_op jit(solution)/shard_map/hqk,khd->qhd/dot_general | solution.py:159
  314.0 29.4 %fusion.63 = (f32[512]{0:T(512)S(1)}, f32[512]{0:T(512)S(1)}, f32[512,4096]{1,0:T(8,128)}, f32[512,4096]{1,0:T(8,128)}, f32[512,4096]{1,0:T(8,128)}) fusion(f32[4096]{0:T(1024)S(1)} %bitcast.138, bf16[1024,4096]{1,0:T(8,128)(2,1)} %all-gather.10.cloned.1.call-done, f32[512,1024]{1,0:T(8,128)} %copy-done.4, f32[1024]{0:T(1024)S(1)} %bitcast.166, ...), kind=kOutput, calls=%fused_computation.191 | convolution fusion | flops 4440194048 | bytes 35684352 | tf_op jit(solution)/shard_map/dot_general | solution.py:175
  343.5 13.7 multiply_reduce_fusion
  357.2 14.6 %convert_reduce_fusion = (f32[4096]{0:T(1024)S(1)}, bf16[512,4096]{1,0:T(8,128)(2,1)S(1)}) fusion(f32[512,4096]{1,0:T(8,128)} %get-tuple-element.81, f32[512]{0:T(512)S(1)} %broadcast_multiply_fusion, f32[512,4096]{1,0:T(8,128)} %get-tuple-element.80, f32[512]{0:T(512)S(1)} %get-tuple-element.106, f32[512]{0:T(512)S(1)} %broadcast_multiply_fusion.1, ...), kind=kLoop, calls=%fused_computation.17 | loop fusion | flops 50327552 | bytes 37806080 | tf_op jit(solution)/shard_map/reduce_sum | solution.py:194
  371.8 9.0 multiply_reduce_fusion.4
  393.7 24.4 %fusion.3 = f32[16,64,1536]{2,1,0:T(8,128)} fusion(bf16[512,16,64]{0,2,1:T(8,128)(2,1)S(1)} %get-tuple-element.78, f32[16,512,1536]{2,1,0:T(8,128)} %get-tuple-element.112, f32[16,512]{1,0:T(8,128)S(1)} %log_add_fusion, pred[512,1536]{1,0:T(8,128)(4,1)S(1)} %copy-done.15), kind=kOutput, calls=%fused_computation.8 | convolution fusion | flops 1660944384 | bytes 58490880 | tf_op jit(solution)/shard_map/hqk,qhd->khd/dot_general | solution.py:232
  418.0 31.4 %multiply_convert_fusion = bf16[16,512,1536]{2,1,0:T(8,128)(2,1)} fusion(f32[16,512,1536]{2,1,0:T(8,128)} %get-tuple-element.112, bf16[512,16,64]{0,2,1:T(8,128)(2,1)S(1)} %get-tuple-element.78, bf16[1536,16,64]{0,2,1:T(8,128)(2,1)} %bitcast.120, f32[16,512]{1,0:T(8,128)S(1)} %bitcast.143, f32[16,512]{1,0:T(8,128)S(1)} %log_add_fusion, ...), kind=kOutput, calls=%fused_computation | convolution fusion | flops 1686110208 | bytes 80543744 | tf_op jit(solution)/shard_map/qhd,khd->hqk/dot_general | solution.py:215
  449.5 10.7 convolution_multiply_fusion
  468.6 13.9 convert_reduce_fusion.5
  482.5 123.9 %collective-permute-done.3 = f32[2,512,1024]{1,2,0:T(8,128)} collective-permute-done((f32[2,512,1024]{1,2,0:T(8,128)}, f32[2,512,1024]{1,2,0:T(8,128)}, u32[]{:S(2)}, u32[]{:S(2)}) %collective-permute-start.3) | collective-permute-done | bytes 4194336 | tf_op jit(solution)/shard_map/ppermute | solution.py:23
  606.4 5.9 fusion.17
  615.1 9.7 fusion.37
  626.0 14.0 fusion.62
  641.9 11.3 fusion.60
  656.1 10.3 fusion.30
  668.6 90.2 %reduce-scatter.11.cloned.1.call-done = f32[64,3072]{1,0:T(8,128)} async-done(((f32[1024,3072]{1,0:T(8,128)}), f32[64,3072]{1,0:T(8,128)}) %reduce-scatter.11.cloned.1.call-update) | async-done | bytes 786448 | tf_op jit(solution)/shard_map/reduce_scatter | solution.py:264
  758.7 182.4 %reduce-scatter.17.cloned.1.call-done = f32[256,1024]{1,0:T(8,128)} async-done(((f32[4096,1024]{1,0:T(8,128)}), f32[256,1024]{1,0:T(8,128)}) %reduce-scatter.17.cloned.1.call-update) | async-done | bytes 1048592 | tf_op jit(solution)/shard_map/reduce_scatter | solution.py:270
  941.1 182.3 %reduce-scatter.15.cloned.1.call-done = f32[1024,256]{1,0:T(8,128)} async-done(((f32[1024,4096]{1,0:T(8,128)}), f32[1024,256]{1,0:T(8,128)}) %reduce-scatter.15.cloned.1.call-update) | async-done | bytes 1048592 | tf_op jit(solution)/shard_map/reduce_scatter | solution.py:269
  1123.4 11.3 add_convert_fusion.2
  1134.8 53.4 %reduce-scatter.21.cloned.1.call-done = f32[256,3]{1,0:T(8,128)} async-done(((f32[4096,3]{1,0:T(8,128)}), f32[256,3]{1,0:T(8,128)}) %reduce-scatter.21.cloned.1.call-update) | async-done | bytes 3088
  1189.3 4.2 fusion.29
  1193.5 53.5 %reduce-scatter.19.cloned.1.call-done = f32[64,10]{1,0:T(8,128)} async-done(((f32[1024,10]{1,0:T(8,128)}), f32[64,10]{1,0:T(8,128)}) %reduce-scatter.19.cloned.1.call-update) | async-done | bytes 2576
  1247.9 8.3 all-reduce.1
  1257.4 77.6 %all-reduce.5.cloned.1.call-done = (f32[64,3072]{1,0:T(8,128)}, f32[64,1024]{1,0:T(8,128)}, f32[1024,256]{1,0:T(8,128)}, f32[256,1024]{1,0:T(8,128)}) async-done(((f32[64,3072]{1,0:T(8,128)}, f32[64,1024]{1,0:T(8,128)}, f32[1024,256]{1,0:T(8,128)}, f32[256,1024]{1,0:T(8,128)}), (f32[64,3072]{1,0:T(8,128)}, f32[64,1024]{1,0:T(8,128)}, f32[1024,256]{1,0:T(8,128)}, ...) | async-done | bytes 3145744 | tf_op jit(solution)/shard_map/psum | solution.py:273
  1346.8 33.7 %all-reduce = (f32[]{:T(128)}, f32[16]{0:T(128)S(1)}) all-reduce(f32[]{:T(128)S(6)} %add.422, f32[16]{0:T(128)S(1)} %get-tuple-element.48), channel_id=1, replica_groups=mesh['dp'=2,'wide'=16] {'wide'}, use_global_device_ids=true, to_apply=%region_54.55 | all-reduce | flops 17 | bytes 136 | tf_op jit(solution)/shard_map/psum | solution.py:277
  (235 shorter events, 93.9 us)
Async XLA Ops:
  7.2 68.3 %all-gather.6.cloned.1.call-start = ((), (), s32[]{:S(2)}) async-start(), calls=%async_computation.6 | async-start | bytes 6684672 | tf_op jit(solution)/shard_map/all_gather | solution.py:109
  9.3 298.4 %all-gather.8.cloned.1.call-start = ((), (), s32[]{:S(2)}) async-start(), calls=%async_computation.7 | async-start | bytes 2228224 | tf_op jit(solution)/shard_map/all_gather | solution.py:110
  11.0 303.0 %all-gather.10.cloned.1.call-start = ((), (), s32[]{:S(2)}) async-start(), calls=%async_computation.8 | async-start | bytes 8912896 | tf_op jit(solution)/shard_map/all_gather | solution.py:170
  13.1 330.3 %all-gather.12.cloned.1.call-start = ((), (), s32[]{:S(2)}) async-start(), calls=%async_computation.9 | async-start | bytes 8912896 | tf_op jit(solution)/shard_map/all_gather | solution.py:171
  15.3 653.3 %reduce-scatter.13.cloned.1.call-start = ((), (), s32[]{:S(2)}) async-start(), calls=%async_computation.11 | async-start | bytes 4456448 | tf_op jit(solution)/shard_map/reduce_scatter | solution.py:265
  83.6 141.3 %collective-permute-start.1 = (bf16[2,512,1024]{2,1,0:T(8,128)(2,1)}, bf16[2,512,1024]{2,1,0:T(8,128)(2,1)}, u32[]{:S(2)}, u32[]{:S(2)}) collective-permute-start(bf16[2,512,1024]{2,1,0:T(8,128)(2,1)} %pad_maximum_fusion.3), channel_id=1, source_target_pairs={{0,2},{1,3},{2,4},{3,5},{4,6},{5,7},{6,8},{7,9},{8,10},{9,11},{10,... | collective-permute-start | bytes 6291464 | tf_op jit(solution)/shard_map/ppermute | solution.py:23
  87.5 137.5 %collective-permute-start = (bf16[2,512,1024]{2,1,0:T(8,128)(2,1)}, bf16[2,512,1024]{2,1,0:T(8,128)(2,1)}, u32[]{:S(2)}, u32[]{:S(2)}) collective-permute-start(bf16[2,512,1024]{2,1,0:T(8,128)(2,1)} %pad_maximum_fusion.3), channel_id=1, source_target_pairs={{0,1},{1,2},{2,3},{3,4},{4,5},{5,6},{6,7},{7,8},{8,9},{9,10},{10,1... | collective-permute-start | bytes 6291464 | tf_op jit(solution)/shard_map/ppermute | solution.py:23
  387.8 370.9 %reduce-scatter.11.cloned.1.call-start = ((), (), s32[]{:S(2)}) async-start(), calls=%async_computation.10 | async-start | bytes 13369344 | tf_op jit(solution)/shard_map/reduce_scatter | solution.py:264
  466.0 16.5 %collective-permute-start.2 = (f32[2,512,1024]{1,2,0:T(8,128)}, f32[2,512,1024]{1,2,0:T(8,128)}, u32[]{:S(2)}, u32[]{:S(2)}) collective-permute-start(f32[2,512,1024]{1,2,0:T(8,128)} %get-tuple-element.84), channel_id=1, source_target_pairs={{1,0},{2,1},{3,2},{4,3},{5,4},{6,5},{7,6},{8,7},{9,8},{10,9},{11,1... | collective-permute-start | bytes 12582920 | tf_op jit(solution)/shard_map/ppermute | solution.py:23
  467.3 139.1 %collective-permute-start.3 = (f32[2,512,1024]{1,2,0:T(8,128)}, f32[2,512,1024]{1,2,0:T(8,128)}, u32[]{:S(2)}, u32[]{:S(2)}) collective-permute-start(f32[2,512,1024]{1,2,0:T(8,128)} %get-tuple-element.85), channel_id=1, source_target_pairs={{2,0},{3,1},{4,2},{5,3},{6,4},{7,5},{8,6},{9,7},{10,8},{11,9},{12,... | collective-permute-start | bytes 12582920 | tf_op jit(solution)/shard_map/ppermute | solution.py:23
  482.4 132.6 %copy-start.10 = (bf16[512,1024]{1,0:T(8,128)(2,1)S(1)}, bf16[512,1024]{1,0:T(8,128)(2,1)}, u32[]{:S(2)}) copy-start(bf16[512,1024]{1,0:T(8,128)(2,1)} %param.25) | copy-start | bytes 3145732
  482.4 132.6 %copy-start.21 = (bf16[16,64,512]{2,1,0:T(8,128)(2,1)S(1)}, bf16[16,64,512]{2,1,0:T(8,128)(2,1)}, u32[]{:S(2)}) copy-start(bf16[16,64,512]{2,1,0:T(8,128)(2,1)} %get-tuple-element.122) | copy-start | bytes 3145732
  482.4 132.6 %copy-start.36 = (f32[512]{0:T(512)S(1)}, f32[512]{0:T(512)}, u32[]{:S(2)}) copy-start(f32[512]{0:T(512)} %copy-done.35) | copy-start | bytes 6148
  482.4 132.6 %copy-start.38 = (f32[1,1024]{1,0:T(1,128)S(1)}, f32[1,1024]{1,0:T(1,128)}, u32[]{:S(2)}) copy-start(f32[1,1024]{1,0:T(1,128)} %copy-done.37) | copy-start | bytes 12292
  624.8 316.4 %reduce-scatter.17.cloned.1.call-start = ((), (), s32[]{:S(2)}) async-start(), calls=%async_computation.13 | async-start | bytes 17825792 | tf_op jit(solution)/shard_map/reduce_scatter | solution.py:270
  640.0 483.4 %reduce-scatter.15.cloned.1.call-start = ((), (), s32[]{:S(2)}) async-start(), calls=%async_computation.12 | async-start | bytes 17825792 | tf_op jit(solution)/shard_map/reduce_scatter | solution.py:269
  653.2 535.1 %reduce-scatter.21.cloned.1.call-start = ((), (), s32[]{:S(2)}) async-start(), calls=%async_computation.15 | async-start | bytes 2228224
  656.1 467.4 %copy-start.48 = (f32[1,1024]{1,0:T(1,128)S(1)}, f32[1,1024]{1,0:T(1,128)}, u32[]{:S(2)}) copy-start(f32[1,1024]{1,0:T(1,128)} %get-tuple-element.94) | copy-start | bytes 12292
  656.1 591.0 %reduce-scatter.19.cloned.1.call-start = ((), (), s32[]{:S(2)}) async-start(), calls=%async_computation.14 | async-start | bytes 557056
  667.8 667.3 %all-reduce.5.cloned.1.call-start = ((), (), s32[]{:S(2)}) async-start(), calls=%async_computation.16 | async-start | bytes 6291456 | tf_op jit(solution)/shard_map/psum | solution.py:273
  1134.7 247.7 %copy-start.56 = (f32[16]{0:T(128)S(1)}, f32[16]{0:T(128)}, u32[]{:S(2)}) copy-start(f32[16]{0:T(128)} %param.47) | copy-start | bytes 196
  1134.7 247.7 %copy-start.57 = (f32[16]{0:T(128)S(1)}, f32[16]{0:T(128)}, u32[]{:S(2)}) copy-start(f32[16]{0:T(128)} %param.49) | copy-start | bytes 196
  1134.7 247.7 %copy-start.58 = (f32[16]{0:T(128)S(1)}, f32[16]{0:T(128)}, u32[]{:S(2)}) copy-start(f32[16]{0:T(128)} %param.48) | copy-start | bytes 196
  1134.8 248.3 %copy-start.43 = (f32[3,256]{1,0:T(4,128)S(1)}, f32[3,256]{1,0:T(4,128)}, u32[]{:S(2)}) copy-start(f32[3,256]{1,0:T(4,128)} %param.44) | copy-start | bytes 9220
  1134.8 248.3 %copy-start.51 = (f32[3,256]{1,0:T(4,128)S(1)}, f32[3,256]{1,0:T(4,128)}, u32[]{:S(2)}) copy-start(f32[3,256]{1,0:T(4,128)} %param.46) | copy-start | bytes 9220
  1134.8 248.3 %copy-start.52 = (f32[3,256]{1,0:T(4,128)S(1)}, f32[3,256]{1,0:T(4,128)}, u32[]{:S(2)}) copy-start(f32[3,256]{1,0:T(4,128)} %param.45) | copy-start | bytes 9220
  1134.8 248.9 %copy-start.34 = (f32[10,64]{1,0:T(8,128)S(1)}, f32[10,64]{1,0:T(8,128)}, u32[]{:S(2)}) copy-start(f32[10,64]{1,0:T(8,128)} %param.41) | copy-start | bytes 7684
  1134.8 248.9 %copy-start.44 = (f32[10,64]{1,0:T(8,128)S(1)}, f32[10,64]{1,0:T(8,128)}, u32[]{:S(2)}) copy-start(f32[10,64]{1,0:T(8,128)} %param.43) | copy-start | bytes 7684
  1134.8 248.9 %copy-start.45 = (f32[10,64]{1,0:T(8,128)S(1)}, f32[10,64]{1,0:T(8,128)}, u32[]{:S(2)}) copy-start(f32[10,64]{1,0:T(8,128)} %param.42) | copy-start | bytes 7684
  1134.8 249.5 %copy-start.29 = (f32[64,1024]{1,0:T(8,128)S(1)}, f32[64,1024]{1,0:T(8,128)}, u32[]{:S(2)}) copy-start(f32[64,1024]{1,0:T(8,128)} %param.32) | copy-start | bytes 786436
  1193.5 196.7 %copy-start.16 = (f32[1024,256]{1,0:T(8,128)S(1)}, f32[1024,256]{1,0:T(8,128)}, u32[]{:S(2)}) copy-start(f32[1024,256]{1,0:T(8,128)} %param.35) | copy-start | bytes 3145732
  1193.5 196.7 %copy-start.23 = (f32[1024,256]{1,0:T(8,128)S(1)}, f32[1024,256]{1,0:T(8,128)}, u32[]{:S(2)}) copy-start(f32[1024,256]{1,0:T(8,128)} %param.37) | copy-start | bytes 3145732
  (42 other events, 945.5 us)
Sparse Core Ops, SparseCore 0:
  10.9 64.5 all-gather.5
  78.3 46.0 all-gather.7
  127.1 98.1 all-gather.9
  227.9 72.4 all-gather.11
  387.9 71.0 reduce-scatter.12
  624.9 133.7 reduce-scatter.10
  763.4 177.6 reduce-scatter.16
  945.8 177.5 reduce-scatter.14
  1127.6 60.6 reduce-scatter.20
  1192.2 54.7 reduce-scatter.18
  1249.7 85.3 all-reduce.4
where the time goes:
time: 1410 us; the launch traced here: 1400 us
  waiting for transfers between devices  798 us (57%)
  matrix products  249 us (18%)
  blocking collectives  196 us (14%)
  other arithmetic  96.5 us (7%)
  local copies, waits for them, and re-layouts  30.1 us (2%)
  between operations  22.4 us (2%)
    reduce_scatter x1, waiting for transfers between devices, body(): lax.psum_scatter(fc2_grad, 'wide', scatter_dimension=0, tiled=True)  182 us
    reduce_scatter x1, waiting for transfers between devices, body(): lax.psum_scatter(fc1_grad, 'wide', scatter_dimension=1, tiled=True)  182 us
    all_gather x1, blocking collectives, body(): lax.all_gather(hidden_vectors.astype(jnp.bfloat16), 'wide', axis=1, tiled...  131 us
    ppermute x4, waiting for transfers between devices, from_behind(): return lax.ppermute(shard, axis, pairs)  124 us
    unnamed x13, waiting for transfers between devices  107 us
    reduce_scatter x1, waiting for transfers between devices, body(): lax.psum_scatter(qkv_grad, 'wide', scatter_dimension=0, tiled=True)  90.2 us
    psum x1, waiting for transfers between devices, body(): lax.psum((qkv_part, out_part, fc1_part, fc2_part, vector_part, hidden_par...  77.6 us
    all_gather x1, waiting for transfers between devices, body(): lax.all_gather(qkv_weight.astype(jnp.bfloat16), 'wide', axis=0, tiled=True)  34.8 us
  transfers between devices with their start and end apart: 15, of which 8 were waited for; matrix products, arithmetic and copies ran while one was open for 21% of the time, Pallas kernels for 0%

commit v1 on v0

v1 whole, which is shorter than its diff:
```python
import functools

import jax
import jax.numpy as jnp
from jax import lax
from jax.experimental import pallas as pl
from jax.experimental.pallas import tpu as pltpu
from jax.sharding import PartitionSpec as P

DOC_MOST = 1024
MESH = pl.DeviceIdType.MESH
HBM = pl.BlockSpec(memory_space=pltpu.HBM)
VMEM = pl.BlockSpec(memory_space=pltpu.VMEM)
BF16 = jnp.bfloat16
F32 = jnp.float32

norm_epsilon = 1e-05
clip_limit = 1.0
first_decay = 0.9
second_decay = 0.98
adam_epsilon = 1e-08
matrix_rate = 0.1
vector_rate = 0.4
weight_decay = 0.1
masked_score = -1e30


def layer_norm(values_in, gain, shift):
    center = values_in - jnp.mean(values_in, axis=-1, keepdims=True)
    variance = jnp.mean(center * center, axis=-1, keepdims=True)
    scale = lax.rsqrt(variance + norm_epsilon)
    normed = center * scale
    return (normed * gain + shift, normed, scale)


def norm_back(grad, normed, scale, gain):
    scaled = grad * gain
    mean_plain = jnp.mean(scaled, axis=-1, keepdims=True)
    mean_cross = jnp.mean(scaled * normed, axis=-1, keepdims=True)
    return scale * (scaled - mean_plain - normed * mean_cross)


def middle_forward(activated, first_mean, second_mean, gain, shift):
    scale = lax.rsqrt(second_mean - first_mean * first_mean + norm_epsilon)
    normed = (activated - first_mean) * scale
    return (normed * gain + shift, normed, scale)


def exact_gelu(values_in):
    return jax.nn.gelu(values_in, approximate=False)


def doc_labels(doc_lengths, start, count, row_length):
    doc_count = doc_lengths.shape[1]
    places = start + jnp.arange(count, dtype=jnp.int32)
    row_number = start // row_length
    ends = jnp.cumsum(doc_lengths, axis=1)
    row_ends = lax.dynamic_slice_in_dim(ends, jnp.maximum(row_number, 0), 1, 0)[0]
    within = places - row_number * row_length
    document = jnp.sum((within[:, None] >= row_ends[None, :]).astype(jnp.int32), axis=1)
    return (row_number * doc_count + document, places)


def adam_step(grad, weight, first, second, step, rate, decay):
    first_new = first_decay * first + (1.0 - first_decay) * grad
    second_new = second_decay * second + (1.0 - second_decay) * grad * grad
    fix_one = 1.0 - jnp.power(jnp.float32(first_decay), step)
    fix_two = 1.0 - jnp.power(jnp.float32(second_decay), step)
    direction = first_new / fix_one / (jnp.sqrt(second_new / fix_two) + adam_epsilon)
    weight_new = weight - rate * (direction + decay * weight)
    return (first_new, second_new, weight_new)


def from_behind(shard, axis, by):
    count = lax.axis_size(axis)
    pairs = [(i, i + by) for i in range(count) if 0 <= i + by < count]
    return lax.ppermute(shard, axis, pairs)


class Place:
    def __init__(self):
        self.y = lax.axis_index("dp")
        self.w = lax.axis_index("wide")
        self.z = self.w // 4
        self.x = (self.w // 2) % 2
        self.c = self.w % 2

    def slab(self, z, x, c):
        return z * 4 + x * 2 + c

    def wide(self, w):
        return (self.y, w)

    def core_mate(self):
        return self.wide(self.slab(self.z, self.x, 1 - self.c))

    def x_mate(self):
        return self.wide(self.slab(self.z, 1 - self.x, self.c))

    def y_mate(self):
        return (1 - self.y, self.w)

    def up(self):
        return self.wide(lax.rem(self.w + 4, 16))

    def down(self):
        return self.wide(lax.rem(self.w + 12, 16))


def greet(me, extra=()):
    barrier = pltpu.get_barrier_semaphore()

    def hello(target):
        pl.semaphore_signal(barrier, inc=1, device_id=target, device_id_type=MESH)

    always = [me.core_mate(), me.x_mate(), me.y_mate(), *extra]
    sometimes = [
        (me.z < 3, me.up()),
        (me.z > 0, me.down()),
        (me.w < 14, me.wide(lax.rem(me.w + 2, 16))),
        (me.w >= 2, me.wide(lax.rem(me.w + 14, 16))),
    ]
    for target in always:
        hello(target)
    for holds, target in sometimes:
        pl.when(holds)(functools.partial(hello, target))
    count = len(always) + sum(holds.astype(jnp.int32) for holds, _ in sometimes)
    pl.semaphore_wait(barrier, count)


class Wire:
    def __init__(self, send, recv):
        self.send, self.recv = send, recv
        self.started = []

    def copy(self, source, target, index, device):
        return pltpu.make_async_remote_copy(
            src_ref=source,
            dst_ref=target,
            send_sem=self.send.at[index],
            recv_sem=self.recv.at[index],
            device_id=device,
            device_id_type=MESH,
        )

    def put(self, source, target, index, device, holds=None):
        moved = self.copy(source, target, index, device)
        if holds is None:
            moved.start()
        else:
            pl.when(holds)(moved.start)
        self.started.append((holds, moved))

    def got(self, target, index, device):
        self.copy(target, target, index, device).wait_recv()

    def finish(self):
        for holds, moved in self.started:
            if holds is None:
                moved.wait_send()
            else:
                pl.when(holds)(moved.wait_send)


def both(*conditions):
    held = [one for one in conditions if one is not None]
    total = held[0] if held else None
    for one in held[1:]:
        total = jnp.logical_and(total, one)
    return total


def when(holds, action):
    if holds is None:
        action()
    else:
        pl.when(holds)(action)


def ag_steps(me, wire, base, own, full, third):
    rows = own.shape[0]
    plane = (
        pl.ds(pl.multiple_of(me.y * third, 16), rows - third) if third else pl.ds(0, rows)
    )
    share = pl.ds(pl.multiple_of(me.y * (rows - third), 16), third) if third else None
    other = pl.ds(pl.multiple_of((1 - me.y) * (rows - third), 16), third) if third else None
    my_slab = me.slab(me.z, me.x, me.c)
    ups, downs, xs, ys, cs, ts = (base + k for k in (0, 4, 8, 12, 20, 28))

    def pass_on(z, x, holds):
        slab = me.slab(z, x, me.c)
        place = z * 2 + x
        block = full.at[slab, plane]
        if third:
            piece = full.at[slab, share]
            wire.put(piece, piece, ys + place, me.y_mate(), holds)
        wire.put(block, block, cs + place, me.core_mate(), holds)

    wire.put(own.at[plane], full.at[my_slab, plane], ups + me.z, me.up(), me.z < 3)
    wire.put(own.at[plane], full.at[my_slab, plane], downs + me.z, me.down(), me.z > 0)
    wire.put(own.at[plane], full.at[my_slab, plane], xs + me.z, me.x_mate())
    wire.put(own, full.at[my_slab], cs + me.z * 2 + me.x, me.core_mate())
    yield
    for tick in range(1, 5):
        if tick < 4:
            for away, holds, onward, follow, sems in (
                (me.z - tick, me.z - tick >= 0, me.up(), me.z < 3, ups),
                (me.z + tick, me.z + tick <= 3, me.down(), me.z > 0, downs),
            ):
                safe = lax.rem(away + 4, 4)
                block = full.at[me.slab(safe, me.x, me.c), plane]
                pl.when(holds)(functools.partial(wire.got, block, sems + safe, onward))
                wire.put(block, block, sems + safe, onward, both(holds, follow))
                wire.put(block, block, xs + safe, me.x_mate(), holds)
                pass_on(safe, me.x, holds)
        before = tick - 1
        for away, holds in (
            ((me.z, None),)
            if before == 0
            else (
                (me.z - before, me.z - before >= 0),
                (me.z + before, me.z + before <= 3),
            )
        ):
            safe = lax.rem(away + 4, 4)
            block = full.at[me.slab(safe, 1 - me.x, me.c), plane]
            when(holds, functools.partial(wire.got, block, xs + safe, me.x_mate()))
            pass_on(safe, 1 - me.x, holds)
        yield
    if third:
        for k in range(1, 8):
            place = lax.rem(me.z * 2 + me.x + k, 8)
            piece = full.at[me.slab(place // 2, place % 2, me.c), other]
            wire.got(piece, ys + place, me.y_mate())
            wire.put(piece, piece, ts + place, me.core_mate())
        yield
    mine = me.z * 2 + me.x
    wire.got(full.at[me.slab(me.z, me.x, 1 - me.c)], cs + mine, me.core_mate())
    for k in range(1, 8):
        place = lax.rem(mine + k, 8)
        slab = me.slab(place // 2, place % 2, 1 - me.c)
        wire.got(full.at[slab, plane], cs + place, me.core_mate())
        if third:
            wire.got(full.at[slab, other], ts + place, me.core_mate())
    yield


AG_SEMS = 36


def run_all(steps):
    waiting, active = list(steps), []
    while waiting or active:
        if waiting:
            active.append(waiting.pop(0))
        active = [one for one in reversed(active) if next(one, active) is not active][::-1]


def gather_kernel(thirds, *refs):
    count = len(thirds)
    owns, tokens = refs[:count], refs[count]
    fulls, halo = refs[count + 1 : 2 * count + 1], refs[2 * count + 1]
    blank, send, recv, local = refs[2 * count + 2 :]
    me = Place()
    first, second = AG_SEMS * count, AG_SEMS * count + 1
    keep = [
        pltpu.make_async_copy(own, full.at[me.w], local.at[k])
        for k, (own, full) in enumerate(zip(owns, fulls))
    ]
    for one in keep:
        one.start()
    blank[...] = jnp.zeros_like(blank)
    clear = [
        (me.w < 2, pltpu.make_async_copy(blank, halo.at[0], local.at[count])),
        (me.w < 1, pltpu.make_async_copy(blank, halo.at[1], local.at[count + 1])),
    ]
    for holds, one in clear:
        pl.when(holds)(one.start)
    greet(me)
    wire = Wire(send, recv)
    wire.put(tokens, halo.at[0], first, me.wide(lax.rem(me.w + 2, 16)), me.w < 14)
    wire.put(tokens, halo.at[1], second, me.core_mate(), me.c == 0)

    def halo_steps():
        yield
        yield
        pl.when(me.w >= 2)(functools.partial(wire.got, halo.at[0], first, me.core_mate()))
        wire.put(
            halo.at[0], halo.at[1], second, me.core_mate(), both(me.c == 1, me.w >= 2)
        )
        pl.when(me.w >= 1)(functools.partial(wire.got, halo.at[1], second, me.core_mate()))
        yield

    run_all(
        [
            ag_steps(me, wire, AG_SEMS * k, own, full, third)
            for k, (own, full, third) in enumerate(zip(owns, fulls, thirds))
        ]
        + [halo_steps()]
    )
    wire.finish()
    for one in keep:
        one.wait()
    for holds, one in clear:
        pl.when(holds)(one.wait)


def gather_all(shards, thirds, tokens):
    count = len(shards)
    wide = lax.axis_size("wide")
    if lax.axis_size("dp") == 2 and wide == 16:
        out_shape = [jax.ShapeDtypeStruct((wide, *one.shape), one.dtype) for one in shards]
        out_shape.append(jax.ShapeDtypeStruct((2, *tokens.shape), tokens.dtype))
        sems = AG_SEMS * count + 2
        return pl.pallas_call(
            functools.partial(gather_kernel, thirds),
            out_shape=out_shape,
            in_specs=[VMEM] * (count + 1),
            out_specs=[HBM] * (count + 1),
            scratch_shapes=[
                pltpu.VMEM(tokens.shape, tokens.dtype),
                pltpu.SemaphoreType.DMA((sems,)),
                pltpu.SemaphoreType.DMA((sems,)),
                pltpu.SemaphoreType.DMA((count + 2,)),
            ],
            compiler_params=pltpu.CompilerParams(
                collective_id=0, has_side_effects=True, vmem_limit_bytes=24 << 20
            ),
            name="gather_all",
        )(*shards, tokens)
    fulls = [lax.all_gather(one, "wide", axis=0, tiled=False) for one in shards]
    halo = jnp.stack([from_behind(tokens, "wide", 2), from_behind(tokens, "wide", 1)])
    return [*fulls, halo]


def row_chunk(rows, columns, most):
    chunk = min(rows, max(16, most // columns // 16 * 16))
    while rows % chunk:
        chunk -= 16
    return chunk


def accumulate(target, source):
    *lead, rows, columns = source.shape
    chunk = row_chunk(rows, columns, 65536)
    per = rows // chunk
    many = per
    for size in lead:
        many *= size

    def step(number, carry):
        part = pl.ds(pl.multiple_of(lax.rem(number, per) * chunk, 16), chunk)
        rest, index = number // per, []
        for size in reversed(lead):
            index.insert(0, lax.rem(rest, size))
            rest = rest // size
        at = (*index, part)
        target[at] = (target[at].astype(F32) + source[at].astype(F32)).astype(target.dtype)
        return carry

    lax.fori_loop(0, many, step, 0)


RS_SEMS = 12


def rs_steps(me, wire, base, local, grad, quarter, held, bufs, final, squares, limit):
    from_core, from_y, from_x, from_down, from_up, from_last = bufs
    count, columns = held.shape[-2:]
    take = pltpu.make_async_copy(grad.at[:, :, me.c], held, local)
    take.start()
    wire.put(grad.at[:, :, 1 - me.c], from_core, base, me.core_mate())
    yield
    take.wait()
    wire.got(from_core, base, me.core_mate())
    accumulate(held, from_core)
    inside = count - quarter
    plane = pl.ds(pl.multiple_of(me.y * quarter, 16), inside) if quarter else pl.ds(0, count)
    if quarter:
        share = pl.ds(pl.multiple_of(me.y * inside, 16), quarter)
        other = pl.ds(pl.multiple_of((1 - me.y) * inside, 16), quarter)
        wire.put(held.at[:, :, other], from_y, base + 1, me.y_mate())
        yield
        wire.got(from_y, base + 1, me.y_mate())
        accumulate(held.at[:, :, share], from_y)
    mine = held.at[:, me.x, plane]
    wire.put(held.at[:, 1 - me.x, plane], from_x, base + 2, me.x_mate())
    yield
    wire.got(from_x, base + 2, me.x_mate())
    accumulate(mine, from_x)
    for tick in range(4):
        for place, sign, source, sems, onward, back in (
            (me.z, 1, from_down, 4, me.up(), me.down()),
            (3 - me.z, -1, from_up, 8, me.down(), me.up()),
        ):
            goal = me.z if tick == 3 else lax.rem(me.z + sign * (3 - tick) + 8, 4)
            sends = None if tick == 3 else both(place <= tick, place < 3)
            block, arrived = mine.at[goal], source.at[goal]

            def take_in(block=block, arrived=arrived, index=base + sems + goal, back=back):
                wire.got(arrived, index, back)
                accumulate(block, arrived)

            pl.when(both(sends, place > 0))(take_in)
            if sends is not None:
                wire.put(block, arrived, base + sems + goal, onward, sends)
        if tick < 3:
            yield
    wire.put(mine.at[me.z], from_last, base + 3, me.y_mate())
    yield
    wire.got(from_last, base + 3, me.y_mate())
    own = held.at[me.z, me.x]
    middle = count - 2 * quarter
    chunk = row_chunk(middle, columns, 32768)

    def add_planes(number, carry):
        at = pl.multiple_of(quarter + number * chunk, 16)
        there = pl.multiple_of(at - (1 - me.y) * quarter, 16)
        final[pl.ds(at, chunk)] = own[pl.ds(at, chunk)].astype(F32) + from_last[
            pl.ds(there, chunk)
        ].astype(F32)
        return carry

    lax.fori_loop(0, middle // chunk, add_planes, 0)
    if quarter:
        for plane_of, at, there in ((0, 0, 0), (1, count - quarter, count - 2 * quarter)):

            def from_held(at=at):
                final[pl.ds(at, quarter)] = own[pl.ds(at, quarter)].astype(F32)

            def from_mate(at=at, there=there):
                final[pl.ds(at, quarter)] = from_last[pl.ds(there, quarter)].astype(F32)

            pl.when(me.y == plane_of)(from_held)
            pl.when(me.y != plane_of)(from_mate)

    def square(number, total):
        value = final[pl.ds(pl.multiple_of(number * 8, 8), 8)]
        power = value * value
        if limit % 8:
            place = number * 8 + lax.broadcasted_iota(jnp.int32, power.shape, 0)
            power = jnp.where(place < limit, power, 0.0)
        folded = power[:, :128]
        for lane in range(128, columns, 128):
            folded = folded + power[:, lane : lane + 128]
        return total + folded

    squares[...] = squares[...] + lax.fori_loop(
        0, (limit + 7) // 8, square, jnp.zeros((8, 128), F32)
    )
    yield


def reduce_kernel(pieces, *refs):
    refs = list(refs)
    arrays = 1 + max(piece[0] for piece in pieces)
    count = len(pieces)
    grads, halo = refs[:arrays], refs[arrays]
    finals, back, norm = refs[arrays + 1 : 2 * arrays + 1], refs[2 * arrays + 1], refs[2 * arrays + 2]
    scratch = refs[2 * arrays + 3 :]
    blank, passing, joined, tiles, send, recv, local = scratch[-7:]
    me = Place()
    ending = RS_SEMS * count
    blank[...] = jnp.zeros_like(blank)
    tiles[...] = jnp.zeros_like(tiles)
    clear = [
        (me.w >= 14, pltpu.make_async_copy(blank, back.at[0], local.at[count])),
        (me.c == 1, pltpu.make_async_copy(blank, back.at[1], local.at[count + 1])),
    ]
    for holds, one in clear:
        pl.when(holds)(one.start)
    rounds = [me.wide(jnp.bitwise_xor(me.w, bit)) for bit in (1, 2, 4, 8)]
    greet(me, rounds[2:])
    wire = Wire(send, recv)

    def halo_steps():
        far = me.wide(lax.rem(me.w + 14, 16))
        inner = me.w >= 2
        wire.put(halo.at[0], back.at[0], ending, far, both(me.c == 0, inner))
        wire.put(halo.at[1], back.at[1], ending + 1, me.core_mate(), me.c == 1)
        wire.put(halo.at[1], passing, ending + 2, me.core_mate(), both(me.c == 0, inner))
        load = pltpu.make_async_copy(halo.at[0], joined, local.at[count + 2])
        joins = both(me.c == 1, inner)
        pl.when(joins)(load.start)
        yield

        def join():
            load.wait()
            wire.got(passing, ending + 2, me.core_mate())
            accumulate(joined, passing)

        pl.when(joins)(join)
        wire.put(joined, back.at[0], ending, far, joins)
        for _ in range(6):
            yield
        pl.when(me.w < 14)(functools.partial(wire.got, back.at[0], ending, far))
        pl.when(me.c == 0)(functools.partial(wire.got, back.at[1], ending + 1, me.core_mate()))
        yield

    sequences = []
    for k, (number, first, rows, quarter, limit) in enumerate(pieces):
        here = pl.ds(first, rows)
        sequences.append(
            rs_steps(
                me, wire, RS_SEMS * k, local.at[k],
                grads[number].at[:, :, :, here], quarter, scratch[7 * k],
                scratch[7 * k + 1 : 7 * k + 7], finals[number].at[here], tiles.at[0], limit,
            )
        )
    run_all([sequences[0], halo_steps(), *sequences[1:]])
    for k, partner in enumerate(rounds):
        index = ending + 3 + k
        moved = wire.copy(tiles.at[k], tiles.at[5 + k], index, partner)
        moved.start()
        moved.wait()
        tiles[k + 1] = tiles[k] + tiles[5 + k]
    norm[...] = tiles[4]
    wire.finish()
    for holds, one in clear:
        pl.when(holds)(one.wait)


def piece_buffers(rows, columns, quarter, dtype):
    inside = rows - quarter
    some = (4, 2, quarter, columns) if quarter else (1, 1, 16, 128)
    shapes = [
        (4, 2, rows, columns),
        (4, 2, rows, columns),
        some,
        (4, inside, columns),
        (4, inside, columns),
        (4, inside, columns),
        (inside, columns),
    ]
    return [pltpu.VMEM(shape, dtype) for shape in shapes]


def reduce_all(grads, halo, pieces):
    wide = lax.axis_size("wide")
    if lax.axis_size("dp") == 2 and wide == 16:
        count = len(pieces)
        tokens = halo.shape[1:]
        out_shape = [jax.ShapeDtypeStruct(one.shape[1:], F32) for one in grads]
        out_shape.append(jax.ShapeDtypeStruct(halo.shape, halo.dtype))
        out_shape.append(jax.ShapeDtypeStruct((8, 128), F32))
        scratch = []
        for number, _, rows, quarter, _ in pieces:
            one = grads[number]
            scratch += piece_buffers(rows, one.shape[2], quarter, one.dtype)
        sems = RS_SEMS * count + 7
        return pl.pallas_call(
            functools.partial(reduce_kernel, pieces),
            out_shape=out_shape,
            in_specs=[HBM] * (len(grads) + 1),
            out_specs=[VMEM] * len(grads) + [HBM, VMEM],
            scratch_shapes=scratch
            + [
                pltpu.VMEM(tokens, BF16),
                pltpu.VMEM(tokens, BF16),
                pltpu.VMEM(tokens, BF16),
                pltpu.VMEM((9, 8, 128), F32),
                pltpu.SemaphoreType.DMA((sems,)),
                pltpu.SemaphoreType.DMA((sems,)),
                pltpu.SemaphoreType.DMA((count + 3,)),
            ],
            compiler_params=pltpu.CompilerParams(
                collective_id=1, has_side_effects=True, vmem_limit_bytes=60 << 20
            ),
            name="reduce_all",
        )(*[one.reshape(4, 2, 2, *one.shape[1:]) for one in grads], halo)
    totals = [
        lax.psum(
            lax.psum_scatter(one.astype(F32), "wide", scatter_dimension=0, tiled=False), "dp"
        )
        for one in grads
    ]
    back = jnp.stack([from_behind(halo[0], "wide", -2), from_behind(halo[1], "wide", -1)])
    squares = jnp.float32(0.0)
    for number, first, rows, _, limit in pieces:
        part = totals[number][first : first + limit]
        squares = squares + jnp.sum(part * part)
    norm = jnp.zeros((8, 128), F32).at[0, 0].set(lax.psum(squares, "wide"))
    return [*totals, back, norm]


def pack(parts):
    flat = jnp.concatenate(parts, axis=1)
    size = -(-flat.shape[1] // 2048) * 2048
    return jnp.pad(flat, ((0, 0), (0, size - flat.shape[1]))).reshape(flat.shape[0], -1, 128)


def to_slabs(rows, wide):
    count, columns = rows.shape
    return rows.reshape(count, wide, -1).transpose(1, 0, 2).reshape(wide, -1)


def unpack(slabs, count):
    return slabs.reshape(slabs.shape[0], count, -1).transpose(1, 0, 2).reshape(count, -1)


def body(
    inputs,
    out_grad,
    doc_lengths,
    step_count,
    qkv_weight,
    qkv_first,
    qkv_second,
    out_weight,
    out_first,
    out_second,
    fc1_weight,
    fc1_first,
    fc1_second,
    fc2_weight,
    fc2_first,
    fc2_second,
    model_vectors,
    vectors_first,
    vectors_second,
    hidden_vectors,
    hidden_first,
    hidden_second,
    head_scale,
    head_first,
    head_second,
):
    tokens_dev = inputs.shape[0]
    width = inputs.shape[1]
    heads_count = head_scale.shape[0]
    head_size = width // heads_count
    wide = lax.axis_size("wide")
    row_length = tokens_dev * wide
    score_scale = head_size ** (-0.5)
    block_index = lax.axis_index("dp") * wide + lax.axis_index("wide")
    first_token = block_index * tokens_dev
    hidden_width = hidden_vectors.shape[1] * wide
    vector_rows, hidden_rows = model_vectors.shape[0], hidden_vectors.shape[0]
    vector_size, hidden_size = model_vectors.size, hidden_vectors.size

    small = pack(
        [model_vectors.astype(BF16).reshape(1, -1), hidden_vectors.astype(BF16).reshape(1, -1)]
    )[0]
    small_full, qkv_full, out_full, fc1_full, fc2_full, halo = gather_all(
        [
            small,
            qkv_weight.astype(BF16),
            out_weight.astype(BF16),
            fc1_weight.astype(BF16),
            fc2_weight.astype(BF16),
        ],
        (0, 16, 16, 256, 64),
        inputs,
    )
    flat = small_full.reshape(wide, -1)
    vectors = unpack(flat[:, :vector_size], vector_rows).astype(F32)
    hidden_par = unpack(flat[:, vector_size : vector_size + hidden_size], hidden_rows).astype(F32)
    qkv_full = qkv_full.reshape(width, 3 * width)
    out_full = out_full.reshape(width, width)
    fc2_full = fc2_full.reshape(hidden_width, width)
    heads_low = lax.optimization_barrier(head_scale.astype(BF16)).astype(F32)

    tokens_in = inputs.astype(F32)
    tokens_all = jnp.concatenate([halo.reshape(-1, width), inputs], axis=0)
    normed_in, hat_in, scale_in = layer_norm(tokens_all.astype(F32), vectors[0], vectors[3])
    normed_low = normed_in.astype(BF16)
    own = slice(2 * tokens_dev, None)
    queries = (
        jnp.dot(normed_low[own], qkv_full[:, :width], preferred_element_type=F32) + vectors[4]
    ).astype(BF16)
    projected = jnp.dot(normed_low, qkv_full[:, width:], preferred_element_type=F32)
    keys_all = projected[:, :width].astype(BF16).reshape(-1, heads_count, head_size)
    values_all = (
        (projected[:, width:] + vectors[5]).astype(BF16).reshape(-1, heads_count, head_size)
    )
    labels, places = [], []
    for back in (2, 1, 0):
        labels_here, places_here = doc_labels(
            doc_lengths, first_token - back * tokens_dev, tokens_dev, row_length
        )
        labels.append(labels_here)
        places.append(places_here)
    allowed = (labels[2][:, None] == jnp.concatenate(labels)[None, :]) & (
        jnp.concatenate(places)[None, :] <= places[2][:, None]
    )
    queries_split = queries.reshape(tokens_dev, heads_count, head_size)

    def masked_scores():
        raw = (
            jnp.einsum("qhd,khd->hqk", queries_split, keys_all, preferred_element_type=F32)
            * score_scale
        )
        return jnp.where(allowed[None], raw, masked_score)

    scores = masked_scores()
    highest = jnp.max(scores, axis=-1, keepdims=True)
    weights_exp = jnp.exp(scores - highest)
    totals = jnp.sum(weights_exp, axis=-1, keepdims=True)
    log_totals = highest + jnp.log(totals)
    probs_low = (weights_exp / totals).astype(BF16)
    attended = jnp.einsum("hqk,khd->qhd", probs_low, values_all, preferred_element_type=F32)
    mixed_low = (attended * heads_low[None, :, None]).astype(BF16).reshape(tokens_dev, width)
    proj_out = jnp.dot(mixed_low, out_full, preferred_element_type=F32) + vectors[6]
    normed_post, hat_post, scale_post = layer_norm(proj_out, vectors[1], vectors[7])
    residual = tokens_in + normed_post
    normed_two, hat_two, scale_two = layer_norm(residual, vectors[2], vectors[8])
    rows_low = normed_two.astype(BF16)
    grad_in = out_grad.astype(F32)

    pre_act = (
        jnp.einsum("td,wdf->twf", rows_low, fc1_full, preferred_element_type=F32).reshape(
            tokens_dev, hidden_width
        )
        + hidden_par[2]
    )
    activated, gelu_back = jax.vjp(exact_gelu, pre_act)
    first_mean = jnp.mean(activated, axis=-1, keepdims=True)
    second_mean = jnp.mean(activated * activated, axis=-1, keepdims=True)
    middle, hat_mid, scale_mid = middle_forward(
        activated, first_mean, second_mean, hidden_par[0], hidden_par[1]
    )
    middle_low = middle.astype(BF16)
    ffn_out = jnp.dot(middle_low, fc2_full, preferred_element_type=F32)
    output = (residual + (ffn_out + vectors[9])).astype(BF16)
    fc2_grad = jnp.einsum("tf,td->fd", middle_low, out_grad, preferred_element_type=F32)
    middle_grad = jnp.einsum("td,fd->tf", out_grad, fc2_full, preferred_element_type=F32)
    mid_gain_grad = jnp.sum(middle_grad * hat_mid, axis=0)
    mid_bias_grad = jnp.sum(middle_grad, axis=0)
    scaled_mid = middle_grad * hidden_par[0]
    plain_mean = jnp.mean(scaled_mid, axis=-1, keepdims=True)
    cross_mean = jnp.mean(scaled_mid * hat_mid, axis=-1, keepdims=True)
    act_grad = scale_mid * (scaled_mid - plain_mean - hat_mid * cross_mean)
    pre_low = gelu_back(act_grad)[0].astype(BF16)
    fc1_bias_grad = jnp.sum(pre_low.astype(F32), axis=0)
    pre_split = pre_low.reshape(tokens_dev, wide, -1)
    fc1_grad = jnp.einsum("td,twf->wdf", rows_low, pre_split, preferred_element_type=F32)
    rows_grad = jnp.einsum("twf,wdf->td", pre_split, fc1_full, preferred_element_type=F32)
    hidden_grad = jnp.stack([mid_gain_grad, mid_bias_grad, fc1_bias_grad])
    out_bias_total = jnp.sum(grad_in, axis=0)
    residual_grad = grad_in + norm_back(rows_grad, hat_two, scale_two, vectors[2])
    gain_two_grad = jnp.sum(rows_grad * hat_two, axis=0)
    bias_two_grad = jnp.sum(rows_grad, axis=0)
    gain_post_grad = jnp.sum(residual_grad * hat_post, axis=0)
    bias_post_grad = jnp.sum(residual_grad, axis=0)
    proj_low = norm_back(residual_grad, hat_post, scale_post, vectors[1]).astype(BF16)
    proj_bias_grad = jnp.sum(proj_low.astype(F32), axis=0)
    out_weight_grad = jnp.einsum("td,te->de", mixed_low, proj_low, preferred_element_type=F32)
    mixed_grad = jnp.einsum(
        "te,de->td", proj_low, out_full, preferred_element_type=F32
    ).reshape(tokens_dev, heads_count, head_size)
    head_grad = jnp.sum(mixed_grad * attended, axis=(0, 2))
    attended_low = (mixed_grad * heads_low[None, :, None]).astype(BF16)
    probs = jnp.exp(masked_scores() - log_totals)
    probs_grad = jnp.einsum("qhd,khd->hqk", attended_low, values_all, preferred_element_type=F32)
    delta = jnp.transpose(jnp.sum(attended_low.astype(F32) * attended, axis=-1))[:, :, None]
    scores_low = (probs * (probs_grad - delta)).astype(BF16)
    query_grad = (
        (
            jnp.einsum("hqk,khd->qhd", scores_low, keys_all, preferred_element_type=F32)
            * score_scale
        )
        .astype(BF16)
        .reshape(tokens_dev, width)
    )
    key_grad = (
        jnp.einsum("hqk,qhd->khd", scores_low, queries_split, preferred_element_type=F32)
        * score_scale
    )
    value_grad = jnp.einsum(
        "hqk,qhd->khd", probs.astype(BF16), attended_low, preferred_element_type=F32
    )
    pair_low = jnp.concatenate(
        [key_grad.reshape(-1, width), value_grad.reshape(-1, width)], axis=1
    ).astype(BF16)
    query_bias_grad = jnp.sum(query_grad.astype(F32), axis=0)
    value_bias_grad = jnp.sum(pair_low[:, width:].astype(F32), axis=0)
    qkv_grad = jnp.concatenate(
        [
            jnp.einsum("td,te->de", normed_low[own], query_grad, preferred_element_type=F32),
            jnp.einsum("td,te->de", normed_low, pair_low, preferred_element_type=F32),
        ],
        axis=1,
    )
    normed_grad = jnp.einsum("te,de->td", pair_low, qkv_full[:, width:], preferred_element_type=F32)
    halo_grad = normed_grad[: 2 * tokens_dev]
    own_grad = normed_grad[own] + jnp.einsum(
        "te,de->td", query_grad, qkv_full[:, :width], preferred_element_type=F32
    )
    gain_in_grad = jnp.sum(halo_grad * hat_in[: 2 * tokens_dev], axis=0) + jnp.sum(
        own_grad * hat_in[own], axis=0
    )
    bias_in_grad = jnp.sum(halo_grad, axis=0) + jnp.sum(own_grad, axis=0)
    vector_grad = jnp.stack(
        [
            gain_in_grad,
            gain_post_grad,
            gain_two_grad,
            bias_in_grad,
            query_bias_grad,
            value_bias_grad,
            proj_bias_grad,
            bias_post_grad,
            bias_two_grad,
            out_bias_total,
        ]
    )
    small_grad = pack(
        [
            to_slabs(vector_grad, wide),
            to_slabs(hidden_grad, wide),
            jnp.broadcast_to(head_grad[None], (wide, heads_count)),
        ]
    )
    counted = (vector_size + hidden_size) // 128
    fc1_rows, fc2_rows = fc1_weight.shape[0], fc2_weight.shape[0]
    qkv_rows, out_rows = qkv_weight.shape[0], out_weight.shape[0]
    small_part, qkv_part, out_part, fc1_part, fc2_part, halo_back, norm_tile = reduce_all(
        [
            small_grad,
            qkv_grad.astype(BF16).reshape(wide, -1, 3 * width),
            out_weight_grad.astype(BF16).reshape(wide, -1, width),
            fc1_grad.astype(BF16),
            fc2_grad.astype(BF16).reshape(wide, -1, width),
        ],
        halo_grad.astype(BF16).reshape(2, tokens_dev, width),
        (
            (3, 0, fc1_rows // 2, fc1_rows // 8, fc1_rows // 2),
            (3, fc1_rows // 2, fc1_rows // 2, fc1_rows // 8, fc1_rows // 2),
            (4, 0, fc2_rows // 2, fc2_rows // 8, fc2_rows // 2),
            (4, fc2_rows // 2, fc2_rows // 2, fc2_rows // 8, fc2_rows // 2),
            (0, 0, small_grad.shape[1], 0, counted),
            (1, 0, qkv_rows, qkv_rows // 4, qkv_rows),
            (2, 0, out_rows, out_rows // 4, out_rows),
        ),
    )
    total_grad = own_grad + halo_back[0].astype(F32) + halo_back[1].astype(F32)
    input_grad = residual_grad + norm_back(total_grad, hat_in[own], scale_in[own], vectors[0])
    flat = small_part.reshape(-1)
    vector_part = flat[:vector_size].reshape(model_vectors.shape)
    hidden_part = flat[vector_size : vector_size + hidden_size].reshape(hidden_vectors.shape)
    head_total = flat[vector_size + hidden_size :][:heads_count]
    grad_norm = jnp.sqrt(jnp.sum(norm_tile) + jnp.sum(head_total * head_total))
    factor = jnp.minimum(1.0, clip_limit / (grad_norm + 1e-06))
    step = step_count[0].astype(F32)
    grads = (qkv_part, out_part, fc1_part, fc2_part, vector_part, hidden_part, head_total)
    params = (
        qkv_weight,
        out_weight,
        fc1_weight,
        fc2_weight,
        model_vectors,
        hidden_vectors,
        head_scale,
    )
    firsts = (qkv_first, out_first, fc1_first, fc2_first, vectors_first, hidden_first, head_first)
    seconds = (
        qkv_second,
        out_second,
        fc1_second,
        fc2_second,
        vectors_second,
        hidden_second,
        head_second,
    )
    rates = (
        matrix_rate,
        matrix_rate,
        matrix_rate,
        matrix_rate,
        vector_rate,
        vector_rate,
        vector_rate,
    )
    decays = (weight_decay, weight_decay, weight_decay, weight_decay, 0.0, 0.0, 0.0)
    updated = []
    for number in range(7):
        updated.extend(
            adam_step(
                grads[number] * factor,
                params[number],
                firsts[number],
                seconds[number],
                step,
                rates[number],
                decays[number],
            )
        )
    return (
        output,
        input_grad,
        grad_norm.reshape(1),
        updated[0],
        updated[1],
        updated[2],
        updated[3],
        updated[4],
        updated[5],
        updated[6],
        updated[7],
        updated[8],
        updated[9],
        updated[10],
        updated[11],
        updated[12],
        updated[13],
        updated[14],
        updated[15],
        updated[16],
        updated[17],
        updated[18],
        updated[19],
        updated[20],
    )


def solution(mesh):
    placed = (
        P(("dp", "wide"), None),
        P(("dp", "wide"), None),
        P(),
        P(),
        P("wide", None),
        P("wide", None),
        P("wide", None),
        P("wide", None),
        P("wide", None),
        P("wide", None),
        P(None, "wide"),
        P(None, "wide"),
        P(None, "wide"),
        P("wide", None),
        P("wide", None),
        P("wide", None),
        P(None, "wide"),
        P(None, "wide"),
        P(None, "wide"),
        P(None, "wide"),
        P(None, "wide"),
        P(None, "wide"),
        P(),
        P(),
        P(),
    )
    return jax.shard_map(
        body,
        mesh=mesh,
        in_specs=placed,
        out_specs=(
            P(("dp", "wide"), None),
            P(("dp", "wide"), None),
            P(),
            P("wide", None),
            P("wide", None),
            P("wide", None),
            P("wide", None),
            P("wide", None),
            P("wide", None),
            P(None, "wide"),
            P(None, "wide"),
            P(None, "wide"),
            P("wide", None),
            P("wide", None),
            P("wide", None),
            P(None, "wide"),
            P(None, "wide"),
            P(None, "wide"),
            P(None, "wide"),
            P(None, "wide"),
            P(None, "wide"),
            P(),
            P(),
            P(),
        ),
        check_vma=False,
    )
```

time: 1410 us -> 773 us (0.55)
  waiting for transfers between devices: 798 us -> 0 us
  Pallas kernels: 0 us -> 319 us
  blocking collectives: 196 us -> 0 us
  other arithmetic: 96.5 us -> 125 us
  local copies, waits for them, and re-layouts: 30.1 us -> 57.1 us
  between operations: 22.4 us -> 5.37 us
    reduce_scatter x4 -> x0, waiting for transfers between devices: 455 us -> none  [the longest x1 182 us: body(): lax.psum_scatter(fc2_grad, 'wide', scatter_dimension=0, tiled=True)]
    pallas_call x0 -> x2, Pallas kernels: none -> 319 us  [the longest x1 187 us: reduce_all(): pl.pallas_call(functools.partial(reduce_kernel, pieces), out_shape=out_sh...]
    all_gather x2 -> x0, blocking collectives: 154 us -> none  [the longest x1 131 us: body(): lax.all_gather(hidden_vectors.astype(jnp.bfloat16), 'wide', axis=1, tiled...]
    ppermute x4 -> x0, waiting for transfers between devices: 124 us -> none  [from_behind(): return lax.ppermute(shard, axis, pairs)]
    unnamed x13 -> x0, waiting for transfers between devices: 107 us -> none
    psum x1 -> x0, waiting for transfers between devices: 77.6 us -> none  [body(): lax.psum((qkv_part, out_part, fc1_part, fc2_part, vector_part, hidden_par...]
    psum x2 -> x0, blocking collectives: 42 us -> none  [the longest x1 33.7 us: body(): norm_terms = lax.psum((local_squares, summed[6]), 'wide')]
    all_gather x4 -> x0, waiting for transfers between devices: 34.8 us -> none  [the longest x1 34.8 us: body(): lax.all_gather(qkv_weight.astype(jnp.bfloat16), 'wide', axis=0, tiled=True)]
  transfers between devices with their start and end apart: 15 -> 0, of which waited for: 8 -> 0; matrix products, arithmetic and copies ran while one was open for 21% -> 0% of each run, Pallas kernels for 0% -> 0%
where the time goes in v1:
time: 773 us; the launch traced here: 768 us
  Pallas kernels  319 us (41%)
  matrix products  261 us (34%)
  other arithmetic  125 us (16%)
  local copies, waits for them, and re-layouts  57.1 us (7%)
    pallas_call x1, Pallas kernels, reduce_all(): pl.pallas_call(functools.partial(reduce_kernel, pieces), out_shape=out_sh...  187 us
    pallas_call x1, Pallas kernels, gather_all(): pl.pallas_call(functools.partial(gather_kernel, thirds), out_shape=out_sh...  132 us
    dot_general x1, matrix products, body(): jnp.einsum('qhd,khd->hqk', attended_low, values_all, preferred_element_ty...  31.6 us
    dot_general x1, matrix products, body(): jnp.einsum('td,fd->tf', out_grad, fc2_full, preferred_element_type=F32)  30.3 us
    dot_general x1, matrix products, body(): jnp.einsum('hqk,khd->qhd', probs_low, values_all, preferred_element_type=...  22.7 us
    dot_general x1, matrix products, body(): jnp.einsum('hqk,qhd->khd', probs.astype(BF16), attended_low, preferred_el...  22.5 us
    dot_general x1, matrix products, masked_scores(): jnp.einsum('qhd,khd->hqk', queries_split, keys_all, preferred_element_typ...  22.4 us
    reduce_sum x1, other arithmetic, body(): first_mean = jnp.mean(activated, axis=-1, keepdims=True)  22.1 us

profile of v1, /device:TPU:0, one launch (start us, length us, event | category | flops | bytes accessed | tf_op | source)
XLA Modules:
  0.0 767.8 jit_solution(12547209167498151009)
XLA Ops:
  8.2 132.1 %gather_all.1 = (bf16[16,16,128]{2,1,0:T(8,128)(2,1)S(1)}, bf16[16,64,3072]{2,1,0:T(8,128)(2,1)S(1)}, bf16[16,64,1024]{2,1,0:T(8,128)(2,1)S(1)}, bf16[16,1024,25...) custom-call(bf16[16,128]{1,0:T(8,128)(2,1)S(1)} %bitcast.209, ...), custom_call_target="tpu_custom_call" | custom-call | tf_op jit(solution)/shard_map/gather_all/pallas_call | solution.py:315
  157.6 4.0 fusion.23
  161.7 12.3 %fusion.45 = f32[1536,2048]{1,0:T(8,128)} fusion(bf16[1536,1024]{1,0:T(8,128)(2,1)S(1)} %get-tuple-element.117, bf16[1024,3072]{1,0:T(8,128)(2,1)} %bitcast.204), kind=kOutput, calls=%fused_computation.93 | convolution fusion | flops 6442450944 | bytes 19922944 | tf_op jit(solution)/shard_map/dot_general | solution.py:671
  174.1 5.5 fusion.27
  179.6 4.7 copy.71
  185.6 4.3 add_convert_fusion.7
  191.5 5.4 slice.228
  196.9 4.7 copy.73
  201.6 22.4 %fusion.2 = (f32[16,512]{1,0:T(8,128)S(1)}, f32[16,512,1536]{2,1,0:T(8,128)}) fusion(pred[512,1536]{1,0:T(8,128)(4,1)S(1)} %compare_and_fusion, bf16[512,16,64]{0,2,1:T(8,128)(2,1)S(1)} %bitcast.218, bf16[1536,16,64]{0,2,1:T(8,128)(2,1)} %bitcast.215), kind=kOutput, calls=%fused_computation.7 | convolution fusion | flops 1648353280 | bytes 55345152 | tf_op jit(solution)/shard_map/qhd,khd->hqk/dot_general | solution.py:690
  224.0 22.1 %fusion = f32[16,512]{1,0:T(8,128)S(1)} fusion(f32[16,512,1536]{2,1,0:T(8,128)} %get-tuple-element.128, f32[16,512]{1,0:T(8,128)S(1)} %get-tuple-element.127, pred[512,1536]{1,0:T(8,128)(4,1)S(1)} %compare_and_fusion), kind=kLoop, calls=%fused_computation.5 | loop fusion | flops 50323456 | bytes 51183616 | tf_op jit(solution)/shard_map/reduce_sum | solution.py:698
  246.1 22.7 %fusion.51 = (bf16[512,16,64]{0,2,1:T(8,128)(2,1)S(1)}, f32[16,64,512]{2,1,0:T(8,128)}) fusion(f32[16]{0:T(128)S(1)} %convert_element_type.184, bf16[1536,16,64]{0,2,1:T(8,128)(2,1)} %bitcast.229, f32[16,512,1536]{2,1,0:T(8,128)} %get-tuple-element.128, f32[16,512]{1,0:T(8,128)S(1)} %fusion, f32[16,512]{1,0:T(8,128)S(1)} %get-tuple-element.127, ...), kind=kOutput, calls=%fused_computation.114 | convolution fusion | flops 1674575872 | bytes 57475136 | tf_op jit(solution)/shard_map/hqk,khd->qhd/dot_general | solution.py:701
  275.6 11.2 %fusion.37 = (u16[512,256]{0,1:T(8,128)(2,1)S(1)}, u16[512,256]{0,1:T(8,128)(2,1)S(1)}, f32[512,16,256]{0,2,1:T(8,128)S(1)}) fusion(f32[16,256]{1,0:T(8,128)S(1)} %bitcast.252, bf16[16,1024,256]{2,1,0:T(8,128)(2,1)} %copy-done.5, f32[512,1024]{1,0:T(8,128)} %get-tuple-element.115, f32[1024]{0:T(1024)S(1)} %add.414, f32[1024]{0:T(1024)S(1)} %mul.624, ...), kind=kOutput, calls=%fused_computation.85 | convolution fusion | flops 4326686720 | bytes 19427328 | tf_op jit(solution)/shard_map/td,wdf->twf/dot_general | solution.py:711
  286.8 22.1 %fusion.91 = (f32[512]{0:T(512)S(1)}, f32[512]{0:T(512)S(1)}, f32[512,16,256]{0,2,1:T(8,128)}) fusion(u16[512,256]{0,1:T(8,128)(2,1)S(1)} %get-tuple-element.54, u16[512,256]{0,1:T(8,128)(2,1)S(1)} %get-tuple-element.53, f32[512,16,256]{0,2,1:T(8,128)S(1)} %get-tuple-element.133, f32[16,256]{1,0:T(8,128)S(1)} %bitcast.253), kind=kLoop, calls=%fused_computation.250 | loop fusion | flops 153091072 | bytes 17321984 | tf_op jit(solution)/shard_map/reduce_sum | solution.py:717
  309.0 12.2 %fusion.50 = bf16[512,1024]{1,0:T(8,128)(2,1)} fusion(f32[512,1024]{1,0:T(8,128)} %get-tuple-element.115, bf16[16,256,1024]{2,1,0:T(8,128)(2,1)} %copy-done.6, f32[512,16,256]{0,2,1:T(8,128)} %get-tuple-element.113, f32[16,256]{1,0:T(8,128)S(1)} %get-tuple-element.145, f32[16,256]{1,0:T(8,128)S(1)} %get-tuple-element.146, f32[512]{0:T(512)S(1)} %get-tuple-element.123, ...), kind=kOutput, calls=%fused_computation.109 | convolution fusion | flops 4307025920 | bytes 19963904 | tf_op jit(solution)/shard_map/dot_general | solution.py:723
  321.2 30.3 %fusion.10 = (f32[4096]{0:T(1024)S(1)}, f32[512]{0:T(512)S(1)}, f32[512]{0:T(512)S(1)}, f32[512,4096]{0,1:T(8,128)}, f32[512,4096]{0,1:T(8,128)}, /*index=5*/f32[4096,512]{1,0:T(8,128)S(1)}) fusion(f32[4096]{0:T(1024)S(1)} %bitcast.246, f32[512]{0:T(512)S(1)} %get-tuple-element.123, f32[512]{0:T(512)S(1)} %get-tuple-element.122, f32[4096]{0:T(1024)S(1)} %bitcast.244, ...), kind=kOutput, calls=%fused_computation.23 | convolution fusion | flops 4448054272 | bytes 43048960 | tf_op jit(solution)/shard_map/td,fd->tf/dot_general | solution.py:726
  351.5 14.3 %convert_reduce_fusion = (f32[4096]{0:T(1024)S(1)}, bf16[512,4096]{0,1:T(8,128)(2,1)}) fusion(f32[512,4096]{0,1:T(8,128)} %get-tuple-element.112, f32[512,4096]{0,1:T(8,128)} %get-tuple-element.111, f32[512]{0:T(512)S(1)} %broadcast_multiply_fusion.1, f32[512]{0:T(512)S(1)} %broadcast_multiply_fusion.2, f32[4096]{0:T(1024)S(1)} %bitcast.247, ...), kind=kLoop, calls=%fused_computation.27 | loop fusion | flops 46133248 | bytes 37804032 | tf_op jit(solution)/shard_map/reduce_sum | solution.py:734
  365.8 8.3 %fusion.48 = (f32[1024]{0:T(1024)S(1)}, f32[512]{0:T(512)S(1)}, f32[512]{0:T(512)S(1)}, f32[1024]{0:T(1024)S(1)}, f32[512,1024,1]{1,0,2:T(8,128)S(1)}) fusion(f32[512,1024]{1,0:T(8,128)} %get-tuple-element.115, f32[512]{0:T(512)S(1)} %add_rsqrt_fusion.2, f32[512]{0:T(512)S(1)} %broadcast_multiply_fusion.10, f32[1024]{0:T(1024)S(1)} %mul.624, ...), kind=kOutput, calls=%fused_computation.106 | convolution fusion | flops 4299682816 | bytes 16797696 | tf_op jit(solution)/shard_map/twf,wdf->td/dot_general | solution.py:737
  378.0 4.0 reduce_sum.383
  388.8 22.5 %fusion.41 = bf16[16,64,1536]{2,1,0:T(8,128)(2,1)} fusion(bf16[512,16,64]{0,2,1:T(8,128)(2,1)S(1)} %get-tuple-element.109, f32[16,512,1536]{2,1,0:T(8,128)} %get-tuple-element.128, f32[16,512]{1,0:T(8,128)S(1)} %log_add_fusion, pred[512,1536]{1,0:T(8,128)(4,1)S(1)} %copy-done.19), kind=kOutput, calls=%fused_computation.89 | convolution fusion | flops 1662517248 | bytes 55345152 | tf_op jit(solution)/shard_map/hqk,qhd->khd/dot_general | solution.py:769
  411.3 31.6 %multiply_convert_fusion = bf16[16,512,1536]{2,1,0:T(8,128)(2,1)} fusion(f32[16,512,1536]{2,1,0:T(8,128)} %get-tuple-element.128, bf16[512,16,64]{0,2,1:T(8,128)(2,1)} %copy-done.70, bf16[1536,16,64]{0,2,1:T(8,128)(2,1)} %bitcast.230, f32[16,512]{1,0:T(8,128)S(1)} %bitcast.257, f32[16,512]{1,0:T(8,128)S(1)} %log_add_fusion, pred[512,1536]{1,0:T(8,128)(4,1)S(1)} %copy-done.20), kind=kOutput, calls=%fused_computation | convolution fusion | flops 1686110208 | bytes 80543744 | tf_op jit(solution)/shard_map/qhd,khd->hqk/dot_general | solution.py:754
  442.9 14.3 %multiply_convert_fusion.1 = bf16[16,64,1536]{2,1,0:T(8,128)(2,1)} fusion(bf16[512,16,64]{0,2,1:T(8,128)(2,1)S(1)} %bitcast.219, bf16[16,512,1536]{2,1,0:T(8,128)(2,1)} %multiply_convert_fusion), kind=kOutput, calls=%fused_computation.73 | convolution fusion | flops 1613758464 | bytes 29360128 | tf_op jit(solution)/shard_map/hqk,qhd->khd/dot_general | solution.py:766
  457.2 10.2 %fusion.39 = f32[1536,1024]{1,0:T(8,128)S(1)} fusion(bf16[1536,1024]{0,1:T(8,128)(2,1)} %bitcast.231, bf16[1536,1024]{0,1:T(8,128)(2,1)} %bitcast.227, bf16[1024,3072]{1,0:T(8,128)(2,1)} %bitcast.206), kind=kOutput, calls=%fused_computation.87 | convolution fusion | flops 6455033856 | bytes 16777216 | tf_op jit(solution)/shard_map/te,de->td/dot_general | solution.py:784
  471.7 13.8 %convert_reduce_fusion.5 = (f32[16,64]{1,0:T(8,128)S(1)}, bf16[16,64,512]{2,1,0:T(8,128)(2,1)}) fusion(bf16[1536,16,64]{0,2,1:T(8,128)(2,1)S(1)} %bitcast.216, bf16[16,512,1536]{2,1,0:T(8,128)(2,1)} %multiply_convert_fusion), kind=kOutput, calls=%fused_computation.120 | convolution fusion | flops 1612708864 | bytes 29364224 | tf_op jit(solution)/shard_map/hqk,khd->qhd/dot_general | solution.py:759
  485.5 4.5 fusion.93
  494.1 11.7 %fusion.40 = bf16[1024,2048]{1,0:T(8,128)(2,1)} fusion(bf16[1536,1024]{1,0:T(8,128)(2,1)} %copy-done.23, bf16[1536,1024]{0,1:T(8,128)(2,1)} %bitcast.232, bf16[1536,1024]{0,1:T(8,128)(2,1)} %bitcast.228), kind=kOutput, calls=%fused_computation.88 | convolution fusion | flops 6457131008 | bytes 13631488 | tf_op jit(solution)/shard_map/td,te->de/dot_general | solution.py:780
  510.4 4.0 convolution_convert_fusion.2
  514.4 5.0 pad_maximum_fusion.1.refs_1_
  523.2 7.0 convert_bitcast_fusion
  530.2 12.4 %copy.79 = bf16[16,1024,256]{2,1,0:T(8,128)(2,1)} copy(bf16[16,1024,256]{1,2,0:T(8,128)(2,1)} %convert_bitcast_fusion) | data formatting | bytes 16777216 | tf_op jit(solution)/shard_map/convert_element_type | solution.py:822
  542.6 9.2 %convolution_convert_fusion = bf16[4096,1024]{1,0:T(8,128)(2,1)} fusion(bf16[512,1024]{1,0:T(8,128)(2,1)S(1)} %copy-done.37, f32[512,4096]{0,1:T(8,128)} %get-tuple-element.111, f32[4096]{0:T(1024)S(1)} %bitcast.251, f32[4096]{0:T(1024)S(1)} %bitcast.248), kind=kOutput, calls=%fused_computation.62 | convolution fusion | flops 4305453056 | bytes 17858560 | tf_op jit(solution)/shard_map/tf,td->fd/dot_general | solution.py:725
  555.6 186.7 %reduce_all.1 = (f32[16,128]{1,0:T(8,128)}, f32[64,3072]{1,0:T(8,128)}, f32[64,1024]{1,0:T(8,128)}, f32[1024,256]{1,0:T(8,128)}, f32[256,1024]{1,0:T(8,128)}, /*...) custom-call(f32[4,2,2,16,128]{4,3,2,1,0:T(8,128)} %bitcast.236, bf16[4,2,2,64,3072]{4,3,2,1,0:T(8,128)(2,1)} %pad_maximum_fusion.1.refs_1_, ...), custom_call_target="tpu_custom_call" | custom-call | tf_op jit(solution)/shard_map/reduce_all/pallas_call | solution.py:551
  758.0 4.0 multiply_subtract_fusion.1
  (264 shorter events, 82.8 us)
Async XLA Ops:
  0.7 153.6 %copy-start.1 = (bf16[512,1024]{1,0:T(8,128)(2,1)S(1)}, bf16[512,1024]{1,0:T(8,128)(2,1)}, u32[]{:S(2)}) copy-start(bf16[512,1024]{1,0:T(8,128)(2,1)} %refs_5_.1) | copy-start | bytes 3145732
  154.2 91.8 %copy-start.68 = (f32[16]{0:T(128)}, f32[16]{0:T(128)S(1)}, u32[]{:S(2)}) copy-start(f32[16]{0:T(128)S(1)} %convert_element_type.184) | copy-start | bytes 196
  157.5 16.6 %copy-start.47 = (f32[1536]{0:T(1024)}, f32[1536]{0:T(1024)S(1)}, u32[]{:S(2)}) copy-start(f32[1536]{0:T(1024)S(1)} %add_rsqrt_fusion) | copy-start | bytes 18436
  157.6 16.4 %copy-start.48 = (f32[1024]{0:T(1024)}, f32[1024]{0:T(1024)S(1)}, u32[]{:S(2)}) copy-start(f32[1024]{0:T(1024)S(1)} %mul.601) | copy-start | bytes 12292
  161.7 12.4 %copy-start.23 = (bf16[1536,1024]{1,0:T(8,128)(2,1)}, bf16[1536,1024]{1,0:T(8,128)(2,1)S(1)}, u32[]{:S(2)}) copy-start(bf16[1536,1024]{1,0:T(8,128)(2,1)S(1)} %get-tuple-element.117) | copy-start | bytes 9437188
  185.5 38.4 %copy-start.18 = (pred[512,1536]{1,0:T(8,128)(4,1)}, pred[512,1536]{1,0:T(8,128)(4,1)S(1)}, u32[]{:S(2)}) copy-start(pred[512,1536]{1,0:T(8,128)(4,1)S(1)} %compare_and_fusion) | copy-start | bytes 2359300
  191.5 32.5 %copy-start.16 = (bf16[512,1024]{0,1:T(8,128)(2,1)}, bf16[512,1024]{0,1:T(8,128)(2,1)S(1)}, u32[]{:S(2)}) copy-start(bf16[512,1024]{0,1:T(8,128)(2,1)S(1)} %copy.72) | copy-start | bytes 3145732
  224.0 22.1 %copy-start.38 = (f32[16,512]{1,0:T(8,128)}, f32[16,512]{1,0:T(8,128)S(1)}, u32[]{:S(2)}) copy-start(f32[16,512]{1,0:T(8,128)S(1)} %get-tuple-element.127) | copy-start | bytes 98308
  246.1 22.8 %copy-start.42 = (f32[16,512]{1,0:T(8,128)}, f32[16,512]{1,0:T(8,128)S(1)}, u32[]{:S(2)}) copy-start(f32[16,512]{1,0:T(8,128)S(1)} %fusion) | copy-start | bytes 98308
  246.1 22.8 %copy-start.3 = (bf16[16,64,1024]{2,1,0:T(8,128)(2,1)S(1)}, bf16[16,64,1024]{2,1,0:T(8,128)(2,1)}, u32[]{:S(2)}) copy-start(bf16[16,64,1024]{2,1,0:T(8,128)(2,1)} %copy-done.2) | copy-start | bytes 6291460
  246.1 24.6 %copy-start.46 = (f32[1024]{0:T(1024)S(1)}, f32[1024]{0:T(1024)}, u32[]{:S(2)}) copy-start(f32[1024]{0:T(1024)} %mul.618) | copy-start | bytes 12292
  246.1 24.6 %copy-start.55 = (f32[1024]{0:T(1024)S(1)}, f32[1024]{0:T(1024)}, u32[]{:S(2)}) copy-start(f32[1024]{0:T(1024)} %add.409) | copy-start | bytes 12292
  273.5 35.4 %copy-start.44 = (f32[1,16,256]{2,0,1:T(1,128)}, f32[1,16,256]{2,0,1:T(1,128)S(1)}, u32[]{:S(2)}) copy-start(f32[1,16,256]{2,0,1:T(1,128)S(1)} %get-tuple-element.120) | copy-start | bytes 49156
  273.6 13.2 %copy-start.59 = (f32[1024]{0:T(1024)}, f32[1024]{0:T(1024)S(1)}, u32[]{:S(2)}) copy-start(f32[1024]{0:T(1024)S(1)} %add.414) | copy-start | bytes 12292
  286.8 22.1 %copy-start.10 = (f32[512,16,256]{0,2,1:T(8,128)}, f32[512,16,256]{0,2,1:T(8,128)S(1)}, u32[]{:S(2)}) copy-start(f32[512,16,256]{0,2,1:T(8,128)S(1)} %get-tuple-element.133) | copy-start | bytes 25165828
  286.8 22.1 %copy-start.51 = (f32[16,64]{1,0:T(8,128)S(1)}, f32[16,64]{1,0:T(8,128)}, u32[]{:S(2)}) copy-start(f32[16,64]{1,0:T(8,128)} %get-tuple-element.73) | copy-start | bytes 12292
  309.0 12.2 %copy-start.11 = (f32[512,16,256]{0,2,1:T(8,128)S(1)}, f32[512,16,256]{0,2,1:T(8,128)}, u32[]{:S(2)}) copy-start(f32[512,16,256]{0,2,1:T(8,128)} %copy-done.10) | copy-start | bytes 25165828
  309.0 12.2 %copy-start.36 = (bf16[512,1024]{1,0:T(8,128)(2,1)S(1)}, bf16[512,1024]{1,0:T(8,128)(2,1)}, u32[]{:S(2)}) copy-start(bf16[512,1024]{1,0:T(8,128)(2,1)} %param.26) | copy-start | bytes 3145732
  309.0 56.8 %slice-start = ((s8[8388608]{0:T(1024)(128)(4,1)}), s8[4194304]{0:T(1024)(128)(4,1)S(1)}, s32[]{:S(2)}) async-start(s8[8388608]{0:T(1024)(128)(4,1)} %bitcast.210), calls=%async_computation | async-start | bytes 8388608
  321.2 44.6 %slice-start.1 = ((s8[8388608]{0:T(1024)(128)(4,1)}), s8[4194304]{0:T(1024)(128)(4,1)S(1)}, s32[]{:S(2)}) async-start(s8[8388608]{0:T(1024)(128)(4,1)} %bitcast.210), calls=%async_computation.1 | async-start | bytes 8388608
  351.5 14.3 %copy-start.12 = (f32[4096,512]{1,0:T(8,128)}, f32[4096,512]{1,0:T(8,128)S(1)}, u32[]{:S(2)}) copy-start(f32[4096,512]{1,0:T(8,128)S(1)} %get-tuple-element.134) | copy-start | bytes 25165828
  385.2 26.1 %copy-start.33 = (bf16[512,1024]{1,0:T(8,128)(2,1)}, bf16[512,1024]{1,0:T(8,128)(2,1)S(1)}, u32[]{:S(2)}) copy-start(bf16[512,1024]{1,0:T(8,128)(2,1)S(1)} %get-tuple-element.106) | copy-start | bytes 3145732
  388.7 22.5 %copy-start.70 = (bf16[512,16,64]{0,2,1:T(8,128)(2,1)}, bf16[512,16,64]{0,2,1:T(8,128)(2,1)S(1)}, u32[]{:S(2)}) copy-start(bf16[512,16,64]{0,2,1:T(8,128)(2,1)S(1)} %get-tuple-element.109) | copy-start | bytes 3145732
  388.8 22.5 %copy-start.20 = (pred[512,1536]{1,0:T(8,128)(4,1)S(1)}, pred[512,1536]{1,0:T(8,128)(4,1)}, u32[]{:S(2)}) copy-start(pred[512,1536]{1,0:T(8,128)(4,1)} %copy-done.18) | copy-start | bytes 2359300
  411.3 31.6 %copy-start.17 = (bf16[512,1024]{0,1:T(8,128)(2,1)S(1)}, bf16[512,1024]{0,1:T(8,128)(2,1)}, u32[]{:S(2)}) copy-start(bf16[512,1024]{0,1:T(8,128)(2,1)} %copy-done.16) | copy-start | bytes 3145732
  442.9 24.6 %slice-start.2 = ((s8[6291456]{0:T(1024)(128)(4,1)}), s8[2097152]{0:T(1024)(128)(4,1)S(1)}, s32[]{:S(2)}) async-start(s8[6291456]{0:T(1024)(128)(4,1)} %bitcast.213), calls=%async_computation.2 | async-start | bytes 4194304
  494.1 16.3 %copy-start.22 = (bf16[16,64,512]{2,1,0:T(8,128)(2,1)S(1)}, bf16[16,64,512]{2,1,0:T(8,128)(2,1)}, u32[]{:S(2)}) copy-start(bf16[16,64,512]{2,1,0:T(8,128)(2,1)} %get-tuple-element.138) | copy-start | bytes 3145732
  530.2 12.4 %copy-start.37 = (bf16[512,1024]{1,0:T(8,128)(2,1)S(1)}, bf16[512,1024]{1,0:T(8,128)(2,1)}, u32[]{:S(2)}) copy-start(bf16[512,1024]{1,0:T(8,128)(2,1)} %param.26) | copy-start | bytes 3145732
  530.2 12.4 %copy-start.45 = (f32[1,16,256]{2,0,1:T(1,128)S(1)}, f32[1,16,256]{2,0,1:T(1,128)}, u32[]{:S(2)}) copy-start(f32[1,16,256]{2,0,1:T(1,128)} %copy-done.44) | copy-start | bytes 49156
  555.6 186.8 %copy-start.49 = (f32[1024]{0:T(1024)S(1)}, f32[1024]{0:T(1024)}, u32[]{:S(2)}) copy-start(f32[1024]{0:T(1024)} %copy-done.48) | copy-start | bytes 12292
  745.4 12.6 %copy-start.25 = (f32[1024,256]{1,0:T(8,128)S(1)}, f32[1024,256]{1,0:T(8,128)}, u32[]{:S(2)}) copy-start(f32[1024,256]{1,0:T(8,128)} %param.35) | copy-start | bytes 3145732
  748.9 13.1 %copy-start.26 = (f32[256,1024]{1,0:T(8,128)S(1)}, f32[256,1024]{1,0:T(8,128)}, u32[]{:S(2)}) copy-start(f32[256,1024]{1,0:T(8,128)} %param.38) | copy-start | bytes 3145732
  (44 other events, 297.6 us)

commit v2 on v1

--- a/solution.py
+++ b/solution.py
@@ -50,15 +50,10 @@
     return jax.nn.gelu(values_in, approximate=False)
 
 
-def doc_labels(doc_lengths, start, count, row_length):
-    doc_count = doc_lengths.shape[1]
-    places = start + jnp.arange(count, dtype=jnp.int32)
-    row_number = start // row_length
-    ends = jnp.cumsum(doc_lengths, axis=1)
-    row_ends = lax.dynamic_slice_in_dim(ends, jnp.maximum(row_number, 0), 1, 0)[0]
-    within = places - row_number * row_length
-    document = jnp.sum((within[:, None] >= row_ends[None, :]).astype(jnp.int32), axis=1)
-    return (row_number * doc_count + document, places)
+def doc_starts(doc_lengths, row, first, count):
+    ends = lax.dynamic_slice_in_dim(jnp.cumsum(doc_lengths, axis=1), row, 1, 0)[0]
+    places = first + jnp.arange(count, dtype=jnp.int32)
+    return jnp.max(jnp.where(ends[None, :] <= places[:, None], ends[None, :], 0), axis=1)
 
 
 def adam_step(grad, weight, first, second, step, rate, decay):
@@ -248,12 +243,12 @@
 AG_SEMS = 36
 
 
-def run_all(steps):
+def run_all(steps, at_once):
     waiting, active = list(steps), []
     while waiting or active:
-        if waiting:
-            active.append(waiting.pop(0))
-        active = [one for one in reversed(active) if next(one, active) is not active][::-1]
+        active = waiting[:at_once] + active
+        del waiting[:at_once]
+        active = [one for one in active if next(one, active) is not active]
 
 
 def gather_kernel(thirds, *refs):
@@ -296,7 +291,8 @@
             ag_steps(me, wire, AG_SEMS * k, own, full, third)
             for k, (own, full, third) in enumerate(zip(owns, fulls, thirds))
         ]
-        + [halo_steps()]
+        + [halo_steps()],
+        count + 1,
     )
     wire.finish()
     for one in keep:
@@ -454,10 +450,11 @@
 def reduce_kernel(pieces, *refs):
     refs = list(refs)
     arrays = 1 + max(piece[0] for piece in pieces)
+    results = 1 + max(piece[5] for piece in pieces)
     count = len(pieces)
     grads, halo = refs[:arrays], refs[arrays]
-    finals, back, norm = refs[arrays + 1 : 2 * arrays + 1], refs[2 * arrays + 1], refs[2 * arrays + 2]
-    scratch = refs[2 * arrays + 3 :]
+    finals, (back, norm) = refs[arrays + 1 :][:results], refs[arrays + 1 + results :][:2]
+    scratch = refs[arrays + 3 + results :]
     blank, passing, joined, tiles, send, recv, local = scratch[-7:]
     me = Place()
     ending = RS_SEMS * count
@@ -498,16 +495,17 @@
         yield
 
     sequences = []
-    for k, (number, first, rows, quarter, limit) in enumerate(pieces):
+    for k, (number, first, rows, quarter, limit, result, column) in enumerate(pieces):
         here = pl.ds(first, rows)
+        final = finals[result].at[here, pl.ds(column, grads[number].shape[-1])]
         sequences.append(
             rs_steps(
                 me, wire, RS_SEMS * k, local.at[k],
                 grads[number].at[:, :, :, here], quarter, scratch[7 * k],
-                scratch[7 * k + 1 : 7 * k + 7], finals[number].at[here], tiles.at[0], limit,
+                scratch[7 * k + 1 : 7 * k + 7], final, tiles.at[0], limit,
             )
         )
-    run_all([sequences[0], halo_steps(), *sequences[1:]])
+    run_all([sequences[0], halo_steps(), *sequences[1:]], 1)
     for k, partner in enumerate(rounds):
         index = ending + 3 + k
         moved = wire.copy(tiles.at[k], tiles.at[5 + k], index, partner)
@@ -540,11 +538,15 @@
     if lax.axis_size("dp") == 2 and wide == 16:
         count = len(pieces)
         tokens = halo.shape[1:]
-        out_shape = [jax.ShapeDtypeStruct(one.shape[1:], F32) for one in grads]
+        sizes = {}
+        for number, _, _, _, _, result, column in pieces:
+            _, rows, columns = grads[number].shape
+            sizes[result] = (rows, max(column + columns, sizes.get(result, (0, 0))[1]))
+        out_shape = [jax.ShapeDtypeStruct(sizes[k], F32) for k in range(len(sizes))]
         out_shape.append(jax.ShapeDtypeStruct(halo.shape, halo.dtype))
         out_shape.append(jax.ShapeDtypeStruct((8, 128), F32))
         scratch = []
-        for number, _, rows, quarter, _ in pieces:
+        for number, _, rows, quarter, *_ in pieces:
             one = grads[number]
             scratch += piece_buffers(rows, one.shape[2], quarter, one.dtype)
         sems = RS_SEMS * count + 7
@@ -552,7 +554,7 @@
             functools.partial(reduce_kernel, pieces),
             out_shape=out_shape,
             in_specs=[HBM] * (len(grads) + 1),
-            out_specs=[VMEM] * len(grads) + [HBM, VMEM],
+            out_specs=[VMEM] * len(sizes) + [HBM, VMEM],
             scratch_shapes=scratch
             + [
                 pltpu.VMEM(tokens, BF16),
@@ -568,19 +570,193 @@
             ),
             name="reduce_all",
         )(*[one.reshape(4, 2, 2, *one.shape[1:]) for one in grads], halo)
-    totals = [
+    whole = [
         lax.psum(
             lax.psum_scatter(one.astype(F32), "wide", scatter_dimension=0, tiled=False), "dp"
         )
         for one in grads
     ]
+    totals = []
+    for result in range(1 + max(piece[5] for piece in pieces)):
+        columns = {piece[6]: whole[piece[0]] for piece in pieces if piece[5] == result}
+        totals.append(jnp.concatenate([columns[key] for key in sorted(columns)], axis=1))
     back = jnp.stack([from_behind(halo[0], "wide", -2), from_behind(halo[1], "wide", -1)])
     squares = jnp.float32(0.0)
-    for number, first, rows, _, limit in pieces:
-        part = totals[number][first : first + limit]
+    for number, first, _, _, limit, *_ in pieces:
+        part = whole[number][first : first + limit]
         squares = squares + jnp.sum(part * part)
     norm = jnp.zeros((8, 128), F32).at[0, 0].set(lax.psum(squares, "wide"))
     return [*totals, back, norm]
+
+
+def dot(a, b, left=1, right=0):
+    return lax.dot_general(
+        a, b, (((left,), (right,)), ((), ())), preferred_element_type=F32
+    )
+
+
+Q_TILE = 256
+
+
+def split_pair(pair, size):
+    lane = lax.broadcasted_iota(jnp.int32, pair.shape, 1)
+    zero = jnp.zeros_like(pair)
+    return jnp.where(lane < size, pair, zero), jnp.where(lane < size, zero, pair)
+
+
+def fill_mask(starts, bias, tokens, span, keys_before):
+    for tile in range(tokens // Q_TILE):
+        query = lax.broadcasted_iota(jnp.int32, (span, Q_TILE), 1) + tile * Q_TILE + keys_before
+        key = lax.broadcasted_iota(jnp.int32, (span, Q_TILE), 0) + tile * Q_TILE
+        first = starts[:, tile * Q_TILE : (tile + 1) * Q_TILE]
+        seen = jnp.logical_and(key <= query, key >= first)
+        bias[tile] = jnp.where(seen, 0.0, masked_score)
+
+
+def attend_kernel(size, starts, scale_ref, q_ref, k_ref, v_ref, o_ref, c_ref, lse_ref, bias, vt, ot):
+    tokens, window = q_ref.shape[0], k_ref.shape[0]
+    before = window - tokens
+    span = before + Q_TILE
+
+    @pl.when(pl.program_id(0) == 0)
+    def _():
+        fill_mask(starts, bias, tokens, span, before)
+
+    vt[...] = v_ref[...].T
+    for tile in range(tokens // Q_TILE):
+        rows = slice(tile * Q_TILE, (tile + 1) * Q_TILE)
+        keys = slice(tile * Q_TILE, tile * Q_TILE + span)
+        k_pair = k_ref[keys, :]
+        for head, q_one in enumerate(split_pair(q_ref[rows, :], size)):
+            scores = dot(k_pair, q_one, 1, 1) + bias[tile]
+            highest = jnp.max(scores, axis=0, keepdims=True)
+            powers = jnp.exp(scores - highest)
+            total = jnp.sum(powers, axis=0, keepdims=True)
+            probs = (powers * (1.0 / total)).astype(BF16)
+            lse_ref[0, head : head + 1, rows] = highest + jnp.log(total)
+            part = slice(head * size, (head + 1) * size)
+            ot[part, rows] = dot(vt[part, keys], probs)
+    attended = ot[...].T
+    o_ref[...] = attended
+    c_ref[...] = (attended * scale_ref[...]).astype(BF16)
+
+
+def attend(queries, keys, values, starts, scales, heads):
+    tokens, width = queries.shape
+    window = keys.shape[0]
+    pairs = heads // 2
+    lanes = width // pairs
+    span = window - tokens + Q_TILE
+    by_rows = lambda rows: pl.BlockSpec((rows, lanes), lambda p: (0, p))
+    return pl.pallas_call(
+        functools.partial(attend_kernel, width // heads),
+        grid=(pairs,),
+        in_specs=[
+            pl.BlockSpec((1, tokens), lambda p: (0, 0)),
+            by_rows(1),
+            by_rows(tokens),
+            by_rows(window),
+            by_rows(window),
+        ],
+        out_specs=[
+            by_rows(tokens),
+            by_rows(tokens),
+            pl.BlockSpec((1, 2, tokens), lambda p: (p, 0, 0)),
+        ],
+        out_shape=[
+            jax.ShapeDtypeStruct((tokens, width), F32),
+            jax.ShapeDtypeStruct((tokens, width), BF16),
+            jax.ShapeDtypeStruct((pairs, 2, tokens), F32),
+        ],
+        scratch_shapes=[
+            pltpu.VMEM((tokens // Q_TILE, span, Q_TILE), F32),
+            pltpu.VMEM((lanes, window), BF16),
+            pltpu.VMEM((lanes, tokens), F32),
+        ],
+        compiler_params=pltpu.CompilerParams(vmem_limit_bytes=40 << 20),
+        name="attend",
+    )(starts, scales, queries, keys, values)
+
+
+def attend_back_kernel(
+    size, starts, q_ref, k_ref, v_ref, do_ref, lse_ref, delta_ref,
+    dq_ref, dk_ref, dv_ref, bias, dk_sum, dv_sum, kt, dqt,
+):
+    tokens, window = q_ref.shape[0], k_ref.shape[0]
+    before = window - tokens
+    span = before + Q_TILE
+
+    @pl.when(pl.program_id(0) == 0)
+    def _():
+        fill_mask(starts, bias, tokens, span, before)
+
+    kt[...] = k_ref[...].T
+    dk_sum[...] = jnp.zeros_like(dk_sum)
+    dv_sum[...] = jnp.zeros_like(dv_sum)
+    for tile in range(tokens // Q_TILE):
+        rows = slice(tile * Q_TILE, (tile + 1) * Q_TILE)
+        keys = slice(tile * Q_TILE, tile * Q_TILE + span)
+        k_pair, v_pair = k_ref[keys, :], v_ref[keys, :]
+        for head, (q_one, do_one) in enumerate(
+            zip(split_pair(q_ref[rows, :], size), split_pair(do_ref[rows, :], size))
+        ):
+            scores = dot(k_pair, q_one, 1, 1) + bias[tile]
+            probs = jnp.exp(scores - lse_ref[0, head : head + 1, rows])
+            grads = dot(v_pair, do_one, 1, 1) - delta_ref[0, head : head + 1, rows]
+            low = (probs * grads).astype(BF16)
+            dv_sum[keys, :] += dot(probs.astype(BF16), do_one)
+            dk_sum[keys, :] += dot(low, q_one)
+            part = slice(head * size, (head + 1) * size)
+            dqt[part, rows] = dot(kt[part, keys], low)
+    dq_ref[...] = (dqt[...].T * size ** (-0.5)).astype(BF16)
+    dk_ref[...] = dk_sum[...].astype(BF16)
+    dv_ref[...] = dv_sum[...].astype(BF16)
+
+
+def attend_back(queries, keys, values, outs_grad, lse, delta, starts, heads):
+    tokens, width = queries.shape
+    window = keys.shape[0]
+    pairs = heads // 2
+    lanes = width // pairs
+    span = window - tokens + Q_TILE
+    by_rows = lambda rows: pl.BlockSpec((rows, lanes), lambda p: (0, p))
+    stats = pl.BlockSpec((1, 2, tokens), lambda p: (p, 0, 0))
+    return pl.pallas_call(
+        functools.partial(attend_back_kernel, width // heads),
+        grid=(pairs,),
+        in_specs=[
+            pl.BlockSpec((1, tokens), lambda p: (0, 0)),
+            by_rows(tokens),
+            by_rows(window),
+            by_rows(window),
+            by_rows(tokens),
+            stats,
+            stats,
+        ],
+        out_specs=[
+            by_rows(tokens),
+            by_rows(window),
+            by_rows(window),
+        ],
+        out_shape=[
+            jax.ShapeDtypeStruct((tokens, width), BF16),
+            jax.ShapeDtypeStruct((window, width), BF16),
+            jax.ShapeDtypeStruct((window, width), BF16),
+        ],
+        scratch_shapes=[
+            pltpu.VMEM((tokens // Q_TILE, span, Q_TILE), F32),
+            pltpu.VMEM((window, lanes), F32),
+            pltpu.VMEM((window, lanes), F32),
+            pltpu.VMEM((lanes, window), BF16),
+            pltpu.VMEM((lanes, tokens), F32),
+        ],
+        compiler_params=pltpu.CompilerParams(vmem_limit_bytes=40 << 20),
+        name="attend_back",
+    )(starts, queries, keys, values, outs_grad, lse, delta)
+
+
+def plane_share(rows):
+    return rows // 16 * 3 // 8 * 16
 
 
 def pack(parts):
@@ -630,14 +806,13 @@
     heads_count = head_scale.shape[0]
     head_size = width // heads_count
     wide = lax.axis_size("wide")
-    row_length = tokens_dev * wide
     score_scale = head_size ** (-0.5)
-    block_index = lax.axis_index("dp") * wide + lax.axis_index("wide")
-    first_token = block_index * tokens_dev
     hidden_width = hidden_vectors.shape[1] * wide
     vector_rows, hidden_rows = model_vectors.shape[0], hidden_vectors.shape[0]
     vector_size, hidden_size = model_vectors.size, hidden_vectors.size
 
+    fc1_rows, fc2_rows = fc1_weight.shape[0], fc2_weight.shape[0]
+    qkv_rows, out_rows = qkv_weight.shape[0], out_weight.shape[0]
     small = pack(
         [model_vectors.astype(BF16).reshape(1, -1), hidden_vectors.astype(BF16).reshape(1, -1)]
     )[0]
@@ -649,7 +824,7 @@
             fc1_weight.astype(BF16),
             fc2_weight.astype(BF16),
         ],
-        (0, 16, 16, 256, 64),
+        tuple(plane_share(one) for one in (0, qkv_rows, out_rows, fc1_rows, fc2_rows)),
         inputs,
     )
     flat = small_full.reshape(wide, -1)
@@ -667,39 +842,18 @@
     own = slice(2 * tokens_dev, None)
     queries = (
         jnp.dot(normed_low[own], qkv_full[:, :width], preferred_element_type=F32) + vectors[4]
-    ).astype(BF16)
+    ).astype(BF16) * jnp.asarray(score_scale, BF16)
     projected = jnp.dot(normed_low, qkv_full[:, width:], preferred_element_type=F32)
-    keys_all = projected[:, :width].astype(BF16).reshape(-1, heads_count, head_size)
-    values_all = (
-        (projected[:, width:] + vectors[5]).astype(BF16).reshape(-1, heads_count, head_size)
-    )
-    labels, places = [], []
-    for back in (2, 1, 0):
-        labels_here, places_here = doc_labels(
-            doc_lengths, first_token - back * tokens_dev, tokens_dev, row_length
-        )
-        labels.append(labels_here)
-        places.append(places_here)
-    allowed = (labels[2][:, None] == jnp.concatenate(labels)[None, :]) & (
-        jnp.concatenate(places)[None, :] <= places[2][:, None]
-    )
-    queries_split = queries.reshape(tokens_dev, heads_count, head_size)
-
-    def masked_scores():
-        raw = (
-            jnp.einsum("qhd,khd->hqk", queries_split, keys_all, preferred_element_type=F32)
-            * score_scale
-        )
-        return jnp.where(allowed[None], raw, masked_score)
-
-    scores = masked_scores()
-    highest = jnp.max(scores, axis=-1, keepdims=True)
-    weights_exp = jnp.exp(scores - highest)
-    totals = jnp.sum(weights_exp, axis=-1, keepdims=True)
-    log_totals = highest + jnp.log(totals)
-    probs_low = (weights_exp / totals).astype(BF16)
-    attended = jnp.einsum("hqk,khd->qhd", probs_low, values_all, preferred_element_type=F32)
-    mixed_low = (attended * heads_low[None, :, None]).astype(BF16).reshape(tokens_dev, width)
+    keys_all = projected[:, :width].astype(BF16)
+    values_all = (projected[:, width:] + vectors[5]).astype(BF16)
+    starts = doc_starts(
+        doc_lengths, lax.axis_index("dp"), lax.axis_index("wide") * tokens_dev, tokens_dev
+    )
+    starts = jnp.maximum(starts - (lax.axis_index("wide") - 2) * tokens_dev, 0).reshape(1, -1)
+    scales = jnp.repeat(heads_low, head_size).reshape(1, width)
+    attended, mixed_low, log_totals = attend(
+        queries, keys_all, values_all, starts, scales, heads_count
+    )
     proj_out = jnp.dot(mixed_low, out_full, preferred_element_type=F32) + vectors[6]
     normed_post, hat_post, scale_post = layer_norm(proj_out, vectors[1], vectors[7])
     residual = tokens_in + normed_post
@@ -745,43 +899,25 @@
     proj_low = norm_back(residual_grad, hat_post, scale_post, vectors[1]).astype(BF16)
     proj_bias_grad = jnp.sum(proj_low.astype(F32), axis=0)
     out_weight_grad = jnp.einsum("td,te->de", mixed_low, proj_low, preferred_element_type=F32)
-    mixed_grad = jnp.einsum(
-        "te,de->td", proj_low, out_full, preferred_element_type=F32
-    ).reshape(tokens_dev, heads_count, head_size)
-    head_grad = jnp.sum(mixed_grad * attended, axis=(0, 2))
-    attended_low = (mixed_grad * heads_low[None, :, None]).astype(BF16)
-    probs = jnp.exp(masked_scores() - log_totals)
-    probs_grad = jnp.einsum("qhd,khd->hqk", attended_low, values_all, preferred_element_type=F32)
-    delta = jnp.transpose(jnp.sum(attended_low.astype(F32) * attended, axis=-1))[:, :, None]
-    scores_low = (probs * (probs_grad - delta)).astype(BF16)
-    query_grad = (
-        (
-            jnp.einsum("hqk,khd->qhd", scores_low, keys_all, preferred_element_type=F32)
-            * score_scale
-        )
-        .astype(BF16)
-        .reshape(tokens_dev, width)
-    )
-    key_grad = (
-        jnp.einsum("hqk,qhd->khd", scores_low, queries_split, preferred_element_type=F32)
-        * score_scale
-    )
-    value_grad = jnp.einsum(
-        "hqk,qhd->khd", probs.astype(BF16), attended_low, preferred_element_type=F32
-    )
-    pair_low = jnp.concatenate(
-        [key_grad.reshape(-1, width), value_grad.reshape(-1, width)], axis=1
-    ).astype(BF16)
+    mixed_grad = jnp.einsum("te,de->td", proj_low, out_full, preferred_element_type=F32)
+    head_grad = jnp.sum((mixed_grad * attended).reshape(tokens_dev, heads_count, -1), axis=(0, 2))
+    attended_low = (mixed_grad * scales).astype(BF16)
+    delta = (
+        jnp.sum((attended_low.astype(F32) * attended).reshape(tokens_dev, heads_count, -1), axis=-1)
+        .transpose(1, 0)
+        .reshape(heads_count // 2, 2, tokens_dev)
+    )
+    query_grad, key_grad, value_grad = attend_back(
+        queries, keys_all, values_all, attended_low, log_totals, delta, starts, heads_count
+    )
     query_bias_grad = jnp.sum(query_grad.astype(F32), axis=0)
-    value_bias_grad = jnp.sum(pair_low[:, width:].astype(F32), axis=0)
-    qkv_grad = jnp.concatenate(
-        [
-            jnp.einsum("td,te->de", normed_low[own], query_grad, preferred_element_type=F32),
-            jnp.einsum("td,te->de", normed_low, pair_low, preferred_element_type=F32),
-        ],
-        axis=1,
-    )
-    normed_grad = jnp.einsum("te,de->td", pair_low, qkv_full[:, width:], preferred_element_type=F32)
+    value_bias_grad = jnp.sum(value_grad.astype(F32), axis=0)
+    query_part = jnp.einsum("td,te->de", normed_low[own], query_grad, preferred_element_type=F32)
+    key_part = jnp.einsum("td,te->de", normed_low, key_grad, preferred_element_type=F32)
+    value_part = jnp.einsum("td,te->de", normed_low, value_grad, preferred_element_type=F32)
+    normed_grad = jnp.einsum(
+        "te,de->td", key_grad, qkv_full[:, width : 2 * width], preferred_element_type=F32
+    ) + jnp.einsum("te,de->td", value_grad, qkv_full[:, 2 * width :], preferred_element_type=F32)
     halo_grad = normed_grad[: 2 * tokens_dev]
     own_grad = normed_grad[own] + jnp.einsum(
         "te,de->td", query_grad, qkv_full[:, :width], preferred_element_type=F32
@@ -812,25 +948,31 @@
         ]
     )
     counted = (vector_size + hidden_size) // 128
-    fc1_rows, fc2_rows = fc1_weight.shape[0], fc2_weight.shape[0]
-    qkv_rows, out_rows = qkv_weight.shape[0], out_weight.shape[0]
     small_part, qkv_part, out_part, fc1_part, fc2_part, halo_back, norm_tile = reduce_all(
         [
             small_grad,
-            qkv_grad.astype(BF16).reshape(wide, -1, 3 * width),
+            query_part.astype(BF16).reshape(wide, -1, width),
+            key_part.astype(BF16).reshape(wide, -1, width),
+            value_part.astype(BF16).reshape(wide, -1, width),
             out_weight_grad.astype(BF16).reshape(wide, -1, width),
             fc1_grad.astype(BF16),
             fc2_grad.astype(BF16).reshape(wide, -1, width),
         ],
         halo_grad.astype(BF16).reshape(2, tokens_dev, width),
-        (
-            (3, 0, fc1_rows // 2, fc1_rows // 8, fc1_rows // 2),
-            (3, fc1_rows // 2, fc1_rows // 2, fc1_rows // 8, fc1_rows // 2),
-            (4, 0, fc2_rows // 2, fc2_rows // 8, fc2_rows // 2),
-            (4, fc2_rows // 2, fc2_rows // 2, fc2_rows // 8, fc2_rows // 2),
-            (0, 0, small_grad.shape[1], 0, counted),
-            (1, 0, qkv_rows, qkv_rows // 4, qkv_rows),
-            (2, 0, out_rows, out_rows // 4, out_rows),
+        tuple(
+            (6, k * (fc2_rows // 4), fc2_rows // 4, fc2_rows // 16, fc2_rows // 4, 4, 0)
+            for k in range(4)
+        )
+        + tuple(
+            (5, k * (fc1_rows // 4), fc1_rows // 4, plane_share(fc1_rows // 4), fc1_rows // 4, 3, 0)
+            for k in range(4)
+        )
+        + (
+            (4, 0, out_rows, out_rows // 4, out_rows, 2, 0),
+            (0, 0, small_grad.shape[1], 0, counted, 0, 0),
+            (1, 0, qkv_rows, qkv_rows // 4, qkv_rows, 1, 0),
+            (2, 0, qkv_rows, qkv_rows // 4, qkv_rows, 1, width),
+            (3, 0, qkv_rows, qkv_rows // 4, qkv_rows, 1, 2 * width),
         ),
     )
     total_grad = own_grad + halo_back[0].astype(F32) + halo_back[1].astype(F32)

time: 773 us -> 634 us (0.82)
  matrix products: 261 us -> 119 us
  Pallas kernels: 319 us -> 363 us
  other arithmetic: 125 us -> 88.6 us
    dot_general x8 -> x4, matrix products: 149 us -> 18.8 us  [the longest x1 6.84 us: body(): jnp.einsum('td,te->de', normed_low, key_grad, preferred_element_type=F32)]
    pallas_call x0 -> x2, Pallas kernels: none -> 68.8 us  [the longest x1 36.6 us: attend(): pl.pallas_call(functools.partial(attend_kernel, width // heads), grid=(pa...]
    reduce_sum x5 -> x4, other arithmetic: 24.7 us -> 4.01 us  [the longest x1 1.88 us: body(): jnp.sum((attended_low.astype(F32) * attended).reshape(tokens_dev, heads_c...]
    pallas_call x1, Pallas kernels: 132 us -> 120 us  [gather_all(): pl.pallas_call(functools.partial(gather_kernel, thirds), out_shape=out_sh...]
    unnamed x157 -> x179, local copies, waits for them, and re-layouts: 16.2 us -> 28.3 us
    pallas_call x1, Pallas kernels: 187 us -> 175 us  [reduce_all(): pl.pallas_call(functools.partial(reduce_kernel, pieces), out_shape=out_sh...]
where the time goes in v2:
time: 634 us; the launch traced here: 630 us
  Pallas kernels  363 us (57%)
  matrix products  119 us (19%)
  other arithmetic  88.6 us (14%)
  local copies, waits for them, and re-layouts  52.9 us (8%)
    pallas_call x1, Pallas kernels, reduce_all(): pl.pallas_call(functools.partial(reduce_kernel, pieces), out_shape=out_sh...  175 us
    pallas_call x1, Pallas kernels, gather_all(): pl.pallas_call(functools.partial(gather_kernel, thirds), out_shape=out_sh...  120 us
    pallas_call x1, Pallas kernels, attend(): pl.pallas_call(functools.partial(attend_kernel, width // heads), grid=(pa...  36.6 us
    pallas_call x1, Pallas kernels, attend_back(): pl.pallas_call(functools.partial(attend_back_kernel, width // heads), gri...  32.2 us
    dot_general x1, matrix products, body(): jnp.einsum('td,fd->tf', out_grad, fc2_full, preferred_element_type=F32)  29.8 us
    unnamed x179, local copies, waits for them, and re-layouts  28.3 us
    reduce_sum x1, other arithmetic, body(): first_mean = jnp.mean(activated, axis=-1, keepdims=True)  23.1 us

profile of v2, /device:TPU:0, one launch (start us, length us, event | category | flops | bytes accessed | tf_op | source)
XLA Modules:
  0.0 629.7 jit_solution(9252315795760643247)
XLA Ops:
  11.4 119.6 %gather_all.1 = (bf16[16,16,128]{2,1,0:T(8,128)(2,1)S(1)}, bf16[16,64,3072]{2,1,0:T(8,128)(2,1)S(1)}, bf16[16,64,1024]{2,1,0:T(8,128)(2,1)S(1)}, bf16[16,1024,25...) custom-call(bf16[16,128]{1,0:T(8,128)(2,1)S(1)} %bitcast.159, ...), custom_call_target="tpu_custom_call" | custom-call | tf_op jit(solution)/shard_map/gather_all/pallas_call | solution.py:311
  135.0 3.3 copy-done.21
  138.3 3.2 copy-done.20
  146.4 4.0 fusion.16
  150.5 4.0 fusion.49.q_ref
  155.1 6.8 %fusion.23 = f32[1536,2048]{1,0:T(8,128)S(1)} fusion(bf16[1536,1024]{1,0:T(8,128)(2,1)S(1)} %get-tuple-element.129, bf16[1024,3072]{1,0:T(8,128)(2,1)S(1)} %bitcast.150), kind=kOutput, calls=%fused_computation.65 | convolution fusion | flops 6442450944 | bytes 19922944 | tf_op jit(solution)/shard_map/dot_general | solution.py:846
  161.9 4.6 copy-done.32
  167.4 4.4 slice.241.k_ref
  171.9 36.6 %attend.1 = (f32[512,1024]{1,0:T(8,128)S(1)}, bf16[512,1024]{1,0:T(8,128)(2,1)S(1)}, f32[8,2,512]{2,1,0:T(2,128)S(1)}) custom-call(s32[1,512]{1,0:T(1,128)S(1)} %bitcast.157, f32[1,1024]{1,0:T(1,128)S(1)} %reshape_reshape.21.scale_ref, bf16[512,1024]{1,0:T(8,128)(2,1)S(1)} %fusion.49.q_ref, bf16[1536,1024]{1,0:T(8,128)(2,1)S(1)} %slice.241.k_ref, ...), custom_call_target="tpu_custom_call" | custom-call | tf_op jit(solution)/shard_map/attend/pallas_call | solution.py:651
  214.6 10.0 %fusion.32 = (u16[512,256]{0,1:T(8,128)(2,1)S(1)}, u16[512,256]{0,1:T(8,128)(2,1)S(1)}, f32[512,16,256]{0,2,1:T(8,128)}) fusion(f32[16,256]{1,0:T(8,128)S(1)} %bitcast.195, bf16[16,1024,256]{2,1,0:T(8,128)(2,1)S(1)} %bitcast.161, f32[512,1024]{1,0:T(8,128)S(1)} %get-tuple-element.126, f32[1024]{0:T(1024)S(1)} %add.347, f32[1024]{0:T(1024)S(1)} %mul.578, ...), kind=kOutput, calls=%fused_computation.74 | convolution fusion | flops 4326686720 | bytes 19427328 | tf_op jit(solution)/shard_map/td,wdf->twf/dot_general | solution.py:865
  224.7 23.1 %fusion.67 = (f32[512]{0:T(512)S(1)}, f32[512]{0:T(512)S(1)}, f32[512,16,256]{0,2,1:T(8,128)}) fusion(u16[512,256]{0,1:T(8,128)(2,1)S(1)} %get-tuple-element.66, u16[512,256]{0,1:T(8,128)(2,1)S(1)} %get-tuple-element.65, f32[512,16,256]{0,2,1:T(8,128)} %get-tuple-element.138, f32[16,256]{1,0:T(8,128)S(1)} %bitcast.196), kind=kLoop, calls=%fused_computation.206 | loop fusion | flops 153091072 | bytes 17321984 | tf_op jit(solution)/shard_map/reduce_sum | solution.py:871
  247.9 9.4 %fusion.39 = bf16[512,1024]{1,0:T(8,128)(2,1)} fusion(f32[512,1024]{1,0:T(8,128)S(1)} %get-tuple-element.126, bf16[16,256,1024]{2,1,0:T(8,128)(2,1)S(1)} %bitcast.163, f32[512,16,256]{0,2,1:T(8,128)} %get-tuple-element.124, f32[16,256]{1,0:T(8,128)S(1)} %get-tuple-element.142, f32[16,256]{1,0:T(8,128)S(1)} %get-tuple-element.143, ...), kind=kOutput, calls=%fused_computation.94 | convolution fusion | flops 4307025920 | bytes 19963904 | tf_op jit(solution)/shard_map/dot_general | solution.py:877
  257.3 29.8 %fusion.3 = (f32[4096]{0:T(1024)S(1)}, f32[512]{0:T(512)S(1)}, f32[512]{0:T(512)S(1)}, f32[512,4096]{0,1:T(8,128)}, f32[512,4096]{0,1:T(8,128)}, /*index=5*/f32[4096,512]{1,0:T(8,128)}) fusion(f32[4096]{0:T(1024)S(1)} %bitcast.188, f32[512]{0:T(512)S(1)} %get-tuple-element.135, f32[512]{0:T(512)S(1)} %get-tuple-element.134, f32[4096]{0:T(1024)S(1)} %bitcast.186, ...), kind=kOutput, calls=%fused_computation.12 | convolution fusion | flops 4448054272 | bytes 43048960 | tf_op jit(solution)/shard_map/td,fd->tf/dot_general | solution.py:880
  287.1 12.7 %convert_reduce_fusion = (f32[4096]{0:T(1024)S(1)}, bf16[512,4096]{0,1:T(8,128)(2,1)}) fusion(f32[512,4096]{0,1:T(8,128)} %get-tuple-element.123, f32[512,4096]{0,1:T(8,128)} %get-tuple-element.122, f32[512]{0:T(512)S(1)} %get-tuple-element.144, f32[512]{0:T(512)S(1)} %get-tuple-element.145, f32[4096]{0:T(1024)S(1)} %bitcast.189, ...), kind=kLoop, calls=%fused_computation.16 | loop fusion | flops 46133248 | bytes 37804032 | tf_op jit(solution)/shard_map/reduce_sum | solution.py:888
  299.8 4.0 reduce_sum.350
  303.8 9.3 %convolution_convert_fusion = bf16[4096,1024]{1,0:T(8,128)(2,1)} fusion(bf16[512,1024]{1,0:T(8,128)(2,1)S(1)} %copy-done.47, f32[512,4096]{0,1:T(8,128)} %get-tuple-element.122, f32[4096]{0:T(1024)S(1)} %bitcast.194, f32[4096]{0:T(1024)S(1)} %bitcast.190), kind=kOutput, calls=%fused_computation.51 | convolution fusion | flops 4305453056 | bytes 17858560 | tf_op jit(solution)/shard_map/tf,td->fd/dot_general | solution.py:879
  313.2 9.9 %fusion.37 = (f32[1024]{0:T(1024)S(1)}, f32[512]{0:T(512)S(1)}, f32[512]{0:T(512)S(1)}, f32[1024]{0:T(1024)S(1)}, f32[512,1024,1]{1,0,2:T(8,128)}) fusion(f32[512,1024]{1,0:T(8,128)S(1)} %copy-done.28, f32[512]{0:T(512)S(1)} %add_rsqrt_fusion.2, f32[512]{0:T(512)S(1)} %broadcast_multiply_fusion.10, f32[1024]{0:T(1024)S(1)} %mul.578, ...), kind=kOutput, calls=%fused_computation.91 | convolution fusion | flops 4299682816 | bytes 16797696 | tf_op jit(solution)/shard_map/twf,wdf->td/dot_general | solution.py:891
  323.4 4.1 multiply_reduce_fusion.4
  328.4 3.1 convert_multiply_fusion
  331.4 2.9 copy.62
  338.7 32.2 %attend_back.1 = (bf16[512,1024]{1,0:T(8,128)(2,1)S(1)}, bf16[1536,1024]{1,0:T(8,128)(2,1)S(1)}, bf16[1536,1024]{1,0:T(8,128)(2,1)S(1)}) custom-call(s32[1,512]{1,0:T(1,128)S(1)} %bitcast.158, bf16[512,1024]{1,0:T(8,128)(2,1)S(1)} %copy-done.7, bf16[1536,1024]{1,0:T(8,128)(2,1)S(1)} %copy-done.1, bf16[1536,1024]{1,0:T(8,128)(2,1)} %copy-done.2, ...), custom_call_target="tpu_custom_call" | custom-call | tf_op jit(solution)/shard_map/attend_back/pallas_call | solution.py:724
  378.2 4.3 convolution_convert_fusion.1
  382.5 7.2 %convert_bitcast_fusion = bf16[16,1024,256]{1,2,0:T(8,128)(2,1)} fusion(bf16[512,16,256]{0,2,1:T(8,128)(2,1)S(1)} %bitcast.173, f32[512,1024]{1,0:T(8,128)S(1)} %copy-done.29, f32[1024]{0:T(1024)S(1)} %copy-done.68, f32[1024]{0:T(1024)S(1)} %mul.578, f32[512]{0:T(512)S(1)} %add_rsqrt_fusion.2, f32[512]{0:T(512)S(1)} %broadcast_multiply_fusion.10), kind=kOutput, calls=%fused_computation.15 | convolution fusion | flops 4301783040 | bytes 14692352 | tf_op jit(solution)/shard_map/td,twf->wdf/dot_general | solution.py:890
  389.7 12.4 %copy.63 = bf16[16,1024,256]{2,1,0:T(8,128)(2,1)} copy(bf16[16,1024,256]{1,2,0:T(8,128)(2,1)} %convert_bitcast_fusion) | data formatting | bytes 16777216 | tf_op jit(solution)/shard_map/convert_element_type | solution.py:958
  402.2 6.8 %convolution_convert_fusion.3 = bf16[1024,1024]{1,0:T(8,128)(2,1)} fusion(bf16[1536,1024]{1,0:T(8,128)(2,1)} %copy-done.38, bf16[1536,1024]{1,0:T(8,128)(2,1)S(1)} %copy-done.23), kind=kOutput, calls=%fused_computation.116 | convolution fusion | flops 3222274048 | bytes 8388608 | tf_op jit(solution)/shard_map/td,te->de/dot_general | solution.py:916
  409.0 4.9 convolution_convert_fusion.2
  416.6 3.5 fusion.34
  420.2 3.5 convolution_add_fusion
  430.3 175.0 %reduce_all.1 = (f32[16,128]{1,0:T(8,128)}, f32[64,3072]{1,0:T(8,128)}, f32[64,1024]{1,0:T(8,128)}, f32[1024,256]{1,0:T(8,128)}, f32[256,1024]{1,0:T(8,128)}, /*...) custom-call(f32[4,2,2,16,128]{4,3,2,1,0:T(8,128)} %bitcast.178, bf16[4,2,2,64,1024]{4,3,2,1,0:T(8,128)(2,1)} %bitcast.177, ...), custom_call_target="tpu_custom_call" | custom-call | tf_op jit(solution)/shard_map/reduce_all/pallas_call | solution.py:553
  606.8 3.5 fusion.68
  610.5 3.5 multiply_add_fusion
  620.1 3.8 multiply_subtract_fusion.2
  (279 shorter events, 58.6 us)
Async XLA Ops:
  0.7 140.8 %copy-start.4 = (bf16[512,1024]{1,0:T(8,128)(2,1)S(1)}, bf16[512,1024]{1,0:T(8,128)(2,1)}, u32[]{:S(2)}) copy-start(bf16[512,1024]{1,0:T(8,128)(2,1)} %refs_5_.1) | copy-start | bytes 3145732
  3.1 168.8 %copy-start.18 = (s32[512]{0:T(512)}, s32[512]{0:T(512)S(1)}, u32[]{:S(2)}) copy-start(s32[512]{0:T(512)S(1)} %subtract_maximum_fusion) | copy-start | bytes 6148
  145.9 64.5 %copy-start.48 = (f32[1024]{0:T(1024)}, f32[1024]{0:T(1024)S(1)}, u32[]{:S(2)}) copy-start(f32[1024]{0:T(1024)S(1)} %add.338) | copy-start | bytes 12292
  146.0 64.4 %copy-start.52 = (f32[1024]{0:T(1024)}, f32[1024]{0:T(1024)S(1)}, u32[]{:S(2)}) copy-start(f32[1024]{0:T(1024)S(1)} %mul.572) | copy-start | bytes 12292
  146.1 65.5 %copy-start.67 = (f32[1024]{0:T(1024)}, f32[1024]{0:T(1024)S(1)}, u32[]{:S(2)}) copy-start(f32[1024]{0:T(1024)S(1)} %add.347) | copy-start | bytes 12292
  150.5 11.4 %copy-start.38 = (bf16[1536,1024]{1,0:T(8,128)(2,1)}, bf16[1536,1024]{1,0:T(8,128)(2,1)S(1)}, u32[]{:S(2)}) copy-start(bf16[1536,1024]{1,0:T(8,128)(2,1)S(1)} %get-tuple-element.129) | copy-start | bytes 9437188
  155.1 16.8 %copy-start.6 = (bf16[512,1024]{1,0:T(8,128)(2,1)}, bf16[512,1024]{1,0:T(8,128)(2,1)S(1)}, u32[]{:S(2)}) copy-start(bf16[512,1024]{1,0:T(8,128)(2,1)S(1)} %fusion.49.q_ref) | copy-start | bytes 3145732
  167.4 41.1 %copy-start.2 = (bf16[1536,1024]{1,0:T(8,128)(2,1)}, bf16[1536,1024]{1,0:T(8,128)(2,1)S(1)}, u32[]{:S(2)}) copy-start(bf16[1536,1024]{1,0:T(8,128)(2,1)S(1)} %fusion.20.v_ref) | copy-start | bytes 9437188
  167.4 41.1 %copy-start.13 = (bf16[16,64,1024]{2,1,0:T(8,128)(2,1)S(1)}, bf16[16,64,1024]{2,1,0:T(8,128)(2,1)}, u32[]{:S(2)}) copy-start(bf16[16,64,1024]{2,1,0:T(8,128)(2,1)} %copy-done.12) | copy-start | bytes 6291460
  171.9 38.0 %copy-start = (bf16[1536,1024]{1,0:T(8,128)(2,1)}, bf16[1536,1024]{1,0:T(8,128)(2,1)S(1)}, u32[]{:S(2)}) copy-start(bf16[1536,1024]{1,0:T(8,128)(2,1)S(1)} %slice.241.k_ref) | copy-start | bytes 9437188
  209.9 14.7 %copy-start.25 = (f32[512,1024]{1,0:T(8,128)}, f32[512,1024]{1,0:T(8,128)S(1)}, u32[]{:S(2)}) copy-start(f32[512,1024]{1,0:T(8,128)S(1)} %get-tuple-element.137) | copy-start | bytes 6291460
  209.9 14.7 %copy-start.54 = (f32[512]{0:T(512)}, f32[512]{0:T(512)S(1)}, u32[]{:S(2)}) copy-start(f32[512]{0:T(512)S(1)} %broadcast_multiply_fusion.11) | copy-start | bytes 6148
  210.4 14.2 %copy-start.60 = (f32[512]{0:T(512)}, f32[512]{0:T(512)S(1)}, u32[]{:S(2)}) copy-start(f32[512]{0:T(512)S(1)} %add_rsqrt_fusion.3) | copy-start | bytes 6148
  211.2 36.6 %copy-start.27 = (f32[512,1024]{1,0:T(8,128)}, f32[512,1024]{1,0:T(8,128)S(1)}, u32[]{:S(2)}) copy-start(f32[512,1024]{1,0:T(8,128)S(1)} %get-tuple-element.126) | copy-start | bytes 6291460
  211.2 36.6 %slice-start.6 = ((s8[8388608]{0:T(1024)(128)(4,1)}), s8[4194304]{0:T(1024)(128)(4,1)S(1)}, s32[]{:S(2)}) async-start(s8[8388608]{0:T(1024)(128)(4,1)} %bitcast.162), calls=%async_computation.6 | async-start | bytes 8388608
  214.6 33.2 %slice-start.7 = ((s8[8388608]{0:T(1024)(128)(4,1)}), s8[4194304]{0:T(1024)(128)(4,1)S(1)}, s32[]{:S(2)}) async-start(s8[8388608]{0:T(1024)(128)(4,1)} %bitcast.162), calls=%async_computation.7 | async-start | bytes 8388608
  224.6 32.6 %slice-start.10 = ((s8[8388608]{0:T(1024)(128)(4,1)}), s8[4194304]{0:T(1024)(128)(4,1)S(1)}, s32[]{:S(2)}) async-start(s8[8388608]{0:T(1024)(128)(4,1)} %bitcast.168), calls=%async_computation.10 | async-start | bytes 8388608
  247.8 9.5 %slice-start.11 = ((s8[8388608]{0:T(1024)(128)(4,1)}), s8[4194304]{0:T(1024)(128)(4,1)S(1)}, s32[]{:S(2)}) async-start(s8[8388608]{0:T(1024)(128)(4,1)} %bitcast.168), calls=%async_computation.11 | async-start | bytes 8388608
  247.8 9.5 %copy-start.47 = (bf16[512,1024]{1,0:T(8,128)(2,1)S(1)}, bf16[512,1024]{1,0:T(8,128)(2,1)}, u32[]{:S(2)}) copy-start(bf16[512,1024]{1,0:T(8,128)(2,1)} %param.26) | copy-start | bytes 3145732
  303.8 9.4 %copy-start.28 = (f32[512,1024]{1,0:T(8,128)S(1)}, f32[512,1024]{1,0:T(8,128)}, u32[]{:S(2)}) copy-start(f32[512,1024]{1,0:T(8,128)} %copy-done.27) | copy-start | bytes 6291460
  303.8 9.4 %copy-start.36 = (bf16[512,4096]{0,1:T(8,128)(2,1)S(1)}, bf16[512,4096]{0,1:T(8,128)(2,1)}, u32[]{:S(2)}) copy-start(bf16[512,4096]{0,1:T(8,128)(2,1)} %get-tuple-element.118) | copy-start | bytes 12582916
  313.2 10.2 %copy-start.26 = (f32[512,1024]{1,0:T(8,128)S(1)}, f32[512,1024]{1,0:T(8,128)}, u32[]{:S(2)}) copy-start(f32[512,1024]{1,0:T(8,128)} %copy-done.25) | copy-start | bytes 6291460
  313.2 10.2 %copy-start.49 = (f32[1024]{0:T(1024)S(1)}, f32[1024]{0:T(1024)}, u32[]{:S(2)}) copy-start(f32[1024]{0:T(1024)} %copy-done.48) | copy-start | bytes 12292
  313.2 10.2 %copy-start.53 = (f32[1024]{0:T(1024)S(1)}, f32[1024]{0:T(1024)}, u32[]{:S(2)}) copy-start(f32[1024]{0:T(1024)} %copy-done.52) | copy-start | bytes 12292
  313.2 10.2 %copy-start.55 = (f32[512]{0:T(512)S(1)}, f32[512]{0:T(512)}, u32[]{:S(2)}) copy-start(f32[512]{0:T(512)} %copy-done.54) | copy-start | bytes 6148
  313.2 10.2 %copy-start.61 = (f32[512]{0:T(512)S(1)}, f32[512]{0:T(512)}, u32[]{:S(2)}) copy-start(f32[512]{0:T(512)} %copy-done.60) | copy-start | bytes 6148
  389.7 12.4 %copy-start.23 = (bf16[1536,1024]{1,0:T(8,128)(2,1)S(1)}, bf16[1536,1024]{1,0:T(8,128)(2,1)}, u32[]{:S(2)}) copy-start(bf16[1536,1024]{1,0:T(8,128)(2,1)} %copy-done.22) | copy-start | bytes 9437188
  402.2 14.5 %slice-start.2 = ((s8[6291456]{0:T(1024)(128)(4,1)}), s8[4194304]{0:T(1024)(128)(4,1)S(1)}, s32[]{:S(2)}) async-start(s8[6291456]{0:T(1024)(128)(4,1)} %bitcast.151), calls=%async_computation.2 | async-start | bytes 8388608
  430.3 176.5 %copy-start.58 = (f32[1024]{0:T(1024)S(1)}, f32[1024]{0:T(1024)}, u32[]{:S(2)}) copy-start(f32[1024]{0:T(1024)} %copy-done.57) | copy-start | bytes 12292
  610.5 13.3 %copy-start.34 = (f32[1024,256]{1,0:T(8,128)S(1)}, f32[1024,256]{1,0:T(8,128)}, u32[]{:S(2)}) copy-start(f32[1024,256]{1,0:T(8,128)} %param.35) | copy-start | bytes 3145732
  614.0 9.9 %copy-start.40 = (f32[1024,256]{1,0:T(8,128)S(1)}, f32[1024,256]{1,0:T(8,128)}, u32[]{:S(2)}) copy-start(f32[1024,256]{1,0:T(8,128)} %param.37) | copy-start | bytes 3145732
  614.0 9.9 %copy-start.41 = (f32[1024,256]{1,0:T(8,128)S(1)}, f32[1024,256]{1,0:T(8,128)}, u32[]{:S(2)}) copy-start(f32[1024,256]{1,0:T(8,128)} %param.36) | copy-start | bytes 3145732
  (55 other events, 261.8 us)

commit v3 on v1

v3 whole, which is shorter than its diff:
```python
import functools

import jax
import jax.numpy as jnp
from jax import lax
from jax.experimental import pallas as pl
from jax.experimental.pallas import tpu as pltpu
from jax.sharding import PartitionSpec as P

DOC_MOST = 1024
MESH = pl.DeviceIdType.MESH
HBM = pl.BlockSpec(memory_space=pltpu.HBM)
VMEM = pl.BlockSpec(memory_space=pltpu.VMEM)
BF16 = jnp.bfloat16
F32 = jnp.float32

norm_epsilon = 1e-05
clip_limit = 1.0
first_decay = 0.9
second_decay = 0.98
adam_epsilon = 1e-08
matrix_rate = 0.1
vector_rate = 0.4
weight_decay = 0.1
masked_score = -1e30


def layer_norm(values_in, gain, shift):
    center = values_in - jnp.mean(values_in, axis=-1, keepdims=True)
    variance = jnp.mean(center * center, axis=-1, keepdims=True)
    scale = lax.rsqrt(variance + norm_epsilon)
    normed = center * scale
    return (normed * gain + shift, normed, scale)


def norm_back(grad, normed, scale, gain):
    scaled = grad * gain
    mean_plain = jnp.mean(scaled, axis=-1, keepdims=True)
    mean_cross = jnp.mean(scaled * normed, axis=-1, keepdims=True)
    return scale * (scaled - mean_plain - normed * mean_cross)


def doc_starts(doc_lengths, row, first, count):
    ends = lax.dynamic_slice_in_dim(jnp.cumsum(doc_lengths, axis=1), row, 1, 0)[0]
    places = first + jnp.arange(count, dtype=jnp.int32)
    return jnp.max(jnp.where(ends[None, :] <= places[:, None], ends[None, :], 0), axis=1)


def adam_step(grad, weight, first, second, step, rate, decay):
    first_new = first_decay * first + (1.0 - first_decay) * grad
    second_new = second_decay * second + (1.0 - second_decay) * grad * grad
    fix_one = 1.0 - jnp.power(jnp.float32(first_decay), step)
    fix_two = 1.0 - jnp.power(jnp.float32(second_decay), step)
    direction = first_new / fix_one / (jnp.sqrt(second_new / fix_two) + adam_epsilon)
    weight_new = weight - rate * (direction + decay * weight)
    return (first_new, second_new, weight_new)


def from_behind(shard, axis, by):
    count = lax.axis_size(axis)
    pairs = [(i, i + by) for i in range(count) if 0 <= i + by < count]
    return lax.ppermute(shard, axis, pairs)


def dot(a, b, left=1, right=0):
    return lax.dot_general(
        a, b, (((left,), (right,)), ((), ())), preferred_element_type=F32
    )


Q_TILE = 256


def split_pair(pair, size):
    lane = lax.broadcasted_iota(jnp.int32, pair.shape, 1)
    zero = jnp.zeros_like(pair)
    return jnp.where(lane < size, pair, zero), jnp.where(lane < size, zero, pair)


def fill_mask(starts, bias, tokens, span, keys_before):
    for tile in range(tokens // Q_TILE):
        query = lax.broadcasted_iota(jnp.int32, (span, Q_TILE), 1) + tile * Q_TILE + keys_before
        key = lax.broadcasted_iota(jnp.int32, (span, Q_TILE), 0) + tile * Q_TILE
        first = starts[:, tile * Q_TILE : (tile + 1) * Q_TILE]
        seen = jnp.logical_and(key <= query, key >= first)
        bias[tile] = jnp.where(seen, 0.0, masked_score)


def attend_pair(size, q_ref, k_ref, v_ref, scale_ref, o_ref, c_ref, lse_ref, bias, vt, ot):
    tokens, window = q_ref.shape[0], k_ref.shape[0]
    span = window - tokens + Q_TILE
    vt[...] = v_ref[...].T
    for tile in range(tokens // Q_TILE):
        rows = slice(tile * Q_TILE, (tile + 1) * Q_TILE)
        keys = slice(tile * Q_TILE, tile * Q_TILE + span)
        k_pair = k_ref[keys, :]
        for head, q_one in enumerate(split_pair(q_ref[rows, :], size)):
            scores = dot(k_pair, q_one, 1, 1) + bias[tile]
            highest = jnp.max(scores, axis=0, keepdims=True)
            powers = jnp.exp(scores - highest)
            total = jnp.sum(powers, axis=0, keepdims=True)
            probs = (powers * (1.0 / total)).astype(BF16)
            lse_ref[head : head + 1, rows] = highest + jnp.log(total)
            part = slice(head * size, (head + 1) * size)
            ot[part, rows] = dot(vt[part, keys], probs)
    attended = ot[...].T
    o_ref[...] = attended
    c_ref[...] = (attended * scale_ref[...]).astype(BF16)


def attend_kernel(size, starts, scale_ref, q_ref, k_ref, v_ref, o_ref, c_ref, lse_ref, bias, vt, ot):
    tokens, window = q_ref.shape[0], k_ref.shape[0]
    before = window - tokens

    @pl.when(pl.program_id(0) == 0)
    def _():
        fill_mask(starts, bias, tokens, before + Q_TILE, before)

    attend_pair(size, q_ref, k_ref, v_ref, scale_ref, o_ref, c_ref, lse_ref.at[0], bias, vt, ot)


def attend(queries, keys, values, starts, scales, heads):
    tokens, width = queries.shape
    window = keys.shape[0]
    pairs = heads // 2
    lanes = width // pairs
    span = window - tokens + Q_TILE
    by_rows = lambda rows: pl.BlockSpec((rows, lanes), lambda p: (0, p))
    return pl.pallas_call(
        functools.partial(attend_kernel, width // heads),
        grid=(pairs,),
        in_specs=[
            pl.BlockSpec((1, tokens), lambda p: (0, 0)),
            by_rows(1),
            by_rows(tokens),
            by_rows(window),
            by_rows(window),
        ],
        out_specs=[
            by_rows(tokens),
            by_rows(tokens),
            pl.BlockSpec((1, 2, tokens), lambda p: (p, 0, 0)),
        ],
        out_shape=[
            jax.ShapeDtypeStruct((tokens, width), F32),
            jax.ShapeDtypeStruct((tokens, width), BF16),
            jax.ShapeDtypeStruct((pairs, 2, tokens), F32),
        ],
        scratch_shapes=[
            pltpu.VMEM((tokens // Q_TILE, span, Q_TILE), F32),
            pltpu.VMEM((lanes, window), BF16),
            pltpu.VMEM((lanes, tokens), F32),
        ],
        compiler_params=pltpu.CompilerParams(vmem_limit_bytes=40 << 20),
        name="attend",
    )(starts, scales, queries, keys, values)


def attend_back_kernel(
    size, starts, q_ref, k_ref, v_ref, do_ref, lse_ref, delta_ref,
    dq_ref, dk_ref, dv_ref, bias, dk_sum, dv_sum, kt, dqt,
):
    tokens, window = q_ref.shape[0], k_ref.shape[0]
    before = window - tokens
    span = before + Q_TILE

    @pl.when(pl.program_id(0) == 0)
    def _():
        fill_mask(starts, bias, tokens, span, before)

    kt[...] = k_ref[...].T
    dk_sum[...] = jnp.zeros_like(dk_sum)
    dv_sum[...] = jnp.zeros_like(dv_sum)
    for tile in range(tokens // Q_TILE):
        rows = slice(tile * Q_TILE, (tile + 1) * Q_TILE)
        keys = slice(tile * Q_TILE, tile * Q_TILE + span)
        k_pair, v_pair = k_ref[keys, :], v_ref[keys, :]
        for head, (q_one, do_one) in enumerate(
            zip(split_pair(q_ref[rows, :], size), split_pair(do_ref[rows, :], size))
        ):
            scores = dot(k_pair, q_one, 1, 1) + bias[tile]
            probs = jnp.exp(scores - lse_ref[0, head : head + 1, rows])
            grads = dot(v_pair, do_one, 1, 1) - delta_ref[0, head : head + 1, rows]
            low = (probs * grads).astype(BF16)
            dv_sum[keys, :] += dot(probs.astype(BF16), do_one)
            dk_sum[keys, :] += dot(low, q_one)
            part = slice(head * size, (head + 1) * size)
            dqt[part, rows] = dot(kt[part, keys], low)
    dq_ref[...] = (dqt[...].T * size ** (-0.5)).astype(BF16)
    dk_ref[...] = dk_sum[...].astype(BF16)
    dv_ref[...] = dv_sum[...].astype(BF16)


def attend_back(queries, keys, values, outs_grad, lse, delta, starts, heads):
    tokens, width = queries.shape
    window = keys.shape[0]
    pairs = heads // 2
    lanes = width // pairs
    span = window - tokens + Q_TILE
    by_rows = lambda rows: pl.BlockSpec((rows, lanes), lambda p: (0, p))
    stats = pl.BlockSpec((1, 2, tokens), lambda p: (p, 0, 0))
    return pl.pallas_call(
        functools.partial(attend_back_kernel, width // heads),
        grid=(pairs,),
        in_specs=[
            pl.BlockSpec((1, tokens), lambda p: (0, 0)),
            by_rows(tokens),
            by_rows(window),
            by_rows(window),
            by_rows(tokens),
            stats,
            stats,
        ],
        out_specs=[
            by_rows(tokens),
            by_rows(window),
            by_rows(window),
        ],
        out_shape=[
            jax.ShapeDtypeStruct((tokens, width), BF16),
            jax.ShapeDtypeStruct((window, width), BF16),
            jax.ShapeDtypeStruct((window, width), BF16),
        ],
        scratch_shapes=[
            pltpu.VMEM((tokens // Q_TILE, span, Q_TILE), F32),
            pltpu.VMEM((window, lanes), F32),
            pltpu.VMEM((window, lanes), F32),
            pltpu.VMEM((lanes, window), BF16),
            pltpu.VMEM((lanes, tokens), F32),
        ],
        compiler_params=pltpu.CompilerParams(vmem_limit_bytes=40 << 20),
        name="attend_back",
    )(starts, queries, keys, values, outs_grad, lse, delta)


class Place:
    def __init__(self):
        self.y = lax.axis_index("dp")
        self.w = lax.axis_index("wide")
        self.z = self.w // 4
        self.x = (self.w // 2) % 2
        self.c = self.w % 2

    def slab(self, z, x, c):
        return z * 4 + x * 2 + c

    def wide(self, w):
        return (self.y, w)

    def core_mate(self):
        return self.wide(self.slab(self.z, self.x, 1 - self.c))

    def x_mate(self):
        return self.wide(self.slab(self.z, 1 - self.x, self.c))

    def y_mate(self):
        return (1 - self.y, self.w)

    def up(self):
        return self.wide(lax.rem(self.w + 4, 16))

    def down(self):
        return self.wide(lax.rem(self.w + 12, 16))


def greet(me, extra=()):
    barrier = pltpu.get_barrier_semaphore()

    def hello(target):
        pl.semaphore_signal(barrier, inc=1, device_id=target, device_id_type=MESH)

    always = [me.core_mate(), me.x_mate(), me.y_mate(), *extra]
    sometimes = [
        (me.z < 3, me.up()),
        (me.z > 0, me.down()),
        (me.w < 14, me.wide(lax.rem(me.w + 2, 16))),
        (me.w >= 2, me.wide(lax.rem(me.w + 14, 16))),
    ]
    for target in always:
        hello(target)
    for holds, target in sometimes:
        pl.when(holds)(functools.partial(hello, target))
    count = len(always) + sum(holds.astype(jnp.int32) for holds, _ in sometimes)
    pl.semaphore_wait(barrier, count)


class Wire:
    def __init__(self, send, recv):
        self.send, self.recv = send, recv
        self.planned = []

    def copy(self, source, target, index, device):
        return pltpu.make_async_remote_copy(
            src_ref=source,
            dst_ref=target,
            send_sem=self.send.at[index],
            recv_sem=self.recv.at[index],
            device_id=device,
            device_id_type=MESH,
        )

    def put(self, source, target, index, device, holds=None):
        moved = self.copy(source, target, index, device)
        self.planned.append((holds, moved))
        return lambda: when(holds, moved.start)

    def got(self, target, index, device, holds=None):
        moved = self.copy(target, target, index, device)
        return lambda: when(holds, moved.wait_recv)

    def finish(self):
        for holds, moved in self.planned:
            when(holds, moved.wait_send)


def act(actions):
    for one in actions:
        one()


def both(*conditions):
    held = [one for one in conditions if one is not None]
    total = held[0] if held else None
    for one in held[1:]:
        total = jnp.logical_and(total, one)
    return total


def when(holds, action):
    if holds is None:
        action()
    else:
        pl.when(holds)(action)


def gather_ticks(me, wire, base, own, full, third):
    rows = own.shape[0]
    plane = (
        pl.ds(pl.multiple_of(me.y * third, 16), rows - third) if third else pl.ds(0, rows)
    )
    share = pl.ds(pl.multiple_of(me.y * (rows - third), 16), third) if third else None
    other = pl.ds(pl.multiple_of((1 - me.y) * (rows - third), 16), third) if third else None
    my_slab = me.slab(me.z, me.x, me.c)
    ups, downs, xs, ys, cs, ts = (base + k for k in (0, 4, 8, 12, 20, 28))
    mine = me.z * 2 + me.x

    def pass_on(z, x, holds):
        slab = me.slab(z, x, me.c)
        place = z * 2 + x
        block = full.at[slab, plane]
        actions = []
        if third:
            piece = full.at[slab, share]
            actions.append(wire.put(piece, piece, ys + place, me.y_mate(), holds))
        actions.append(wire.put(block, block, cs + place, me.core_mate(), holds))
        return actions

    goal = full.at[my_slab, plane]
    ticks = [
        [
            wire.put(own.at[plane], goal, ups + me.z, me.up(), me.z < 3),
            wire.put(own.at[plane], goal, downs + me.z, me.down(), me.z > 0),
            wire.put(own.at[plane], goal, xs + me.z, me.x_mate()),
            wire.put(own, full.at[my_slab], cs + mine, me.core_mate()),
        ]
    ]
    for tick in range(1, 5):
        actions = []
        if tick < 4:
            for away, holds, onward, follow, sems in (
                (me.z - tick, me.z - tick >= 0, me.up(), me.z < 3, ups),
                (me.z + tick, me.z + tick <= 3, me.down(), me.z > 0, downs),
            ):
                safe = lax.rem(away + 4, 4)
                block = full.at[me.slab(safe, me.x, me.c), plane]
                actions.append(wire.got(block, sems + safe, onward, holds))
                actions.append(wire.put(block, block, sems + safe, onward, both(holds, follow)))
                actions.append(wire.put(block, block, xs + safe, me.x_mate(), holds))
                actions += pass_on(safe, me.x, holds)
        before = tick - 1
        for away, holds in (
            ((me.z, None),)
            if before == 0
            else (
                (me.z - before, me.z - before >= 0),
                (me.z + before, me.z + before <= 3),
            )
        ):
            safe = lax.rem(away + 4, 4)
            block = full.at[me.slab(safe, 1 - me.x, me.c), plane]
            actions.append(wire.got(block, xs + safe, me.x_mate(), holds))
            actions += pass_on(safe, 1 - me.x, holds)
        ticks.append(actions)
    actions = []
    if third:
        for k in range(1, 8):
            place = lax.rem(mine + k, 8)
            piece = full.at[me.slab(place // 2, place % 2, me.c), other]
            actions.append(wire.got(piece, ys + place, me.y_mate()))
            actions.append(wire.put(piece, piece, ts + place, me.core_mate()))
    ticks.append(actions)
    actions = [wire.got(full.at[me.slab(me.z, me.x, 1 - me.c)], cs + mine, me.core_mate())]
    for k in range(1, 8):
        place = lax.rem(mine + k, 8)
        slab = me.slab(place // 2, place % 2, 1 - me.c)
        actions.append(wire.got(full.at[slab, plane], cs + place, me.core_mate()))
        if third:
            actions.append(wire.got(full.at[slab, other], ts + place, me.core_mate()))
    ticks.append(actions)
    return ticks


AG_SEMS = 36


FRONT_BLOCK = 256


def front_kernel(thirds, head_size, *refs):
    owns, (tokens, starts, scale_ref) = refs[:5], refs[5:8]
    fulls, outs = refs[8:13], refs[13:20]
    xs_out, a_out, q_out, k_out, v_out, o_out, c_out = outs
    lse_ref = refs[20]
    (xs, a_all, qkv, q_all, k_all, v_all, o_all, c_all, vecs, small, bias, vt, ot, send, recv, local) = refs[21:]
    me = Place()
    count = len(owns)
    width = tokens.shape[1]
    rows = tokens.shape[0]
    window = 3 * rows
    before = window - rows
    span = before + Q_TILE
    landings = (small, qkv, *fulls[2:])
    keep = [
        pltpu.make_async_copy(own, full.at[me.w], local.at[k])
        for k, (own, full) in enumerate(zip(owns, landings))
    ] + [pltpu.make_async_copy(tokens, xs.at[2], local.at[count])]
    for one in keep:
        one.start()

    def clear(slot):
        xs[slot] = jnp.zeros((rows, width), BF16)

    pl.when(me.w < 2)(functools.partial(clear, 0))
    pl.when(me.w < 1)(functools.partial(clear, 1))
    wire = Wire(send, recv)
    first, second = AG_SEMS * count, AG_SEMS * count + 1
    ticks = [
        gather_ticks(me, wire, AG_SEMS * k, own, landing, third)
        for k, (own, landing, third) in enumerate(zip(owns, landings, thirds))
    ]
    send_block = wire.put(tokens, xs.at[0], first, me.wide(lax.rem(me.w + 2, 16)), me.w < 14)
    send_near = wire.put(tokens, xs.at[1], second, me.core_mate(), me.c == 0)
    get_block = wire.got(xs.at[0], first, me.core_mate(), me.w >= 2)
    pass_block = wire.put(xs.at[0], xs.at[1], second, me.core_mate(), both(me.c == 1, me.w >= 2))
    get_near = wire.got(xs.at[1], second, me.core_mate(), me.w >= 1)
    greet(me)
    early, late = ticks[:2], ticks[2:]
    act(early[0][0] + early[1][0])
    send_block()
    send_near()
    for tick in range(1, 4):
        act(early[0][tick] + early[1][tick])
    for one in late:
        act(one[0])
    get_block()
    pass_block()
    fill_mask(starts, bias, rows, span, before)
    for tick in range(4, 7):
        act(early[0][tick] + early[1][tick])
    get_near()
    for one in keep:
        one.wait()
    shared = [
        pltpu.make_async_copy(small, fulls[0], local.at[0]),
        pltpu.make_async_copy(qkv, fulls[1], local.at[1]),
        pltpu.make_async_copy(xs, xs_out, local.at[2]),
    ]
    for one in shared:
        one.start()

    lane = lax.broadcasted_iota(jnp.int32, (16, 128), 1)
    for pair in range(8):
        even = small[2 * pair].astype(F32)
        odd = pltpu.roll(small[2 * pair + 1].astype(F32), 64, 1)
        vecs[:, pair * 128 : (pair + 1) * 128] = jnp.where(lane < 64, even, odd)

    def project(first_column, column, a_rows):
        weights = qkv[:, :, pl.ds(first_column + column, FRONT_BLOCK)].reshape(width, FRONT_BLOCK)
        return dot(a_rows, weights)

    per = rows // FRONT_BLOCK

    def normalize(number, carry):
        here = pl.ds(pl.multiple_of(lax.rem(number, per) * FRONT_BLOCK, FRONT_BLOCK), FRONT_BLOCK)
        there = pl.ds(pl.multiple_of(number * FRONT_BLOCK, FRONT_BLOCK), FRONT_BLOCK)
        value, _, _ = layer_norm(xs[number // per, here].astype(F32), vecs[0:1], vecs[3:4])
        low = value.astype(BF16)
        a_all[there] = low
        for column in range(0, width, FRONT_BLOCK):
            columns = slice(column, column + FRONT_BLOCK)
            k_all[there, columns] = project(width, column, low).astype(BF16)
            v_all[there, columns] = (
                project(2 * width, column, low) + vecs[5:6, columns]
            ).astype(BF16)
        return carry

    lax.fori_loop(0, window // FRONT_BLOCK, normalize, 0)
    for number in range(per):
        here = pl.ds(number * FRONT_BLOCK, FRONT_BLOCK)
        low = a_all[before + number * FRONT_BLOCK : before + (number + 1) * FRONT_BLOCK]
        for column in range(0, width, FRONT_BLOCK):
            columns = slice(column, column + FRONT_BLOCK)
            query = (project(0, column, low) + vecs[4:5, columns]).astype(BF16)
            q_all[here, columns] = query * jnp.asarray(head_size ** (-0.5), BF16)
    kept = [
        pltpu.make_async_copy(one, out, local.at[3 + k])
        for k, (one, out) in enumerate(
            ((a_all, a_out), (q_all, q_out), (k_all, k_out), (v_all, v_out))
        )
    ]
    for one in kept:
        one.start()

    def pair_step(pair, carry):
        lanes = pl.ds(pl.multiple_of(pair * 128, 128), 128)
        attend_pair(
            head_size, q_all.at[:, lanes], k_all.at[:, lanes], v_all.at[:, lanes],
            scale_ref.at[:, lanes], o_all.at[:, lanes], c_all.at[:, lanes], lse_ref.at[pair], bias, vt, ot,
        )
        for tick, when_done in ((1, 0), (2, 4)):
            pl.when(pair == when_done)(
                lambda tick=tick: act([action for one in late for action in one[tick]])
            )
        return carry

    lax.fori_loop(0, width // 128, pair_step, 0)
    results = [
        pltpu.make_async_copy(o_all, o_out, local.at[7]),
        pltpu.make_async_copy(c_all, c_out, local.at[8]),
    ]
    for one in results:
        one.start()
    for tick in range(3, 7):
        for one in late:
            act(one[tick])
    wire.finish()
    for one in shared + kept + results:
        one.wait()


def plain_front(shards, tokens, starts, scales, heads):
    width = tokens.shape[1]
    fulls = [lax.all_gather(one, "wide", axis=0, tiled=False) for one in shards]
    each = width // fulls[0].shape[0]
    vectors = fulls[0][:, :10, :each].transpose(1, 0, 2).reshape(10, width).astype(F32)
    window = jnp.stack([from_behind(tokens, "wide", 2), from_behind(tokens, "wide", 1), tokens])
    normed, _, _ = layer_norm(window.reshape(-1, width).astype(F32), vectors[0], vectors[3])
    low = normed.astype(BF16)
    weights = fulls[1].reshape(width, 3 * width)
    queries = dot(low[-tokens.shape[0] :], weights[:, :width]) + vectors[4]
    queries = queries.astype(BF16) * jnp.asarray((width // heads) ** (-0.5), BF16)
    keys = dot(low, weights[:, width : 2 * width]).astype(BF16)
    values = (dot(low, weights[:, 2 * width :]) + vectors[5]).astype(BF16)
    attended = attend(queries, keys, values, starts, scales, heads)
    return [*fulls, window, low, queries, keys, values, *attended]


def front(shards, thirds, tokens, starts, scales, heads):
    rows, width = tokens.shape
    wide = lax.axis_size("wide")
    if lax.axis_size("dp") != 2 or wide != 16:
        return plain_front(shards, tokens, starts, scales, heads)
    window = 3 * rows
    like = jax.ShapeDtypeStruct
    out_shape = [like((wide, *one.shape), one.dtype) for one in shards] + [
        like((3, rows, width), BF16),
        like((window, width), BF16),
        like((rows, width), BF16),
        like((window, width), BF16),
        like((window, width), BF16),
        like((rows, width), F32),
        like((rows, width), BF16),
        like((heads // 2, 2, rows), F32),
    ]
    sems = AG_SEMS * len(shards) + 2
    scratch = [
        ((3, rows, width), BF16),
        ((window, width), BF16),
        ((wide, *shards[1].shape), BF16),
        ((rows, width), BF16),
        ((window, width), BF16),
        ((window, width), BF16),
        ((rows, width), F32),
        ((rows, width), BF16),
        ((16, width), F32),
        ((wide, *shards[0].shape), BF16),
        ((rows // Q_TILE, window - rows + Q_TILE, Q_TILE), F32),
        ((128, window), BF16),
        ((128, rows), F32),
    ]
    return pl.pallas_call(
        functools.partial(front_kernel, thirds, width // heads),
        out_shape=out_shape,
        in_specs=[VMEM] * 8,
        out_specs=[HBM] * 12 + [VMEM],
        scratch_shapes=[pltpu.VMEM(shape, dtype) for shape, dtype in scratch]
        + [
            pltpu.SemaphoreType.DMA((sems,)),
            pltpu.SemaphoreType.DMA((sems,)),
            pltpu.SemaphoreType.DMA((9,)),
        ],
        compiler_params=pltpu.CompilerParams(
            collective_id=0, has_side_effects=True, vmem_limit_bytes=58 << 20
        ),
        name="front",
    )(*shards, tokens, starts, scales)


def row_chunk(rows, columns, most):
    chunk = min(rows, max(16, most // columns // 16 * 16))
    while rows % chunk:
        chunk -= 16
    return chunk


def accumulate(target, source):
    *lead, rows, columns = source.shape
    chunk = row_chunk(rows, columns, 65536)
    per = rows // chunk
    many = per
    for size in lead:
        many *= size

    def step(number, carry):
        part = pl.ds(pl.multiple_of(lax.rem(number, per) * chunk, 16), chunk)
        rest, index = number // per, []
        for size in reversed(lead):
            index.insert(0, lax.rem(rest, size))
            rest = rest // size
        at = (*index, part)
        target[at] = (target[at].astype(F32) + source[at].astype(F32)).astype(target.dtype)
        return carry

    lax.fori_loop(0, many, step, 0)


RS_SEMS = 12


def reduce_ticks(me, wire, base, local, grad, quarter, held, bufs, final, squares, limit):
    from_core, from_y, from_x, from_down, from_up, from_last = bufs
    count, columns = held.shape[-2:]
    inside = count - quarter
    plane = pl.ds(pl.multiple_of(me.y * quarter, 16), inside) if quarter else pl.ds(0, count)
    mine = held.at[:, me.x, plane]
    take = pltpu.make_async_copy(grad.at[:, :, me.c], held, local)
    put_core = wire.put(grad.at[:, :, 1 - me.c], from_core, base, me.core_mate())
    got_core = wire.got(from_core, base, me.core_mate())
    put_x = wire.put(held.at[:, 1 - me.x, plane], from_x, base + 2, me.x_mate())
    got_x = wire.got(from_x, base + 2, me.x_mate())
    put_last = wire.put(mine.at[me.z], from_last, base + 3, me.y_mate())
    got_last = wire.got(from_last, base + 3, me.y_mate())
    if quarter:
        share = held.at[:, :, pl.ds(pl.multiple_of(me.y * inside, 16), quarter)]
        other = held.at[:, :, pl.ds(pl.multiple_of((1 - me.y) * inside, 16), quarter)]
        put_y = wire.put(other, from_y, base + 1, me.y_mate())
        got_y = wire.got(from_y, base + 1, me.y_mate())

    def start():
        take.start()
        put_core()

    def join_core():
        take.wait()
        got_core()
        accumulate(held, from_core)
        (put_y if quarter else put_x)()

    def join_y():
        got_y()
        accumulate(share, from_y)
        put_x()

    lines = []
    for tick in range(4):
        actions = []
        for place, sign, source, sems, onward, back in (
            (me.z, 1, from_down, 4, me.up(), me.down()),
            (3 - me.z, -1, from_up, 8, me.down(), me.up()),
        ):
            goal = me.z if tick == 3 else lax.rem(me.z + sign * (3 - tick) + 8, 4)
            sends = None if tick == 3 else both(place <= tick, place < 3)
            block, arrived = mine.at[goal], source.at[goal]
            got = wire.got(arrived, base + sems + goal, back)

            def take_in(block=block, arrived=arrived, got=got):
                got()
                accumulate(block, arrived)

            actions.append(
                functools.partial(when, both(sends, place > 0), take_in)
            )
            if sends is not None:
                actions.append(wire.put(block, arrived, base + sems + goal, onward, sends))
        lines.append(actions)

    def join_x():
        got_x()
        accumulate(mine, from_x)
        act(lines[0])

    def end_line():
        act(lines[3])
        put_last()

    def finish():
        got_last()
        own = held.at[me.z, me.x]
        middle = count - 2 * quarter
        chunk = row_chunk(middle, columns, 32768)

        def add_planes(number, carry):
            at = pl.multiple_of(quarter + number * chunk, 16)
            there = pl.multiple_of(at - (1 - me.y) * quarter, 16)
            final[pl.ds(at, chunk)] = own[pl.ds(at, chunk)].astype(F32) + from_last[
                pl.ds(there, chunk)
            ].astype(F32)
            return carry

        lax.fori_loop(0, middle // chunk, add_planes, 0)
        if quarter:
            for plane_of, at, there in ((0, 0, 0), (1, count - quarter, count - 2 * quarter)):

                def from_held(at=at):
                    final[pl.ds(at, quarter)] = own[pl.ds(at, quarter)].astype(F32)

                def from_mate(at=at, there=there):
                    final[pl.ds(at, quarter)] = from_last[pl.ds(there, quarter)].astype(F32)

                pl.when(me.y == plane_of)(from_held)
                pl.when(me.y != plane_of)(from_mate)

        def square(number, total):
            value = final[pl.ds(pl.multiple_of(number * 8, 8), 8)]
            power = value * value
            if limit % 8:
                place = number * 8 + lax.broadcasted_iota(jnp.int32, power.shape, 0)
                power = jnp.where(place < limit, power, 0.0)
            folded = power[:, :128]
            for lane in range(128, columns, 128):
                folded = folded + power[:, lane : lane + 128]
            return total + folded

        squares[...] = squares[...] + lax.fori_loop(
            0, (limit + 7) // 8, square, jnp.zeros((8, 128), F32)
        )

    return [
        start, join_core, *([join_y] if quarter else []), join_x,
        functools.partial(act, lines[1]), functools.partial(act, lines[2]), end_line, finish,
    ]


def in_rounds(sequences):
    last = max(k + len(one) for k, one in enumerate(sequences))
    rounds = []
    for number in range(last):
        actions = [
            one[number - k] for k, one in enumerate(sequences) if 0 <= number - k < len(one)
        ]
        rounds.append(functools.partial(act, actions[::-1]))
    return rounds


def reduce_kernel(pieces, *refs):
    refs = list(refs)
    arrays = 1 + max(piece[0] for piece in pieces)
    results = 1 + max(piece[5] for piece in pieces)
    count = len(pieces)
    grads, halo = refs[:arrays], refs[arrays]
    finals, (back, norm) = refs[arrays + 1 :][:results], refs[arrays + 1 + results :][:2]
    scratch = refs[arrays + 3 + results :]
    blank, passing, joined, tiles, send, recv, local = scratch[-7:]
    me = Place()
    ending = RS_SEMS * count
    blank[...] = jnp.zeros_like(blank)
    tiles[...] = jnp.zeros_like(tiles)
    clear = [
        (me.w >= 14, pltpu.make_async_copy(blank, back.at[0], local.at[count])),
        (me.c == 1, pltpu.make_async_copy(blank, back.at[1], local.at[count + 1])),
    ]
    for holds, one in clear:
        pl.when(holds)(one.start)
    steps = [me.wide(jnp.bitwise_xor(me.w, bit)) for bit in (1, 2, 4, 8)]
    wire = Wire(send, recv)
    far = me.wide(lax.rem(me.w + 14, 16))
    inner = me.w >= 2
    joins = both(me.c == 1, inner)
    load = pltpu.make_async_copy(halo.at[0], joined, local.at[count + 2])
    firsts = [
        wire.put(halo.at[0], back.at[0], ending, far, both(me.c == 0, inner)),
        wire.put(halo.at[1], back.at[1], ending + 1, me.core_mate(), me.c == 1),
        wire.put(halo.at[1], passing, ending + 2, me.core_mate(), both(me.c == 0, inner)),
    ]
    got_passing = wire.got(passing, ending + 2, me.core_mate())
    put_joined = wire.put(joined, back.at[0], ending, far, joins)
    got_back = [
        wire.got(back.at[0], ending, far, me.w < 14),
        wire.got(back.at[1], ending + 1, me.core_mate(), me.c == 0),
    ]

    def halo_start():
        act(firsts)
        pl.when(joins)(load.start)

    def halo_join():
        def join():
            load.wait()
            got_passing()
            accumulate(joined, passing)

        pl.when(joins)(join)
        put_joined()

    sequences = []
    for k, (number, first, rows, quarter, limit, result, column) in enumerate(pieces):
        here = pl.ds(first, rows)
        final = finals[result].at[here, pl.ds(column, grads[number].shape[-1])]
        sequences.append(
            reduce_ticks(
                me, wire, RS_SEMS * k, local.at[k],
                grads[number].at[:, :, :, here], quarter, scratch[7 * k],
                scratch[7 * k + 1 : 7 * k + 7], final, tiles.at[0], limit,
            )
        )
    greet(me, steps[2:])
    nothing = functools.partial(act, [])
    halo_ticks = [halo_start, halo_join, *[nothing] * 6, functools.partial(act, got_back)]
    act(in_rounds([sequences[0], halo_ticks, *sequences[1:]]))
    for k, partner in enumerate(steps):
        index = ending + 3 + k
        moved = wire.copy(tiles.at[k], tiles.at[5 + k], index, partner)
        moved.start()
        moved.wait()
        tiles[k + 1] = tiles[k] + tiles[5 + k]
    norm[...] = tiles[4]
    wire.finish()
    for holds, one in clear:
        pl.when(holds)(one.wait)


def piece_buffers(rows, columns, quarter, dtype):
    inside = rows - quarter
    some = (4, 2, quarter, columns) if quarter else (1, 1, 16, 128)
    shapes = [
        (4, 2, rows, columns),
        (4, 2, rows, columns),
        some,
        (4, inside, columns),
        (4, inside, columns),
        (4, inside, columns),
        (inside, columns),
    ]
    return [pltpu.VMEM(shape, dtype) for shape in shapes]


def reduce_all(grads, halo, pieces):
    wide = lax.axis_size("wide")
    if lax.axis_size("dp") == 2 and wide == 16:
        count = len(pieces)
        tokens = halo.shape[1:]
        sizes = {}
        for number, _, _, _, _, result, column in pieces:
            _, rows, columns = grads[number].shape
            sizes[result] = (rows, max(column + columns, sizes.get(result, (0, 0))[1]))
        out_shape = [jax.ShapeDtypeStruct(sizes[k], F32) for k in range(len(sizes))]
        out_shape.append(jax.ShapeDtypeStruct(halo.shape, halo.dtype))
        out_shape.append(jax.ShapeDtypeStruct((8, 128), F32))
        scratch = []
        for number, _, rows, quarter, *_ in pieces:
            one = grads[number]
            scratch += piece_buffers(rows, one.shape[2], quarter, one.dtype)
        sems = RS_SEMS * count + 7
        return pl.pallas_call(
            functools.partial(reduce_kernel, pieces),
            out_shape=out_shape,
            in_specs=[HBM] * (len(grads) + 1),
            out_specs=[VMEM] * len(sizes) + [HBM, VMEM],
            scratch_shapes=scratch
            + [
                pltpu.VMEM(tokens, BF16),
                pltpu.VMEM(tokens, BF16),
                pltpu.VMEM(tokens, BF16),
                pltpu.VMEM((9, 8, 128), F32),
                pltpu.SemaphoreType.DMA((sems,)),
                pltpu.SemaphoreType.DMA((sems,)),
                pltpu.SemaphoreType.DMA((count + 3,)),
            ],
            compiler_params=pltpu.CompilerParams(
                collective_id=1, has_side_effects=True, vmem_limit_bytes=60 << 20
            ),
            name="reduce_all",
        )(*[one.reshape(4, 2, 2, *one.shape[1:]) for one in grads], halo)
    whole = [
        lax.psum(
            lax.psum_scatter(one.astype(F32), "wide", scatter_dimension=0, tiled=False), "dp"
        )
        for one in grads
    ]
    totals = []
    for result in range(1 + max(piece[5] for piece in pieces)):
        columns = {piece[6]: whole[piece[0]] for piece in pieces if piece[5] == result}
        totals.append(jnp.concatenate([columns[key] for key in sorted(columns)], axis=1))
    back = jnp.stack([from_behind(halo[0], "wide", -2), from_behind(halo[1], "wide", -1)])
    squares = jnp.float32(0.0)
    for number, first, _, _, limit, *_ in pieces:
        part = whole[number][first : first + limit]
        squares = squares + jnp.sum(part * part)
    norm = jnp.zeros((8, 128), F32).at[0, 0].set(lax.psum(squares, "wide"))
    return [*totals, back, norm]


F_TILE = 256


def lane_sums(values):
    total = values[:, :128]
    for lane in range(128, values.shape[1], 128):
        total = total + values[:, lane : lane + 128]
    return total


def ffn_kernel(
    a_ref, x_ref, gy_ref, w1_ref, w2_ref, par_ref, bias_ref,
    out_ref, mid_ref, df_ref, da_ref, sums_ref,
    act, slope, grad, stats,
):
    blocks, _, units = w1_ref.shape
    tile = a_ref.shape[0]
    count = blocks * units
    first_step = pl.program_id(0) == 0

    @pl.when(first_step)
    def _():
        sums_ref[...] = jnp.zeros_like(sums_ref)

    stats[...] = jnp.zeros_like(stats)

    def columns(k):
        return pl.ds(pl.multiple_of(k * units, units), units)

    def forward(k, carry):
        pre = dot(a_ref[...], w1_ref[k]) + par_ref[2:3, columns(k)]
        half = 0.5 + 0.5 * lax.erf(pre * (0.5**0.5))
        value = pre * half
        act[k] = value
        slope[k] = half + pre * (jnp.exp(-0.5 * pre * pre) * (0.5 / jnp.pi) ** 0.5)
        stats[0] += lane_sums(value)
        stats[1] += lane_sums(value * value)
        return carry

    lax.fori_loop(0, blocks, forward, 0, unroll=2)
    mean = jnp.sum(stats[0], axis=1, keepdims=True) / count
    second = jnp.sum(stats[1], axis=1, keepdims=True) / count
    scale = lax.rsqrt(second - mean * mean + norm_epsilon)

    def middle(k, carry):
        here = columns(k)
        hat = (act[k] - mean) * scale
        mid_ref[:, here] = (hat * par_ref[0:1, here] + par_ref[1:2, here]).astype(BF16)
        down = dot(gy_ref[...], w2_ref[here, :], 1, 1)
        scaled = down * par_ref[0:1, here]
        cross = scaled * hat
        act[k] = hat
        grad[k] = scaled
        stats[2] += lane_sums(scaled)
        stats[3] += lane_sums(cross)
        sums_ref[0:1, here] += jnp.sum(down * hat, axis=0, keepdims=True)
        sums_ref[1:2, here] += jnp.sum(down, axis=0, keepdims=True)
        return carry

    lax.fori_loop(0, blocks, middle, 0, unroll=2)
    plain = jnp.sum(stats[2], axis=1, keepdims=True) / count
    crossed = jnp.sum(stats[3], axis=1, keepdims=True) / count
    width = out_ref.shape[1]
    part = min(width, 512)
    for start in range(0, width, part):
        here = slice(start, start + part)
        total = dot(mid_ref[...], w2_ref[:, here])
        out_ref[:, here] = (x_ref[:, here] + (total + bias_ref[:, here])).astype(BF16)

    def backward(k, carry):
        here = columns(k)
        back = scale * (grad[k] - plain - act[k] * crossed) * slope[k]
        low = back.astype(BF16)
        df_ref[:, here] = low
        sums_ref[2:3, here] += jnp.sum(low.astype(F32), axis=0, keepdims=True)
        return carry

    lax.fori_loop(0, blocks, backward, 0, unroll=2)
    da_ref[...] = jnp.zeros_like(da_ref)

    def back_out(k, carry):
        da_ref[...] += dot(df_ref[:, columns(k)], w1_ref[k], 1, 1)
        return carry

    lax.fori_loop(0, blocks, back_out, 0, unroll=2)


def ffn(rows, residual, out_grad, w1, w2, par, bias):
    tokens, width = rows.shape
    blocks, _, units = w1.shape
    hidden = blocks * units
    by_tile = lambda columns: pl.BlockSpec((F_TILE, columns), lambda t: (t, 0))
    once = pl.Buffered(1)
    return pl.pallas_call(
        ffn_kernel,
        grid=(tokens // F_TILE,),
        in_specs=[
            by_tile(width),
            by_tile(width),
            by_tile(width),
            pl.BlockSpec(w1.shape, lambda t: (0, 0, 0), pipeline_mode=once),
            pl.BlockSpec(w2.shape, lambda t: (0, 0), pipeline_mode=once),
            pl.BlockSpec(par.shape, lambda t: (0, 0)),
            pl.BlockSpec(bias.shape, lambda t: (0, 0)),
        ],
        out_specs=[
            by_tile(width),
            by_tile(hidden),
            by_tile(hidden),
            by_tile(width),
            pl.BlockSpec(par.shape, lambda t: (0, 0)),
        ],
        out_shape=[
            jax.ShapeDtypeStruct((tokens, width), BF16),
            jax.ShapeDtypeStruct((tokens, hidden), BF16),
            jax.ShapeDtypeStruct((tokens, hidden), BF16),
            jax.ShapeDtypeStruct((tokens, width), F32),
            jax.ShapeDtypeStruct(par.shape, F32),
        ],
        scratch_shapes=[pltpu.VMEM((blocks, F_TILE, units), F32)] * 3
        + [pltpu.VMEM((4, F_TILE, 128), F32)],
        compiler_params=pltpu.CompilerParams(vmem_limit_bytes=60 << 20),
        name="ffn",
    )(rows, residual, out_grad, w1, w2, par, bias)


def ffn_weights_kernel(a_ref, gy_ref, mid_ref, df_ref, dw1_ref, dw2_ref, a_t):
    @pl.when(pl.program_id(0) == 0)
    def _():
        a_t[...] = a_ref[...].T

    dw1_ref[0] = dot(a_t[...], df_ref[...]).astype(BF16)
    dw2_ref[0] = dot(mid_ref[...].T, gy_ref[...]).astype(BF16)


def ffn_weights(rows, out_grad, middle, pre_grad, blocks):
    tokens, width = rows.shape
    units = middle.shape[1] // blocks
    whole = pl.BlockSpec((tokens, width), lambda k: (0, 0))
    block = pl.BlockSpec((tokens, units), lambda k: (0, k))
    return pl.pallas_call(
        ffn_weights_kernel,
        grid=(blocks,),
        in_specs=[whole, whole, block, block],
        out_specs=[
            pl.BlockSpec((1, width, units), lambda k: (k, 0, 0)),
            pl.BlockSpec((1, units, width), lambda k: (k, 0, 0)),
        ],
        out_shape=[
            jax.ShapeDtypeStruct((blocks, width, units), BF16),
            jax.ShapeDtypeStruct((blocks, units, width), BF16),
        ],
        scratch_shapes=[pltpu.VMEM((width, tokens), BF16)],
        compiler_params=pltpu.CompilerParams(vmem_limit_bytes=40 << 20),
        name="ffn_weights",
    )(rows, out_grad, middle, pre_grad)


def plane_share(rows):
    return rows // 16 * 3 // 8 * 16


def pack(parts):
    flat = jnp.concatenate(parts, axis=1)
    size = -(-flat.shape[1] // 2048) * 2048
    return jnp.pad(flat, ((0, 0), (0, size - flat.shape[1]))).reshape(flat.shape[0], -1, 128)


def to_slabs(rows, wide):
    count, columns = rows.shape
    return rows.reshape(count, wide, -1).transpose(1, 0, 2).reshape(wide, -1)


def unpack_small(full, vector_shape, hidden_shape):
    wide = full.shape[0]
    count, each = vector_shape
    vectors = full[:, :count, :each].transpose(1, 0, 2).reshape(count, -1)
    rows, size = hidden_shape
    if size % 128 == 0:
        hidden = full[:, count:].reshape(wide, rows, size)
    else:
        hidden = full[:, count:, :size]
    hidden = hidden.transpose(1, 0, 2).reshape(rows, -1)
    return vectors.astype(F32), hidden.astype(F32)


def regroup(blocks, units):
    slabs, rows, columns = blocks.shape
    join = max(1, units // columns)
    if join == 1:
        return blocks
    return blocks.reshape(slabs // join, join, rows, columns).transpose(0, 2, 1, 3).reshape(
        slabs // join, rows, join * columns
    )


def ungroup(blocks, columns):
    slabs, rows, units = blocks.shape
    join = units // columns
    if join == 1:
        return blocks
    return blocks.reshape(slabs, rows, join, columns).transpose(0, 2, 1, 3).reshape(
        slabs * join, rows, columns
    )


def body(
    inputs,
    out_grad,
    doc_lengths,
    step_count,
    qkv_weight,
    qkv_first,
    qkv_second,
    out_weight,
    out_first,
    out_second,
    fc1_weight,
    fc1_first,
    fc1_second,
    fc2_weight,
    fc2_first,
    fc2_second,
    model_vectors,
    vectors_first,
    vectors_second,
    hidden_vectors,
    hidden_first,
    hidden_second,
    head_scale,
    head_first,
    head_second,
):
    tokens_dev = inputs.shape[0]
    width = inputs.shape[1]
    heads_count = head_scale.shape[0]
    head_size = width // heads_count
    wide = lax.axis_size("wide")
    hidden_width = hidden_vectors.shape[1] * wide
    vector_size, hidden_size = model_vectors.size, hidden_vectors.size

    fc1_rows, fc2_rows = fc1_weight.shape[0], fc2_weight.shape[0]
    qkv_rows, out_rows = qkv_weight.shape[0], out_weight.shape[0]
    small = jnp.concatenate(
        [
            jnp.pad(model_vectors, ((0, 0), (0, max(0, 128 - model_vectors.shape[1])))),
            hidden_vectors.reshape(-1, min(128, hidden_vectors.shape[1])),
        ]
        if hidden_vectors.shape[1] % 128 == 0
        else [
            jnp.pad(one, ((0, 0), (0, 128 - one.shape[1]))) for one in (model_vectors, hidden_vectors)
        ]
    ).astype(BF16)
    heads_low = lax.optimization_barrier(head_scale.astype(BF16)).astype(F32)
    starts = doc_starts(
        doc_lengths, lax.axis_index("dp"), lax.axis_index("wide") * tokens_dev, tokens_dev
    )
    starts = jnp.maximum(starts - (lax.axis_index("wide") - 2) * tokens_dev, 0).reshape(1, -1)
    scales = jnp.repeat(heads_low, head_size).reshape(1, width)
    gathered = front(
        [
            small,
            qkv_weight.astype(BF16),
            out_weight.astype(BF16),
            fc1_weight.astype(BF16),
            fc2_weight.astype(BF16),
        ],
        tuple(plane_share(one) for one in (0, qkv_rows, out_rows, fc1_rows, fc2_rows)),
        inputs,
        starts,
        scales,
        heads_count,
    )
    small_full, qkv_full, out_full, fc1_full, fc2_full, tokens_all, normed_low = gathered[:7]
    queries, keys_all, values_all, attended, mixed_low, log_totals = gathered[7:]
    vectors, hidden_par = unpack_small(small_full, model_vectors.shape, hidden_vectors.shape)
    qkv_full = qkv_full.reshape(width, 3 * width)
    out_full = out_full.reshape(width, width)
    fc2_full = fc2_full.reshape(hidden_width, width)

    own = slice(2 * tokens_dev, None)
    tokens_in = inputs.astype(F32)
    _, hat_in, scale_in = layer_norm(
        tokens_all.reshape(-1, width).astype(F32), vectors[0], vectors[3]
    )
    proj_out = jnp.dot(mixed_low, out_full, preferred_element_type=F32) + vectors[6]
    normed_post, hat_post, scale_post = layer_norm(proj_out, vectors[1], vectors[7])
    residual = tokens_in + normed_post
    normed_two, hat_two, scale_two = layer_norm(residual, vectors[2], vectors[8])
    rows_low = normed_two.astype(BF16)
    grad_in = out_grad.astype(F32)

    output, middle_low, pre_low, rows_grad, hidden_grad = ffn(
        rows_low, residual, out_grad, regroup(fc1_full, 256), fc2_full, hidden_par, vectors[9:10]
    )
    fc1_grad, fc2_grad = ffn_weights(rows_low, out_grad, middle_low, pre_low, hidden_width // 256)
    out_bias_total = jnp.sum(grad_in, axis=0)
    residual_grad = grad_in + norm_back(rows_grad, hat_two, scale_two, vectors[2])
    gain_two_grad = jnp.sum(rows_grad * hat_two, axis=0)
    bias_two_grad = jnp.sum(rows_grad, axis=0)
    gain_post_grad = jnp.sum(residual_grad * hat_post, axis=0)
    bias_post_grad = jnp.sum(residual_grad, axis=0)
    proj_low = norm_back(residual_grad, hat_post, scale_post, vectors[1]).astype(BF16)
    proj_bias_grad = jnp.sum(proj_low.astype(F32), axis=0)
    out_weight_grad = jnp.einsum("td,te->de", mixed_low, proj_low, preferred_element_type=F32)
    mixed_grad = jnp.einsum("te,de->td", proj_low, out_full, preferred_element_type=F32)
    head_grad = jnp.sum((mixed_grad * attended).reshape(tokens_dev, heads_count, -1), axis=(0, 2))
    attended_low = (mixed_grad * scales).astype(BF16)
    delta = (
        jnp.sum((attended_low.astype(F32) * attended).reshape(tokens_dev, heads_count, -1), axis=-1)
        .transpose(1, 0)
        .reshape(heads_count // 2, 2, tokens_dev)
    )
    query_grad, key_grad, value_grad = attend_back(
        queries, keys_all, values_all, attended_low, log_totals, delta, starts, heads_count
    )
    query_bias_grad = jnp.sum(query_grad.astype(F32), axis=0)
    value_bias_grad = jnp.sum(value_grad.astype(F32), axis=0)
    query_part = jnp.einsum("td,te->de", normed_low[own], query_grad, preferred_element_type=F32)
    key_part = jnp.einsum("td,te->de", normed_low, key_grad, preferred_element_type=F32)
    value_part = jnp.einsum("td,te->de", normed_low, value_grad, preferred_element_type=F32)
    normed_grad = jnp.einsum(
        "te,de->td", key_grad, qkv_full[:, width : 2 * width], preferred_element_type=F32
    ) + jnp.einsum("te,de->td", value_grad, qkv_full[:, 2 * width :], preferred_element_type=F32)
    halo_grad = normed_grad[: 2 * tokens_dev]
    own_grad = normed_grad[own] + jnp.einsum(
        "te,de->td", query_grad, qkv_full[:, :width], preferred_element_type=F32
    )
    gain_in_grad = jnp.sum(halo_grad * hat_in[: 2 * tokens_dev], axis=0) + jnp.sum(
        own_grad * hat_in[own], axis=0
    )
    bias_in_grad = jnp.sum(halo_grad, axis=0) + jnp.sum(own_grad, axis=0)
    vector_grad = jnp.stack(
        [
            gain_in_grad,
            gain_post_grad,
            gain_two_grad,
            bias_in_grad,
            query_bias_grad,
            value_bias_grad,
            proj_bias_grad,
            bias_post_grad,
            bias_two_grad,
            out_bias_total,
        ]
    )
    small_grad = pack(
        [
            to_slabs(vector_grad, wide),
            to_slabs(hidden_grad, wide),
            jnp.broadcast_to(head_grad[None], (wide, heads_count)),
        ]
    )
    counted = (vector_size + hidden_size) // 128
    small_part, qkv_part, out_part, fc1_part, fc2_part, halo_back, norm_tile = reduce_all(
        [
            small_grad,
            query_part.astype(BF16).reshape(wide, -1, width),
            key_part.astype(BF16).reshape(wide, -1, width),
            value_part.astype(BF16).reshape(wide, -1, width),
            out_weight_grad.astype(BF16).reshape(wide, -1, width),
            ungroup(fc1_grad, fc1_weight.shape[1]),
            fc2_grad.reshape(wide, -1, width),
        ],
        halo_grad.astype(BF16).reshape(2, tokens_dev, width),
        tuple(
            (6, k * (fc2_rows // 4), fc2_rows // 4, fc2_rows // 16, fc2_rows // 4, 4, 0)
            for k in range(4)
        )
        + tuple(
            (5, k * (fc1_rows // 4), fc1_rows // 4, plane_share(fc1_rows // 4), fc1_rows // 4, 3, 0)
            for k in range(4)
        )
        + (
            (4, 0, out_rows, out_rows // 4, out_rows, 2, 0),
            (0, 0, small_grad.shape[1], 0, counted, 0, 0),
            (1, 0, qkv_rows, qkv_rows // 4, qkv_rows, 1, 0),
            (2, 0, qkv_rows, qkv_rows // 4, qkv_rows, 1, width),
            (3, 0, qkv_rows, qkv_rows // 4, qkv_rows, 1, 2 * width),
        ),
    )
    total_grad = own_grad + halo_back[0].astype(F32) + halo_back[1].astype(F32)
    input_grad = residual_grad + norm_back(total_grad, hat_in[own], scale_in[own], vectors[0])
    flat = small_part.reshape(-1)
    vector_part = flat[:vector_size].reshape(model_vectors.shape)
    hidden_part = flat[vector_size : vector_size + hidden_size].reshape(hidden_vectors.shape)
    head_total = flat[vector_size + hidden_size :][:heads_count]
    grad_norm = jnp.sqrt(jnp.sum(norm_tile) + jnp.sum(head_total * head_total))
    factor = jnp.minimum(1.0, clip_limit / (grad_norm + 1e-06))
    step = step_count[0].astype(F32)
    grads = (qkv_part, out_part, fc1_part, fc2_part, vector_part, hidden_part, head_total)
    params = (
        qkv_weight,
        out_weight,
        fc1_weight,
        fc2_weight,
        model_vectors,
        hidden_vectors,
        head_scale,
    )
    firsts = (qkv_first, out_first, fc1_first, fc2_first, vectors_first, hidden_first, head_first)
    seconds = (
        qkv_second,
        out_second,
        fc1_second,
        fc2_second,
        vectors_second,
        hidden_second,
        head_second,
    )
    rates = (
        matrix_rate,
        matrix_rate,
        matrix_rate,
        matrix_rate,
        vector_rate,
        vector_rate,
        vector_rate,
    )
    decays = (weight_decay, weight_decay, weight_decay, weight_decay, 0.0, 0.0, 0.0)
    updated = []
    for number in range(7):
        updated.extend(
            adam_step(
                grads[number] * factor,
                params[number],
                firsts[number],
                seconds[number],
                step,
                rates[number],
                decays[number],
            )
        )
    return (
        output,
        input_grad,
        grad_norm.reshape(1),
        updated[0],
        updated[1],
        updated[2],
        updated[3],
        updated[4],
        updated[5],
        updated[6],
        updated[7],
        updated[8],
        updated[9],
        updated[10],
        updated[11],
        updated[12],
        updated[13],
        updated[14],
        updated[15],
        updated[16],
        updated[17],
        updated[18],
        updated[19],
        updated[20],
    )


def solution(mesh):
    placed = (
        P(("dp", "wide"), None),
        P(("dp", "wide"), None),
        P(),
        P(),
        P("wide", None),
        P("wide", None),
        P("wide", None),
        P("wide", None),
        P("wide", None),
        P("wide", None),
        P(None, "wide"),
        P(None, "wide"),
        P(None, "wide"),
        P("wide", None),
        P("wide", None),
        P("wide", None),
        P(None, "wide"),
        P(None, "wide"),
        P(None, "wide"),
        P(None, "wide"),
        P(None, "wide"),
        P(None, "wide"),
        P(),
        P(),
        P(),
    )
    return jax.shard_map(
        body,
        mesh=mesh,
        in_specs=placed,
        out_specs=(
            P(("dp", "wide"), None),
            P(("dp", "wide"), None),
            P(),
            P("wide", None),
            P("wide", None),
            P("wide", None),
            P("wide", None),
            P("wide", None),
            P("wide", None),
            P(None, "wide"),
            P(None, "wide"),
            P(None, "wide"),
            P("wide", None),
            P("wide", None),
            P("wide", None),
            P(None, "wide"),
            P(None, "wide"),
            P(None, "wide"),
            P(None, "wide"),
            P(None, "wide"),
            P(None, "wide"),
            P(),
            P(),
            P(),
        ),
        check_vma=False,
    )
```

time: 773 us -> 534 us (0.69)
  matrix products: 261 us -> 37.9 us
  Pallas kernels: 319 us -> 409 us
  other arithmetic: 125 us -> 49.3 us
  local copies, waits for them, and re-layouts: 57.1 us -> 22.5 us
    dot_general x16 -> x4, matrix products: 244 us -> 18.5 us  [the longest x1 5.67 us: body(): jnp.einsum('te,de->td', value_grad, qkv_full[:, 2 * width:], preferred_el...]
    pallas_call x1 -> x4, Pallas kernels: 132 us -> 238 us  [the longest x1 143 us: front(): pl.pallas_call(functools.partial(front_kernel, thirds, width // heads), o...]
    reduce_sum x8 -> x5, other arithmetic: 65 us -> 5.6 us  [the longest x1 2.46 us: body(): value_bias_grad = jnp.sum(value_grad.astype(F32), axis=0)]
    convert_element_type x5 -> x1, local copies, waits for them, and re-layouts: 18.6 us -> 0.66 us  [unpack_small(): return (vectors.astype(F32), hidden.astype(F32))]
    pallas_call x1, Pallas kernels: 187 us -> 172 us  [reduce_all(): pl.pallas_call(functools.partial(reduce_kernel, pieces), out_shape=out_sh...]
    slice x4 -> x2, local copies, waits for them, and re-layouts: 10.8 us -> 0.83 us  [the longest x1 0.67 us: body(): vectors[9:10]]
    unnamed x157 -> x101, local copies, waits for them, and re-layouts: 16.2 us -> 11.1 us
where the time goes in v3:
time: 534 us; the launch traced here: 524 us
  Pallas kernels  409 us (77%)
  other arithmetic  49.3 us (9%)
  matrix products  37.9 us (7%)
  local copies, waits for them, and re-layouts  22.5 us (4%)
    pallas_call x1, Pallas kernels, reduce_all(): pl.pallas_call(functools.partial(reduce_kernel, pieces), out_shape=out_sh...  172 us
    pallas_call x1, Pallas kernels, front(): pl.pallas_call(functools.partial(front_kernel, thirds, width // heads), o...  143 us
    pallas_call x1, Pallas kernels, ffn(): pl.pallas_call(ffn_kernel, grid=(tokens // F_TILE,), in_specs=[by_tile(wi...  47.3 us
    pallas_call x1, Pallas kernels, attend_back(): pl.pallas_call(functools.partial(attend_back_kernel, width // heads), gri...  32.1 us
    pallas_call x1, Pallas kernels, ffn_weights(): pl.pallas_call(ffn_weights_kernel, grid=(blocks,), in_specs=[whole, whole...  15.3 us
    sub x7, other arithmetic, adam_step(): weight_new = weight - rate * (direction + decay * weight)  11.1 us
    unnamed x101, local copies, waits for them, and re-layouts  11.1 us

profile of v3, /device:TPU:0, one launch (start us, length us, event | category | flops | bytes accessed | tf_op | source)
XLA Modules:
  0.0 524.0 jit_solution(14057252738894889811)
XLA Ops:
  3.8 2.1 convert_element_type.110.refs_3_
  8.9 143.0 %front.1 = (bf16[16,16,128]{2,1,0:T(8,128)(2,1)}, bf16[16,64,3072]{2,1,0:T(8,128)(2,1)}, bf16[16,64,1024]{2,1,0:T(8,128)(2,1)}, bf16[16,1024,256]{2,1,0:T(8,128)...) custom-call(bf16[16,128]{1,0:T(8,128)(2,1)} %fusion.18.refs_0_, ...), custom_call_target="tpu_custom_call" | custom-call | tf_op jit(solution)/shard_map/front/pallas_call | solution.py:601
  153.0 3.3 add_reduce_fusion
  158.2 2.3 fusion.30
  161.1 1.4 add_convert_fusion.a_ref
  163.8 47.3 %ffn.1 = (bf16[512,1024]{1,0:T(8,128)(2,1)}, bf16[512,4096]{1,0:T(8,128)(2,1)}, bf16[512,4096]{1,0:T(8,128)(2,1)}, f32[512,1024]{1,0:T(8,128)}, f32[3,4096]{1,0:T(4,128)}) custom-call(bf16[512,1024]{1,0:T(8,128)(2,1)} %add_convert_fusion.a_ref, f32[512,1024]{1,0:T(8,128)} %copy-done.9, bf16[512,1024]{1,0:T(8,128)(2,1)} %gy_ref.3, ...), custom_call_target="tpu_custom_call" | custom-call | tf_op jit(solution)/shard_map/ffn/pallas_call | solution.py:1016
  211.2 2.2 copy-done.2
  213.4 2.2 copy-done.3
  215.6 15.3 %ffn_weights.1 = (bf16[16,1024,256]{2,1,0:T(8,128)(2,1)}, bf16[16,256,1024]{2,1,0:T(8,128)(2,1)}) custom-call(bf16[512,1024]{1,0:T(8,128)(2,1)S(1)} %copy-done, bf16[512,1024]{1,0:T(8,128)(2,1)S(1)} %copy-done.1, bf16[512,4096]{1,0:T(8,128)(2,1)S(1)} %copy-done.2, bf16[512,4096]{1,0:T(8,128)(2,1)S(1)} %copy-done.3), custom_call_target="tpu_custom_call" | custom-call | tf_op jit(solution)/shard_map/ffn_weights/pallas_call | solution.py:1063
  232.4 2.4 multiply_reduce_fusion.4
  236.8 2.7 convolution_convert_fusion
  239.6 4.9 convert_multiply_fusion
  244.5 3.0 copy.53
  247.5 2.0 bitcast_reduce_fusion
  249.5 1.9 copy-done.4
  251.4 32.1 %attend_back.1 = (bf16[512,1024]{1,0:T(8,128)(2,1)S(1)}, bf16[1536,1024]{1,0:T(8,128)(2,1)S(1)}, bf16[1536,1024]{1,0:T(8,128)(2,1)S(1)}) custom-call(s32[1,512]{1,0:T(1,128)S(1)} %bitcast.64, bf16[512,1024]{1,0:T(8,128)(2,1)S(1)} %copy-done.6, bf16[1536,1024]{1,0:T(8,128)(2,1)S(1)} %copy-done.4, bf16[1536,1024]{1,0:T(8,128)(2,1)} %get-tuple-element.64.v_ref, ...), custom_call_target="tpu_custom_call" | custom-call | tf_op jit(solution)/shard_map/attend_back/pallas_call | solution.py:202
  283.5 4.7 convolution_convert_fusion.1
  288.2 4.7 convolution_convert_fusion.2
  292.9 2.6 convolution_convert_fusion.3
  295.6 3.5 fusion.5
  299.0 5.7 %convolution_add_fusion = f32[1536,1024]{1,0:T(8,128)} fusion(f32[1536,1024]{1,0:T(8,128)S(1)} %fusion.5, bf16[1536,1024]{1,0:T(8,128)(2,1)S(1)} %get-tuple-element.69, bf16[1024,3072]{1,0:T(8,128)(2,1)S(1)} %bitcast.79), kind=kOutput, calls=%fused_computation.4 | convolution fusion | flops 3222798336 | bytes 17825792 | tf_op jit(solution)/shard_map/te,de->td/dot_general | solution.py:1246
  306.2 2.6 fusion
  308.9 5.9 %fusion.21 = (f32[1024]{0:T(1024)S(1)}, f32[1024]{0:T(1024)S(1)}, f32[512,1024]{1,0:T(8,128)S(1)}) fusion(f32[1536,1024]{1,0:T(8,128)S(1)} %fusion, bf16[512,1024]{1,0:T(8,128)(2,1)S(1)} %get-tuple-element.70, bf16[1024,3072]{1,0:T(8,128)(2,1)} %bitcast.75, f32[1536,1024]{1,0:T(8,128)} %convolution_add_fusion), kind=kOutput, calls=%fused_computation.112 | convolution fusion | flops 1075836928 | bytes 9445376 | tf_op jit(solution)/shard_map/te,de->td/dot_general | solution.py:1248
  314.7 3.0 slice_reduce_fusion
  318.2 2.5 convert_reduce_fusion
  322.4 3.8 slice.168
  326.3 171.6 %reduce_all.1 = (f32[16,128]{1,0:T(8,128)}, f32[64,3072]{1,0:T(8,128)}, f32[64,1024]{1,0:T(8,128)}, f32[1024,256]{1,0:T(8,128)}, f32[256,1024]{1,0:T(8,128)}, /*...) custom-call(f32[4,2,2,16,128]{4,3,2,1,0:T(8,128)} %bitcast.80, bf16[4,2,2,64,1024]{4,3,2,1,0:T(8,128)(2,1)} %bitcast.74, ...), custom_call_target="tpu_custom_call" | custom-call | tf_op jit(solution)/shard_map/reduce_all/pallas_call | solution.py:884
  505.9 4.3 multiply_subtract_fusion
  510.3 2.2 multiply_subtract_fusion.1
  514.2 1.8 multiply_subtract_fusion.2
  516.1 3.0 fusion.20
  519.1 3.4 multiply_add_fusion
  (177 shorter events, 25.9 us)
Async XLA Ops:
  0.7 5.2 copy-start.19
  0.7 6.1 %copy-start.22 = (f32[64,3072]{1,0:T(8,128)S(1)}, f32[64,3072]{1,0:T(8,128)}, u32[]{:S(2)}) copy-start(f32[64,3072]{1,0:T(8,128)} %param.29) | copy-start | bytes 2359300
  3.8 3.8 copy-start.27
  3.8 4.5 copy-start.36
  3.8 4.5 copy-start.37
  163.8 47.3 %copy-start = (bf16[512,1024]{1,0:T(8,128)(2,1)S(1)}, bf16[512,1024]{1,0:T(8,128)(2,1)}, u32[]{:S(2)}) copy-start(bf16[512,1024]{1,0:T(8,128)(2,1)} %add_convert_fusion.a_ref) | copy-start | bytes 3145732
  163.8 47.3 %copy-start.1 = (bf16[512,1024]{1,0:T(8,128)(2,1)S(1)}, bf16[512,1024]{1,0:T(8,128)(2,1)}, u32[]{:S(2)}) copy-start(bf16[512,1024]{1,0:T(8,128)(2,1)} %gy_ref.3) | copy-start | bytes 3145732
  215.5 15.3 %copy-start.10 = (f32[512,1024]{1,0:T(8,128)S(1)}, f32[512,1024]{1,0:T(8,128)}, u32[]{:S(2)}) copy-start(f32[512,1024]{1,0:T(8,128)} %copy-done.9) | copy-start | bytes 6291460
  215.6 15.3 %copy-start.17 = (f32[512,1024]{1,0:T(8,128)S(1)}, f32[512,1024]{1,0:T(8,128)}, u32[]{:S(2)}) copy-start(f32[512,1024]{1,0:T(8,128)} %get-tuple-element.60) | copy-start | bytes 6291460
  251.4 32.1 %copy-start.45 = (bf16[1536,1024]{1,0:T(8,128)(2,1)S(1)}, bf16[1536,1024]{1,0:T(8,128)(2,1)}, u32[]{:S(2)}) copy-start(bf16[1536,1024]{1,0:T(8,128)(2,1)} %get-tuple-element.72) | copy-start | bytes 9437188
  283.5 15.6 %copy-start.5 = (bf16[1536,1024]{1,0:T(8,128)(2,1)}, bf16[1536,1024]{1,0:T(8,128)(2,1)S(1)}, u32[]{:S(2)}) copy-start(bf16[1536,1024]{1,0:T(8,128)(2,1)S(1)} %get-tuple-element.69) | copy-start | bytes 9437188
  283.5 12.1 %slice-start = ((s8[6291456]{0:T(1024)(128)(4,1)}), s8[4194304]{0:T(1024)(128)(4,1)S(1)}, s32[]{:S(2)}) async-start(s8[6291456]{0:T(1024)(128)(4,1)} %bitcast.76), calls=%async_computation | async-start | bytes 8388608
  288.2 7.3 %slice-start.1 = ((s8[6291456]{0:T(1024)(128)(4,1)}), s8[2097152]{0:T(1024)(128)(4,1)S(1)}, s32[]{:S(2)}) async-start(s8[6291456]{0:T(1024)(128)(4,1)} %bitcast.76), calls=%async_computation.1 | async-start | bytes 4194304
  299.0 5.7 %copy-start.14 = (bf16[3,512,1024]{2,1,0:T(8,128)(2,1)S(1)}, bf16[3,512,1024]{2,1,0:T(8,128)(2,1)}, u32[]{:S(2)}) copy-start(bf16[3,512,1024]{2,1,0:T(8,128)(2,1)} %get-tuple-element.61) | copy-start | bytes 9437188
  308.8 5.9 %copy-start.11 = (f32[1536,1024]{1,0:T(8,128)}, f32[1536,1024]{1,0:T(8,128)S(1)}, u32[]{:S(2)}) copy-start(f32[1536,1024]{1,0:T(8,128)S(1)} %fusion) | copy-start | bytes 18874372
  318.1 3.5 copy-start.35
  326.2 176.4 %copy-start.42 = (f32[16]{0:T(128)S(1)}, f32[16]{0:T(128)}, u32[]{:S(2)}) copy-start(f32[16]{0:T(128)} %param.47) | copy-start | bytes 196
  326.2 176.4 %copy-start.43 = (f32[16]{0:T(128)S(1)}, f32[16]{0:T(128)}, u32[]{:S(2)}) copy-start(f32[16]{0:T(128)} %param.49) | copy-start | bytes 196
  326.2 176.4 %copy-start.44 = (f32[16]{0:T(128)S(1)}, f32[16]{0:T(128)}, u32[]{:S(2)}) copy-start(f32[16]{0:T(128)} %param.48) | copy-start | bytes 196
  326.2 177.6 %copy-start.40 = (f32[3,256]{1,0:T(4,128)S(1)}, f32[3,256]{1,0:T(4,128)}, u32[]{:S(2)}) copy-start(f32[3,256]{1,0:T(4,128)} %param.46) | copy-start | bytes 9220
  326.2 177.6 %copy-start.41 = (f32[3,256]{1,0:T(4,128)S(1)}, f32[3,256]{1,0:T(4,128)}, u32[]{:S(2)}) copy-start(f32[3,256]{1,0:T(4,128)} %param.45) | copy-start | bytes 9220
  326.2 179.0 %copy-start.38 = (f32[10,64]{1,0:T(8,128)S(1)}, f32[10,64]{1,0:T(8,128)}, u32[]{:S(2)}) copy-start(f32[10,64]{1,0:T(8,128)} %param.43) | copy-start | bytes 7684
  326.2 179.0 %copy-start.39 = (f32[10,64]{1,0:T(8,128)S(1)}, f32[10,64]{1,0:T(8,128)}, u32[]{:S(2)}) copy-start(f32[10,64]{1,0:T(8,128)} %param.42) | copy-start | bytes 7684
  326.2 179.6 %copy-start.20 = (f32[256,1024]{1,0:T(8,128)S(1)}, f32[256,1024]{1,0:T(8,128)}, u32[]{:S(2)}) copy-start(f32[256,1024]{1,0:T(8,128)} %param.38) | copy-start | bytes 3145732
  505.9 4.3 copy-start.21
  505.9 4.3 copy-start.24
  505.9 4.3 copy-start.25
  505.9 4.3 copy-start.26
  510.2 2.3 copy-start.31
  510.3 3.2 copy-start.29
  510.3 3.2 copy-start.30
  516.1 3.0 copy-start.16
  (17 other events, 32.2 us)

commit v4 on v3

--- a/solution.py
+++ b/solution.py
@@ -31,13 +31,6 @@
     scale = lax.rsqrt(variance + norm_epsilon)
     normed = center * scale
     return (normed * gain + shift, normed, scale)
-
-
-def norm_back(grad, normed, scale, gain):
-    scaled = grad * gain
-    mean_plain = jnp.mean(scaled, axis=-1, keepdims=True)
-    mean_cross = jnp.mean(scaled * normed, axis=-1, keepdims=True)
-    return scale * (scaled - mean_plain - normed * mean_cross)
 
 
 def doc_starts(doc_lengths, row, first, count):
@@ -156,18 +149,11 @@
     )(starts, scales, queries, keys, values)
 
 
-def attend_back_kernel(
-    size, starts, q_ref, k_ref, v_ref, do_ref, lse_ref, delta_ref,
-    dq_ref, dk_ref, dv_ref, bias, dk_sum, dv_sum, kt, dqt,
+def attend_back_pair(
+    size, q_ref, k_ref, v_ref, do_ref, lse_ref, delta_ref, dq_ref, dk_ref, dv_ref, bias, dk_sum, dv_sum, kt, dqt
 ):
     tokens, window = q_ref.shape[0], k_ref.shape[0]
-    before = window - tokens
-    span = before + Q_TILE
-
-    @pl.when(pl.program_id(0) == 0)
-    def _():
-        fill_mask(starts, bias, tokens, span, before)
-
+    span = window - tokens + Q_TILE
     kt[...] = k_ref[...].T
     dk_sum[...] = jnp.zeros_like(dk_sum)
     dv_sum[...] = jnp.zeros_like(dv_sum)
@@ -179,8 +165,8 @@
             zip(split_pair(q_ref[rows, :], size), split_pair(do_ref[rows, :], size))
         ):
             scores = dot(k_pair, q_one, 1, 1) + bias[tile]
-            probs = jnp.exp(scores - lse_ref[0, head : head + 1, rows])
-            grads = dot(v_pair, do_one, 1, 1) - delta_ref[0, head : head + 1, rows]
+            probs = jnp.exp(scores - lse_ref[head : head + 1, rows])
+            grads = dot(v_pair, do_one, 1, 1) - delta_ref[head : head + 1, rows]
             low = (probs * grads).astype(BF16)
             dv_sum[keys, :] += dot(probs.astype(BF16), do_one)
             dk_sum[keys, :] += dot(low, q_one)
@@ -189,6 +175,21 @@
     dq_ref[...] = (dqt[...].T * size ** (-0.5)).astype(BF16)
     dk_ref[...] = dk_sum[...].astype(BF16)
     dv_ref[...] = dv_sum[...].astype(BF16)
+
+
+def attend_back_kernel(
+    size, starts, q_ref, k_ref, v_ref, do_ref, lse_ref, delta_ref, dq_ref, dk_ref, dv_ref, bias, *scratch
+):
+    tokens, window = q_ref.shape[0], k_ref.shape[0]
+    before = window - tokens
+
+    @pl.when(pl.program_id(0) == 0)
+    def _():
+        fill_mask(starts, bias, tokens, before + Q_TILE, before)
+
+    attend_back_pair(
+        size, q_ref, k_ref, v_ref, do_ref, lse_ref.at[0], delta_ref.at[0], dq_ref, dk_ref, dv_ref, bias, *scratch
+    )
 
 
 def attend_back(queries, keys, values, outs_grad, lse, delta, starts, heads):
@@ -418,10 +419,10 @@
 
 def front_kernel(thirds, head_size, *refs):
     owns, (tokens, starts, scale_ref) = refs[:5], refs[5:8]
-    fulls, outs = refs[8:13], refs[13:20]
+    fulls, outs = refs[8:12], refs[12:19]
     xs_out, a_out, q_out, k_out, v_out, o_out, c_out = outs
-    lse_ref = refs[20]
-    (xs, a_all, qkv, q_all, k_all, v_all, o_all, c_all, vecs, small, bias, vt, ot, send, recv, local) = refs[21:]
+    lse_ref, vecs, par = refs[19:22]
+    (xs, a_all, qkv, q_all, k_all, v_all, o_all, c_all, small, bias, vt, ot, send, recv, local) = refs[22:]
     me = Place()
     count = len(owns)
     width = tokens.shape[1]
@@ -429,7 +430,7 @@
     window = 3 * rows
     before = window - rows
     span = before + Q_TILE
-    landings = (small, qkv, *fulls[2:])
+    landings = (small, qkv, *fulls[1:])
     keep = [
         pltpu.make_async_copy(own, full.at[me.w], local.at[k])
         for k, (own, full) in enumerate(zip(owns, landings))
@@ -451,7 +452,8 @@
     send_block = wire.put(tokens, xs.at[0], first, me.wide(lax.rem(me.w + 2, 16)), me.w < 14)
     send_near = wire.put(tokens, xs.at[1], second, me.core_mate(), me.c == 0)
     get_block = wire.got(xs.at[0], first, me.core_mate(), me.w >= 2)
-    pass_block = wire.put(xs.at[0], xs.at[1], second, me.core_mate(), both(me.c == 1, me.w >= 2))
+    passes = both(me.c == 1, me.w >= 2)
+    pass_block = wire.copy(xs.at[0], xs.at[1], second, me.core_mate())
     get_near = wire.got(xs.at[1], second, me.core_mate(), me.w >= 1)
     greet(me)
     early, late = ticks[:2], ticks[2:]
@@ -463,18 +465,15 @@
     for one in late:
         act(one[0])
     get_block()
-    pass_block()
+    when(passes, pass_block.start)
     fill_mask(starts, bias, rows, span, before)
     for tick in range(4, 7):
         act(early[0][tick] + early[1][tick])
     get_near()
+    when(passes, pass_block.wait_send)
     for one in keep:
         one.wait()
-    shared = [
-        pltpu.make_async_copy(small, fulls[0], local.at[0]),
-        pltpu.make_async_copy(qkv, fulls[1], local.at[1]),
-        pltpu.make_async_copy(xs, xs_out, local.at[2]),
-    ]
+    shared = [pltpu.make_async_copy(qkv, fulls[0], local.at[1])]
     for one in shared:
         one.start()
 
@@ -483,6 +482,12 @@
         even = small[2 * pair].astype(F32)
         odd = pltpu.roll(small[2 * pair + 1].astype(F32), 64, 1)
         vecs[:, pair * 128 : (pair + 1) * 128] = jnp.where(lane < 64, even, odd)
+    for slab in range(16):
+        values = small[slab].astype(F32)
+        for row in range(3):
+            for half in range(2):
+                at = slab * 256 + half * 128
+                par[row : row + 1, at : at + 128] = values[10 + 2 * row + half][None]
 
     def project(first_column, column, a_rows):
         weights = qkv[:, :, pl.ds(first_column + column, FRONT_BLOCK)].reshape(width, FRONT_BLOCK)
@@ -493,7 +498,8 @@
     def normalize(number, carry):
         here = pl.ds(pl.multiple_of(lax.rem(number, per) * FRONT_BLOCK, FRONT_BLOCK), FRONT_BLOCK)
         there = pl.ds(pl.multiple_of(number * FRONT_BLOCK, FRONT_BLOCK), FRONT_BLOCK)
-        value, _, _ = layer_norm(xs[number // per, here].astype(F32), vecs[0:1], vecs[3:4])
+        value, hat, _ = layer_norm(xs[number // per, here].astype(F32), vecs[0:1], vecs[3:4])
+        xs[number // per, here] = hat.astype(BF16)
         low = value.astype(BF16)
         a_all[there] = low
         for column in range(0, width, FRONT_BLOCK):
@@ -513,9 +519,9 @@
             query = (project(0, column, low) + vecs[4:5, columns]).astype(BF16)
             q_all[here, columns] = query * jnp.asarray(head_size ** (-0.5), BF16)
     kept = [
-        pltpu.make_async_copy(one, out, local.at[3 + k])
+        pltpu.make_async_copy(one, out, local.at[2 + k])
         for k, (one, out) in enumerate(
-            ((a_all, a_out), (q_all, q_out), (k_all, k_out), (v_all, v_out))
+            ((a_all, a_out), (q_all, q_out), (k_all, k_out), (v_all, v_out), (xs, xs_out))
         )
     ]
     for one in kept:
@@ -551,10 +557,10 @@
 def plain_front(shards, tokens, starts, scales, heads):
     width = tokens.shape[1]
     fulls = [lax.all_gather(one, "wide", axis=0, tiled=False) for one in shards]
-    each = width // fulls[0].shape[0]
-    vectors = fulls[0][:, :10, :each].transpose(1, 0, 2).reshape(10, width).astype(F32)
+    each, units = width // fulls[0].shape[0], shards[3].shape[1]
+    vectors, par = unpack_small(fulls[0], (10, each), (3, units))
     window = jnp.stack([from_behind(tokens, "wide", 2), from_behind(tokens, "wide", 1), tokens])
-    normed, _, _ = layer_norm(window.reshape(-1, width).astype(F32), vectors[0], vectors[3])
+    normed, hat, _ = layer_norm(window.reshape(-1, width).astype(F32), vectors[0], vectors[3])
     low = normed.astype(BF16)
     weights = fulls[1].reshape(width, 3 * width)
     queries = dot(low[-tokens.shape[0] :], weights[:, :width]) + vectors[4]
@@ -562,7 +568,8 @@
     keys = dot(low, weights[:, width : 2 * width]).astype(BF16)
     values = (dot(low, weights[:, 2 * width :]) + vectors[5]).astype(BF16)
     attended = attend(queries, keys, values, starts, scales, heads)
-    return [*fulls, window, low, queries, keys, values, *attended]
+    hat_low = hat.astype(BF16).reshape(window.shape)
+    return [*fulls[1:], hat_low, low, queries, keys, values, *attended, vectors, par]
 
 
 def front(shards, thirds, tokens, starts, scales, heads):
@@ -572,7 +579,7 @@
         return plain_front(shards, tokens, starts, scales, heads)
     window = 3 * rows
     like = jax.ShapeDtypeStruct
-    out_shape = [like((wide, *one.shape), one.dtype) for one in shards] + [
+    out_shape = [like((wide, *one.shape), one.dtype) for one in shards[1:]] + [
         like((3, rows, width), BF16),
         like((window, width), BF16),
         like((rows, width), BF16),
@@ -581,6 +588,8 @@
         like((rows, width), F32),
         like((rows, width), BF16),
         like((heads // 2, 2, rows), F32),
+        like((16, width), F32),
+        like((8, wide * shards[3].shape[1]), F32),
     ]
     sems = AG_SEMS * len(shards) + 2
     scratch = [
@@ -592,7 +601,6 @@
         ((window, width), BF16),
         ((rows, width), F32),
         ((rows, width), BF16),
-        ((16, width), F32),
         ((wide, *shards[0].shape), BF16),
         ((rows // Q_TILE, window - rows + Q_TILE, Q_TILE), F32),
         ((128, window), BF16),
@@ -602,7 +610,7 @@
         functools.partial(front_kernel, thirds, width // heads),
         out_shape=out_shape,
         in_specs=[VMEM] * 8,
-        out_specs=[HBM] * 12 + [VMEM],
+        out_specs=[HBM] * 11 + [VMEM] * 3,
         scratch_shapes=[pltpu.VMEM(shape, dtype) for shape, dtype in scratch]
         + [
             pltpu.SemaphoreType.DMA((sems,)),
@@ -647,7 +655,9 @@
 RS_SEMS = 12
 
 
-def reduce_ticks(me, wire, base, local, grad, quarter, held, bufs, final, squares, limit):
+def reduce_ticks(
+    me, wire, base, local, grad, quarter, held, bufs, final, squares, waits_for=None, frees=None
+):
     from_core, from_y, from_x, from_down, from_up, from_last = bufs
     count, columns = held.shape[-2:]
     inside = count - quarter
@@ -666,7 +676,13 @@
         put_y = wire.put(other, from_y, base + 1, me.y_mate())
         got_y = wire.got(from_y, base + 1, me.y_mate())
 
+    partners = [(None, one) for one in (me.core_mate(), me.x_mate(), me.y_mate())]
+    partners += [(me.z < 3, me.up()), (me.z > 0, me.down())]
+
     def start():
+        if waits_for is not None:
+            ends = (me.z < 3).astype(jnp.int32) + (me.z > 0).astype(jnp.int32)
+            pl.semaphore_wait(waits_for, 3 + ends)
         take.start()
         put_core()
 
@@ -742,18 +758,20 @@
 
         def square(number, total):
             value = final[pl.ds(pl.multiple_of(number * 8, 8), 8)]
-            power = value * value
-            if limit % 8:
-                place = number * 8 + lax.broadcasted_iota(jnp.int32, power.shape, 0)
-                power = jnp.where(place < limit, power, 0.0)
-            folded = power[:, :128]
-            for lane in range(128, columns, 128):
-                folded = folded + power[:, lane : lane + 128]
-            return total + folded
+            return total + lane_groups(value * value)
 
         squares[...] = squares[...] + lax.fori_loop(
-            0, (limit + 7) // 8, square, jnp.zeros((8, 128), F32)
+            0, count // 8, square, jnp.zeros((8, 128), F32)
         )
+        if frees is not None:
+            wire.finish()
+            for holds, device in partners:
+                when(
+                    holds,
+                    functools.partial(
+                        pl.semaphore_signal, frees, inc=1, device_id=device, device_id_type=MESH
+                    ),
+                )
 
     return [
         start, join_core, *([join_y] if quarter else []), join_x,
@@ -762,91 +780,22 @@
 
 
 def in_rounds(sequences):
-    last = max(k + len(one) for k, one in enumerate(sequences))
+    last = max(start + len(one) for start, one in sequences)
+    order = sorted(sequences, key=lambda item: -item[0])
     rounds = []
     for number in range(last):
         actions = [
-            one[number - k] for k, one in enumerate(sequences) if 0 <= number - k < len(one)
+            one[number - start] for start, one in order if 0 <= number - start < len(one)
         ]
-        rounds.append(functools.partial(act, actions[::-1]))
+        rounds.append(functools.partial(act, actions))
     return rounds
 
 
-def reduce_kernel(pieces, *refs):
-    refs = list(refs)
-    arrays = 1 + max(piece[0] for piece in pieces)
-    results = 1 + max(piece[5] for piece in pieces)
-    count = len(pieces)
-    grads, halo = refs[:arrays], refs[arrays]
-    finals, (back, norm) = refs[arrays + 1 :][:results], refs[arrays + 1 + results :][:2]
-    scratch = refs[arrays + 3 + results :]
-    blank, passing, joined, tiles, send, recv, local = scratch[-7:]
-    me = Place()
-    ending = RS_SEMS * count
-    blank[...] = jnp.zeros_like(blank)
-    tiles[...] = jnp.zeros_like(tiles)
-    clear = [
-        (me.w >= 14, pltpu.make_async_copy(blank, back.at[0], local.at[count])),
-        (me.c == 1, pltpu.make_async_copy(blank, back.at[1], local.at[count + 1])),
-    ]
-    for holds, one in clear:
-        pl.when(holds)(one.start)
-    steps = [me.wide(jnp.bitwise_xor(me.w, bit)) for bit in (1, 2, 4, 8)]
-    wire = Wire(send, recv)
-    far = me.wide(lax.rem(me.w + 14, 16))
-    inner = me.w >= 2
-    joins = both(me.c == 1, inner)
-    load = pltpu.make_async_copy(halo.at[0], joined, local.at[count + 2])
-    firsts = [
-        wire.put(halo.at[0], back.at[0], ending, far, both(me.c == 0, inner)),
-        wire.put(halo.at[1], back.at[1], ending + 1, me.core_mate(), me.c == 1),
-        wire.put(halo.at[1], passing, ending + 2, me.core_mate(), both(me.c == 0, inner)),
-    ]
-    got_passing = wire.got(passing, ending + 2, me.core_mate())
-    put_joined = wire.put(joined, back.at[0], ending, far, joins)
-    got_back = [
-        wire.got(back.at[0], ending, far, me.w < 14),
-        wire.got(back.at[1], ending + 1, me.core_mate(), me.c == 0),
-    ]
-
-    def halo_start():
-        act(firsts)
-        pl.when(joins)(load.start)
-
-    def halo_join():
-        def join():
-            load.wait()
-            got_passing()
-            accumulate(joined, passing)
-
-        pl.when(joins)(join)
-        put_joined()
-
-    sequences = []
-    for k, (number, first, rows, quarter, limit, result, column) in enumerate(pieces):
-        here = pl.ds(first, rows)
-        final = finals[result].at[here, pl.ds(column, grads[number].shape[-1])]
-        sequences.append(
-            reduce_ticks(
-                me, wire, RS_SEMS * k, local.at[k],
-                grads[number].at[:, :, :, here], quarter, scratch[7 * k],
-                scratch[7 * k + 1 : 7 * k + 7], final, tiles.at[0], limit,
-            )
-        )
-    greet(me, steps[2:])
-    nothing = functools.partial(act, [])
-    halo_ticks = [halo_start, halo_join, *[nothing] * 6, functools.partial(act, got_back)]
-    act(in_rounds([sequences[0], halo_ticks, *sequences[1:]]))
-    for k, partner in enumerate(steps):
-        index = ending + 3 + k
-        moved = wire.copy(tiles.at[k], tiles.at[5 + k], index, partner)
-        moved.start()
-        moved.wait()
-        tiles[k + 1] = tiles[k] + tiles[5 + k]
-    norm[...] = tiles[4]
-    wire.finish()
-    for holds, one in clear:
-        pl.when(holds)(one.wait)
+def lane_groups(values):
+    total = values[:, :128]
+    for lane in range(128, values.shape[1], 128):
+        total = total + values[:, lane : lane + 128]
+    return total
 
 
 def piece_buffers(rows, columns, quarter, dtype):
@@ -864,87 +813,359 @@
     return [pltpu.VMEM(shape, dtype) for shape in shapes]
 
 
-def reduce_all(grads, halo, pieces):
+BACK_BLOCK = 256
+DURING_PAIRS = ((0, (0, 1)), (1, (2,)), (2, (3,)), (4, (4,)), (5, (5,)), (7, (6,)))
+DURING_BLOCKS = ((1, (7,)), (3, (8,)))
+AFTER_BLOCKS = 9
+
+
+def back_kernel(pieces, sets, head_size, *refs):
+    grads, refs = refs[:3], refs[3:]
+    (q_in, k_in, v_in, do_in, a_in, hat_in, w_in, starts, lse, delta, small_in), refs = refs[:11], refs[11:]
+    finals, refs = refs[:4], refs[4:]
+    (back_out, own_out, small_out, norm), refs = refs[:4], refs[4:]
+    buffers, refs = refs[: 7 * sets], refs[7 * sets :]
+    (dq, dk, dv, dw, halo, passing, small, tiles, send, recv, local, stream, freed) = refs
+    me = Place()
+    count = len(pieces)
+    rows, width = q_in.shape
+    window = k_in.shape[0]
+    before = window - rows
+    span = before + Q_TILE
+    tiles[...] = jnp.zeros_like(tiles)
+    small[0] = small_in[...]
+    arrays = [*grads, *[dw.at[k] for k in range(3)]]
+    wires, sequences = [], []
+    last_of = {}
+    for k, (number, first, size, quarter, result, column, of, start) in enumerate(pieces):
+        here = pl.ds(first, size)
+        wire = Wire(send, recv)
+        again = of in last_of
+        more = any(piece[6] == of for piece in pieces[k + 1 :])
+        final = finals[result].at[here, pl.ds(column, arrays[number].shape[-1])]
+        sequences.append(
+            (
+                start,
+                reduce_ticks(
+                    me, wire, RS_SEMS * k, local.at[k], arrays[number].at[:, :, :, here], quarter,
+                    buffers[7 * of], buffers[7 * of + 1 : 7 * of + 7], final, tiles.at[0],
+                    waits_for=freed.at[last_of[of]] if again else None,
+                    frees=freed.at[k] if more else None,
+                ),
+            )
+        )
+        last_of[of] = k
+        if not more:
+            wires.append(wire)
+
+    ending = RS_SEMS * count
+    wire = Wire(send, recv)
+    wires.append(wire)
+    far = me.wide(lax.rem(me.w + 14, 16))
+    inner = me.w >= 2
+    joins = both(me.c == 1, inner)
+    near = [
+        wire.put(halo.at[1], back_out.at[1], ending + 1, me.core_mate(), me.c == 1),
+        wire.put(halo.at[1], passing, ending + 2, me.core_mate(), both(me.c == 0, inner)),
+    ]
+    got_passing = wire.got(passing, ending + 2, me.core_mate())
+    put_far = wire.put(halo.at[0], back_out.at[0], ending, far, inner)
+    got_back = [
+        wire.got(back_out.at[0], ending, far, me.w < 14),
+        wire.got(back_out.at[1], ending + 1, me.core_mate(), me.c == 0),
+    ]
+
+    def join_halo():
+        got_passing()
+        accumulate(halo.at[0], passing)
+
+    def small_step(k, partner):
+        put = wire.put(small.at[k], small.at[5 + k], ending + 3 + k, partner)
+        got = wire.got(small.at[5 + k], ending + 3 + k, partner)
+
+        def take_in():
+            got()
+            small[k + 1] = small[k] + small[5 + k]
+
+        return put, take_in
+
+    steps = [me.wide(jnp.bitwise_xor(me.w, bit)) for bit in (1, 2, 4, 8)]
+    smalls = [small_step(k, one) for k, one in enumerate([steps[0], me.y_mate(), *steps[1:]])]
+    small_ticks = [smalls[0][0]]
+    for k in range(4):
+        small_ticks.append(functools.partial(act, [smalls[k][1], smalls[k + 1][0]]))
+    small_ticks.append(smalls[4][1])
+    last_start = pieces[-1][-1]
+    computed = pieces[-3][-1]
+    sequences.append((computed, small_ticks))
+    sequences.append(
+        (computed, [functools.partial(act, near), functools.partial(when, joins, join_halo)])
+    )
+    sequences.append((last_start + 3, [put_far]))
+    rounds = in_rounds(sequences)
+    pairs = width // 128
+    blocks = width // BACK_BLOCK
+    greet(me, steps[2:])
+
+    def attention(q_two, k_two, v_two, do_two, bias, dk_sum, dv_sum, kt, dqt):
+        def loads(pair, slot):
+            lanes = pl.ds(pl.multiple_of(pair * 128, 128), 128)
+            return [
+                pltpu.make_async_copy(source.at[:, lanes], target.at[slot], stream.at[slot, k])
+                for k, (source, target) in enumerate(
+                    ((q_in, q_two), (k_in, k_two), (v_in, v_two), (do_in, do_two))
+                )
+            ]
+
+        for one in loads(0, 0):
+            one.start()
+        fill_mask(starts, bias, rows, span, before)
+
+        def pair_step(pair, carry):
+            slot = lax.rem(pair, 2)
+            lanes = pl.ds(pl.multiple_of(pair * 128, 128), 128)
+
+            def prefetch():
+                for one in loads(pair + 1, 1 - slot):
+                    one.start()
+
+            pl.when(pair + 1 < pairs)(prefetch)
+            for k, due in DURING_PAIRS:
+                pl.when(pair == k)(functools.partial(act, [rounds[number] for number in due]))
+            for one in loads(pair, slot):
+                one.wait()
+            attend_back_pair(
+                head_size, q_two.at[slot], k_two.at[slot], v_two.at[slot], do_two.at[slot],
+                lse.at[pair], delta.at[pair], dq.at[:, lanes], dk.at[:, lanes], dv.at[:, lanes],
+                bias, dk_sum, dv_sum, kt, dqt,
+            )
+            small[0, 4:5, lanes] = jnp.sum(dq[:, lanes].astype(F32), axis=0, keepdims=True)
+            small[0, 5:6, lanes] = jnp.sum(dv[:, lanes].astype(F32), axis=0, keepdims=True)
+            return carry
+
+        lax.fori_loop(0, pairs, pair_step, 0)
+
+    pl.run_scoped(
+        attention,
+        pltpu.VMEM((2, rows, 128), BF16),
+        pltpu.VMEM((2, window, 128), BF16),
+        pltpu.VMEM((2, window, 128), BF16),
+        pltpu.VMEM((2, rows, 128), BF16),
+        pltpu.VMEM((rows // Q_TILE, span, Q_TILE), F32),
+        pltpu.VMEM((window, 128), F32),
+        pltpu.VMEM((window, 128), F32),
+        pltpu.VMEM((128, window), BF16),
+        pltpu.VMEM((128, rows), F32),
+    )
+
+    def projections(a_two, hat_two, w_two):
+        def loads(block, slot):
+            here = pl.ds(pl.multiple_of(block * BACK_BLOCK, BACK_BLOCK), BACK_BLOCK)
+            return [
+                pltpu.make_async_copy(source, target.at[slot], stream.at[slot, k])
+                for k, (source, target) in enumerate(
+                    ((a_in.at[:, here], a_two), (hat_in.at[:, here], hat_two), (w_in.at[here], w_two))
+                )
+            ]
+
+        for one in loads(0, 0):
+            one.start()
+
+        def block_step(block, carry):
+            slot = lax.rem(block, 2)
+            here = pl.ds(pl.multiple_of(block * BACK_BLOCK, BACK_BLOCK), BACK_BLOCK)
+
+            def prefetch():
+                for one in loads(block + 1, 1 - slot):
+                    one.start()
+
+            pl.when(block + 1 < blocks)(prefetch)
+            for k, due in DURING_BLOCKS:
+                pl.when(block == k)(functools.partial(act, [rounds[number] for number in due]))
+            for one in loads(block, slot):
+                one.wait()
+            a_t = a_two[slot].T
+            for k, made in enumerate((dot(a_t[:, before:], dq[...]), dot(a_t, dk[...]), dot(a_t, dv[...]))):
+                dw[k, block] = made.astype(BF16).reshape(dw.shape[2:])
+            for k in range(3):
+                part = slice(k * rows, (k + 1) * rows)
+                grad = dot(dk[part, :], w_two[slot, :, width : 2 * width], 1, 1) + dot(
+                    dv[part, :], w_two[slot, :, 2 * width :], 1, 1
+                )
+                if k == 2:
+                    grad = grad + dot(dq[...], w_two[slot, :, :width], 1, 1)
+                    own_out[:, here] = grad
+                else:
+                    halo[k, :, here] = grad.astype(BF16)
+                hat = hat_two[slot, part].astype(F32)
+                small[0, 0:1, here] += jnp.sum(grad * hat, axis=0, keepdims=True)
+                small[0, 3:4, here] += jnp.sum(grad, axis=0, keepdims=True)
+            return carry
+
+        lax.fori_loop(0, blocks, block_step, 0)
+
+    pl.run_scoped(
+        projections,
+        pltpu.VMEM((2, window, BACK_BLOCK), BF16),
+        pltpu.VMEM((2, window, BACK_BLOCK), BF16),
+        pltpu.VMEM((2, BACK_BLOCK, 3 * width), BF16),
+    )
+    dq[...] = jnp.zeros_like(dq)
+    clear = [
+        (me.w >= 14, pltpu.make_async_copy(dq, back_out.at[0], local.at[count])),
+        (me.c == 1, pltpu.make_async_copy(dq, back_out.at[1], local.at[count + 1])),
+    ]
+    for holds, one in clear:
+        when(holds, one.start)
+    act(rounds[AFTER_BLOCKS:])
+    small_out[...] = small[5]
+    for k, partner in enumerate(steps):
+        moved = wire.copy(tiles.at[k], tiles.at[5 + k], ending + 8 + k, partner)
+        moved.start()
+        moved.wait()
+        tiles[k + 1] = tiles[k] + tiles[5 + k]
+    norm[...] = tiles[4]
+    act(got_back)
+    for one in wires:
+        one.finish()
+    for holds, one in clear:
+        when(holds, one.wait)
+
+
+def back(grads, attention, small, starts, stats, heads):
+    queries, keys, values, outs_grad, normed, hat, weights = attention
+    rows, width = queries.shape
+    window = keys.shape[0]
     wide = lax.axis_size("wide")
-    if lax.axis_size("dp") == 2 and wide == 16:
-        count = len(pieces)
-        tokens = halo.shape[1:]
-        sizes = {}
-        for number, _, _, _, _, result, column in pieces:
-            _, rows, columns = grads[number].shape
-            sizes[result] = (rows, max(column + columns, sizes.get(result, (0, 0))[1]))
-        out_shape = [jax.ShapeDtypeStruct(sizes[k], F32) for k in range(len(sizes))]
-        out_shape.append(jax.ShapeDtypeStruct(halo.shape, halo.dtype))
-        out_shape.append(jax.ShapeDtypeStruct((8, 128), F32))
-        scratch = []
-        for number, _, rows, quarter, *_ in pieces:
-            one = grads[number]
-            scratch += piece_buffers(rows, one.shape[2], quarter, one.dtype)
-        sems = RS_SEMS * count + 7
-        return pl.pallas_call(
-            functools.partial(reduce_kernel, pieces),
-            out_shape=out_shape,
-            in_specs=[HBM] * (len(grads) + 1),
-            out_specs=[VMEM] * len(sizes) + [HBM, VMEM],
-            scratch_shapes=scratch
-            + [
-                pltpu.VMEM(tokens, BF16),
-                pltpu.VMEM(tokens, BF16),
-                pltpu.VMEM(tokens, BF16),
-                pltpu.VMEM((9, 8, 128), F32),
-                pltpu.SemaphoreType.DMA((sems,)),
-                pltpu.SemaphoreType.DMA((sems,)),
-                pltpu.SemaphoreType.DMA((count + 3,)),
-            ],
-            compiler_params=pltpu.CompilerParams(
-                collective_id=1, has_side_effects=True, vmem_limit_bytes=60 << 20
-            ),
-            name="reduce_all",
-        )(*[one.reshape(4, 2, 2, *one.shape[1:]) for one in grads], halo)
-    whole = [
+    if lax.axis_size("dp") != 2 or wide != 16:
+        return plain_back(grads, attention, small, starts, stats, heads)
+    fc1, fc2, out = (one.shape for one in grads)
+    tall, pieces = 4, []
+    for array, shape in ((1, fc2), (0, fc1)):
+        size = shape[1] // tall
+        for k in range(tall):
+            quarter = plane_share(size) if array == 0 else size // 4
+            pieces.append((array, k * size, size, quarter, array, 0, len(pieces), len(pieces)))
+    each = width // wide
+    pieces.append((2, 0, each, each // 4, 2, 0, 0, 8))
+    for k in range(3):
+        pieces.append((3 + k, 0, each, each // 4, 3, k * width, 1 + k, AFTER_BLOCKS + k))
+    pieces = tuple(pieces)
+    sets = 2 * tall
+    like = jax.ShapeDtypeStruct
+    out_shape = [like(one.shape[1:], F32) for one in grads] + [
+        like((each, 3 * width), F32),
+        like((2, rows, width), BF16),
+        like((rows, width), F32),
+        like(small.shape, F32),
+        like((8, 128), F32),
+    ]
+    scratch = []
+    for number, _, size, quarter, *_ in pieces[:sets]:
+        scratch += piece_buffers(size, grads[number].shape[2], quarter, grads[number].dtype)
+    count = len(pieces)
+    sems = RS_SEMS * count + 12
+    return pl.pallas_call(
+        functools.partial(back_kernel, pieces, sets, width // heads),
+        out_shape=out_shape,
+        in_specs=[HBM] * 10 + [VMEM] * 4,
+        out_specs=[VMEM] * 4 + [HBM] + [VMEM] * 3,
+        scratch_shapes=scratch
+        + [
+            pltpu.VMEM((rows, width), BF16),
+            pltpu.VMEM((window, width), BF16),
+            pltpu.VMEM((window, width), BF16),
+            pltpu.VMEM((3, 4, 2, 2, each, width), BF16),
+            pltpu.VMEM((2, rows, width), BF16),
+            pltpu.VMEM((rows, width), BF16),
+            pltpu.VMEM((10, *small.shape), F32),
+            pltpu.VMEM((9, 8, 128), F32),
+            pltpu.SemaphoreType.DMA((sems,)),
+            pltpu.SemaphoreType.DMA((sems,)),
+            pltpu.SemaphoreType.DMA((count + 2,)),
+            pltpu.SemaphoreType.DMA((2, 4)),
+            pltpu.SemaphoreType.REGULAR((count,)),
+        ],
+        compiler_params=pltpu.CompilerParams(
+            collective_id=1, has_side_effects=True, vmem_limit_bytes=60 << 20
+        ),
+        name="back",
+    )(
+        *[one.reshape(4, 2, 2, *one.shape[1:]) for one in grads],
+        queries, keys, values, outs_grad, normed, hat, weights, starts, *stats, small,
+    )
+
+
+def plain_back(grads, attention, small, starts, stats, heads):
+    queries, keys, values, outs_grad, normed, hat, weights = attention
+    rows, width = queries.shape
+    wide = lax.axis_size("wide")
+    dq, dk, dv = attend_back(queries, keys, values, outs_grad, *stats, starts, heads)
+    earlier = dot(dk, weights[:, width : 2 * width], 1, 1) + dot(dv, weights[:, 2 * width :], 1, 1)
+    own = earlier[-rows:] + dot(dq, weights[:, :width], 1, 1)
+    earlier = earlier[:-rows]
+    all_grad = jnp.concatenate([earlier, own])
+    dw = [dot(normed[-rows:], dq, 0, 0), dot(normed, dk, 0, 0), dot(normed, dv, 0, 0)]
+    grads = [*grads, jnp.concatenate(dw, axis=1).reshape(wide, -1, 3 * width)]
+    totals = [
         lax.psum(
             lax.psum_scatter(one.astype(F32), "wide", scatter_dimension=0, tiled=False), "dp"
         )
         for one in grads
     ]
-    totals = []
-    for result in range(1 + max(piece[5] for piece in pieces)):
-        columns = {piece[6]: whole[piece[0]] for piece in pieces if piece[5] == result}
-        totals.append(jnp.concatenate([columns[key] for key in sorted(columns)], axis=1))
-    back = jnp.stack([from_behind(halo[0], "wide", -2), from_behind(halo[1], "wide", -1)])
-    squares = jnp.float32(0.0)
-    for number, first, _, _, limit, *_ in pieces:
-        part = whole[number][first : first + limit]
-        squares = squares + jnp.sum(part * part)
-    norm = jnp.zeros((8, 128), F32).at[0, 0].set(lax.psum(squares, "wide"))
-    return [*totals, back, norm]
+    sums = {
+        0: jnp.sum(all_grad * hat.astype(F32), axis=0),
+        3: jnp.sum(all_grad, axis=0),
+        4: jnp.sum(dq.astype(F32), axis=0),
+        5: jnp.sum(dv.astype(F32), axis=0),
+    }
+    small = jnp.concatenate(
+        [sums[k][None] if k in sums else small[k : k + 1] for k in range(small.shape[0])]
+    )
+    low = earlier.astype(BF16).reshape(2, rows, width)
+    returned = jnp.stack([from_behind(low[0], "wide", -2), from_behind(low[1], "wide", -1)])
+    squares = lax.psum(sum(jnp.sum(one * one) for one in totals), "wide")
+    tile = jnp.zeros((8, 128), F32).at[0, 0].set(squares)
+    return [*totals, returned, own, lax.psum(small, ("dp", "wide")), tile]
 
 
 F_TILE = 256
 
 
-def lane_sums(values):
-    total = values[:, :128]
-    for lane in range(128, values.shape[1], 128):
-        total = total + values[:, lane : lane + 128]
-    return total
-
-
-def ffn_kernel(
-    a_ref, x_ref, gy_ref, w1_ref, w2_ref, par_ref, bias_ref,
-    out_ref, mid_ref, df_ref, da_ref, sums_ref,
-    act, slope, grad, stats,
+def grad_through_norm(grad, hat, scale, gain):
+    scaled = grad * gain
+    mean_plain = jnp.mean(scaled, axis=-1, keepdims=True)
+    mean_cross = jnp.mean(scaled * hat, axis=-1, keepdims=True)
+    return scale * (scaled - mean_plain - hat * mean_cross)
+
+
+def down_sums(values):
+    return jnp.sum(values, axis=0, keepdims=True)
+
+
+def middle_kernel(
+    head_size, c_ref, o_ref, x_ref, gy_ref, wo_ref, w1_ref, w2_ref, vec_ref, par_ref, scale_ref,
+    out_ref, mid_ref, df_ref, a_ref, dz_ref, res_ref, do_ref, delta_ref, small_ref,
+    act_all, slope, grad_all, stats, sums, x2, hat_post, hat_two, da,
 ):
     blocks, _, units = w1_ref.shape
-    tile = a_ref.shape[0]
+    width = x_ref.shape[1]
     count = blocks * units
-    first_step = pl.program_id(0) == 0
-
-    @pl.when(first_step)
+
+    @pl.when(pl.program_id(0) == 0)
     def _():
-        sums_ref[...] = jnp.zeros_like(sums_ref)
+        sums[...] = jnp.zeros_like(sums)
+        small_ref[...] = jnp.zeros_like(small_ref)
 
     stats[...] = jnp.zeros_like(stats)
+    projected = dot(c_ref[...], wo_ref[...]) + vec_ref[6:7]
+    value, hat, scale_post = layer_norm(projected, vec_ref[1:2], vec_ref[7:8])
+    hat_post[...] = hat
+    residual = x_ref[...].astype(F32) + value
+    x2[...] = residual
+    value, hat, scale_two = layer_norm(residual, vec_ref[2:3], vec_ref[8:9])
+    hat_two[...] = hat
+    a_ref[...] = value.astype(BF16)
 
     def columns(k):
         return pl.ds(pl.multiple_of(k * units, units), units)
@@ -953,10 +1174,10 @@
         pre = dot(a_ref[...], w1_ref[k]) + par_ref[2:3, columns(k)]
         half = 0.5 + 0.5 * lax.erf(pre * (0.5**0.5))
         value = pre * half
-        act[k] = value
+        act_all[k] = value
         slope[k] = half + pre * (jnp.exp(-0.5 * pre * pre) * (0.5 / jnp.pi) ** 0.5)
-        stats[0] += lane_sums(value)
-        stats[1] += lane_sums(value * value)
+        stats[0] += lane_groups(value)
+        stats[1] += lane_groups(value * value)
         return carry
 
     lax.fori_loop(0, blocks, forward, 0, unroll=2)
@@ -966,131 +1187,162 @@
 
     def middle(k, carry):
         here = columns(k)
-        hat = (act[k] - mean) * scale
+        hat = (act_all[k] - mean) * scale
         mid_ref[:, here] = (hat * par_ref[0:1, here] + par_ref[1:2, here]).astype(BF16)
         down = dot(gy_ref[...], w2_ref[here, :], 1, 1)
         scaled = down * par_ref[0:1, here]
-        cross = scaled * hat
-        act[k] = hat
-        grad[k] = scaled
-        stats[2] += lane_sums(scaled)
-        stats[3] += lane_sums(cross)
-        sums_ref[0:1, here] += jnp.sum(down * hat, axis=0, keepdims=True)
-        sums_ref[1:2, here] += jnp.sum(down, axis=0, keepdims=True)
+        act_all[k] = hat
+        grad_all[k] = scaled
+        stats[2] += lane_groups(scaled)
+        stats[3] += lane_groups(scaled * hat)
+        sums[0:1, here] += down_sums(down * hat)
+        sums[1:2, here] += down_sums(down)
         return carry
 
     lax.fori_loop(0, blocks, middle, 0, unroll=2)
     plain = jnp.sum(stats[2], axis=1, keepdims=True) / count
     crossed = jnp.sum(stats[3], axis=1, keepdims=True) / count
-    width = out_ref.shape[1]
     part = min(width, 512)
     for start in range(0, width, part):
         here = slice(start, start + part)
         total = dot(mid_ref[...], w2_ref[:, here])
-        out_ref[:, here] = (x_ref[:, here] + (total + bias_ref[:, here])).astype(BF16)
+        out_ref[:, here] = (x2[:, here] + (total + vec_ref[9:10, here])).astype(BF16)
 
     def backward(k, carry):
         here = columns(k)
-        back = scale * (grad[k] - plain - act[k] * crossed) * slope[k]
+        back = scale * (grad_all[k] - plain - act_all[k] * crossed) * slope[k]
         low = back.astype(BF16)
         df_ref[:, here] = low
-        sums_ref[2:3, here] += jnp.sum(low.astype(F32), axis=0, keepdims=True)
+        sums[2:3, here] += down_sums(low.astype(F32))
         return carry
 
     lax.fori_loop(0, blocks, backward, 0, unroll=2)
-    da_ref[...] = jnp.zeros_like(da_ref)
+    da[...] = jnp.zeros_like(da)
 
     def back_out(k, carry):
-        da_ref[...] += dot(df_ref[:, columns(k)], w1_ref[k], 1, 1)
+        da[...] += dot(df_ref[:, columns(k)], w1_ref[k], 1, 1)
         return carry
 
     lax.fori_loop(0, blocks, back_out, 0, unroll=2)
-
-
-def ffn(rows, residual, out_grad, w1, w2, par, bias):
-    tokens, width = rows.shape
+    grad_in = gy_ref[...].astype(F32)
+    rows_grad = da[...]
+    residual_grad = grad_in + grad_through_norm(rows_grad, hat_two[...], scale_two, vec_ref[2:3])
+    res_ref[...] = residual_grad
+    dz = grad_through_norm(residual_grad, hat_post[...], scale_post, vec_ref[1:2]).astype(BF16)
+    dz_ref[...] = dz
+    for row, term in (
+        (1, residual_grad * hat_post[...]),
+        (2, rows_grad * hat_two[...]),
+        (6, dz.astype(F32)),
+        (7, residual_grad),
+        (8, rows_grad),
+        (9, grad_in),
+    ):
+        small_ref[row : row + 1] += down_sums(term)
+    mixed_grad = dot(dz, wo_ref[...], 1, 1)
+    outs = o_ref[...]
+    low = (mixed_grad * scale_ref[...]).astype(BF16)
+    do_ref[...] = low
+    head_row = 10 + 3 * count // width
+    small_ref[head_row : head_row + 1] += down_sums(mixed_grad * outs)
+    heads = delta_ref.shape[0]
+    lane = lax.broadcasted_iota(jnp.int32, (heads, width), 1)
+    of = lax.broadcasted_iota(jnp.int32, (heads, width), 0) * head_size
+    chosen = jnp.where(jnp.logical_and(lane >= of, lane < of + head_size), 1.0, 0.0)
+    delta_ref[...] = lax.dot_general(
+        chosen, low.astype(F32) * outs, (((1,), (1,)), ((), ())),
+        precision=lax.Precision.HIGHEST, preferred_element_type=F32,
+    )
+
+    @pl.when(pl.program_id(0) == pl.num_programs(0) - 1)
+    def _():
+        for row in range(3):
+            for start in range(0, count, width):
+                at = 10 + (row * count + start) // width
+                small_ref[at : at + 1] = sums[row : row + 1, start : start + width]
+
+
+def middle_part(mixed, attended, tokens, out_grad, wo, w1, w2, vectors, par, scales, heads):
+    rows, width = tokens.shape
     blocks, _, units = w1.shape
     hidden = blocks * units
     by_tile = lambda columns: pl.BlockSpec((F_TILE, columns), lambda t: (t, 0))
-    once = pl.Buffered(1)
+    once = lambda one: pl.BlockSpec(
+        one.shape, lambda t: (0,) * len(one.shape), pipeline_mode=pl.Buffered(1)
+    )
+    small_rows = -(-(11 + 3 * hidden // width) // 8) * 8
+    like = jax.ShapeDtypeStruct
     return pl.pallas_call(
-        ffn_kernel,
-        grid=(tokens // F_TILE,),
-        in_specs=[
-            by_tile(width),
-            by_tile(width),
-            by_tile(width),
-            pl.BlockSpec(w1.shape, lambda t: (0, 0, 0), pipeline_mode=once),
-            pl.BlockSpec(w2.shape, lambda t: (0, 0), pipeline_mode=once),
-            pl.BlockSpec(par.shape, lambda t: (0, 0)),
-            pl.BlockSpec(bias.shape, lambda t: (0, 0)),
-        ],
+        functools.partial(middle_kernel, width // heads),
+        grid=(rows // F_TILE,),
+        in_specs=[by_tile(width)] * 4 + [once(one) for one in (wo, w1, w2, vectors, par, scales)],
         out_specs=[
             by_tile(width),
             by_tile(hidden),
             by_tile(hidden),
             by_tile(width),
-            pl.BlockSpec(par.shape, lambda t: (0, 0)),
+            by_tile(width),
+            by_tile(width),
+            by_tile(width),
+            pl.BlockSpec((heads, F_TILE), lambda t: (0, t)),
+            pl.BlockSpec((small_rows, width), lambda t: (0, 0)),
         ],
         out_shape=[
-            jax.ShapeDtypeStruct((tokens, width), BF16),
-            jax.ShapeDtypeStruct((tokens, hidden), BF16),
-            jax.ShapeDtypeStruct((tokens, hidden), BF16),
-            jax.ShapeDtypeStruct((tokens, width), F32),
-            jax.ShapeDtypeStruct(par.shape, F32),
+            like((rows, width), BF16),
+            like((rows, hidden), BF16),
+            like((rows, hidden), BF16),
+            like((rows, width), BF16),
+            like((rows, width), BF16),
+            like((rows, width), F32),
+            like((rows, width), BF16),
+            like((heads, rows), F32),
+            like((small_rows, width), F32),
         ],
         scratch_shapes=[pltpu.VMEM((blocks, F_TILE, units), F32)] * 3
-        + [pltpu.VMEM((4, F_TILE, 128), F32)],
+        + [pltpu.VMEM((4, F_TILE, 128), F32), pltpu.VMEM((8, hidden), F32)]
+        + [pltpu.VMEM((F_TILE, width), F32)] * 4,
         compiler_params=pltpu.CompilerParams(vmem_limit_bytes=60 << 20),
-        name="ffn",
-    )(rows, residual, out_grad, w1, w2, par, bias)
-
-
-def ffn_weights_kernel(a_ref, gy_ref, mid_ref, df_ref, dw1_ref, dw2_ref, a_t):
+        name="middle_part",
+    )(mixed, attended, tokens, out_grad, wo, w1, w2, vectors, par, scales)
+
+
+def weights_kernel(a_ref, gy_ref, c_ref, dz_ref, mid_ref, df_ref, dw1_ref, dw2_ref, dwo_ref, a_t):
     @pl.when(pl.program_id(0) == 0)
     def _():
         a_t[...] = a_ref[...].T
+        dwo_ref[...] = dot(c_ref[...].T, dz_ref[...]).astype(BF16)
 
     dw1_ref[0] = dot(a_t[...], df_ref[...]).astype(BF16)
     dw2_ref[0] = dot(mid_ref[...].T, gy_ref[...]).astype(BF16)
 
 
-def ffn_weights(rows, out_grad, middle, pre_grad, blocks):
+def weight_grads(rows, out_grad, mixed, proj_grad, middle, pre_grad, blocks):
     tokens, width = rows.shape
     units = middle.shape[1] // blocks
     whole = pl.BlockSpec((tokens, width), lambda k: (0, 0))
     block = pl.BlockSpec((tokens, units), lambda k: (0, k))
     return pl.pallas_call(
-        ffn_weights_kernel,
+        weights_kernel,
         grid=(blocks,),
-        in_specs=[whole, whole, block, block],
+        in_specs=[whole] * 4 + [block, block],
         out_specs=[
             pl.BlockSpec((1, width, units), lambda k: (k, 0, 0)),
             pl.BlockSpec((1, units, width), lambda k: (k, 0, 0)),
+            pl.BlockSpec((width, width), lambda k: (0, 0)),
         ],
         out_shape=[
             jax.ShapeDtypeStruct((blocks, width, units), BF16),
             jax.ShapeDtypeStruct((blocks, units, width), BF16),
+            jax.ShapeDtypeStruct((width, width), BF16),
         ],
         scratch_shapes=[pltpu.VMEM((width, tokens), BF16)],
         compiler_params=pltpu.CompilerParams(vmem_limit_bytes=40 << 20),
-        name="ffn_weights",
-    )(rows, out_grad, middle, pre_grad)
+        name="weight_grads",
+    )(rows, out_grad, mixed, proj_grad, middle, pre_grad)
 
 
 def plane_share(rows):
     return rows // 16 * 3 // 8 * 16
-
-
-def pack(parts):
-    flat = jnp.concatenate(parts, axis=1)
-    size = -(-flat.shape[1] // 2048) * 2048
-    return jnp.pad(flat, ((0, 0), (0, size - flat.shape[1]))).reshape(flat.shape[0], -1, 128)
-
-
-def to_slabs(rows, wide):
-    count, columns = rows.shape
-    return rows.reshape(count, wide, -1).transpose(1, 0, 2).reshape(wide, -1)
 
 
 def unpack_small(full, vector_shape, hidden_shape):
@@ -1159,7 +1411,6 @@
     head_size = width // heads_count
     wide = lax.axis_size("wide")
     hidden_width = hidden_vectors.shape[1] * wide
-    vector_size, hidden_size = model_vectors.size, hidden_vectors.size
 
     fc1_rows, fc2_rows = fc1_weight.shape[0], fc2_weight.shape[0]
     qkv_rows, out_rows = qkv_weight.shape[0], out_weight.shape[0]
@@ -1193,121 +1444,64 @@
         scales,
         heads_count,
     )
-    small_full, qkv_full, out_full, fc1_full, fc2_full, tokens_all, normed_low = gathered[:7]
-    queries, keys_all, values_all, attended, mixed_low, log_totals = gathered[7:]
-    vectors, hidden_par = unpack_small(small_full, model_vectors.shape, hidden_vectors.shape)
-    qkv_full = qkv_full.reshape(width, 3 * width)
-    out_full = out_full.reshape(width, width)
+    qkv_full, out_full, fc1_full, fc2_full, hat_low, normed_low = gathered[:6]
+    queries, keys_all, values_all, attended, mixed_low, log_totals, vectors, hidden_par = gathered[6:]
     fc2_full = fc2_full.reshape(hidden_width, width)
-
-    own = slice(2 * tokens_dev, None)
-    tokens_in = inputs.astype(F32)
-    _, hat_in, scale_in = layer_norm(
-        tokens_all.reshape(-1, width).astype(F32), vectors[0], vectors[3]
-    )
-    proj_out = jnp.dot(mixed_low, out_full, preferred_element_type=F32) + vectors[6]
-    normed_post, hat_post, scale_post = layer_norm(proj_out, vectors[1], vectors[7])
-    residual = tokens_in + normed_post
-    normed_two, hat_two, scale_two = layer_norm(residual, vectors[2], vectors[8])
-    rows_low = normed_two.astype(BF16)
-    grad_in = out_grad.astype(F32)
-
-    output, middle_low, pre_low, rows_grad, hidden_grad = ffn(
-        rows_low, residual, out_grad, regroup(fc1_full, 256), fc2_full, hidden_par, vectors[9:10]
-    )
-    fc1_grad, fc2_grad = ffn_weights(rows_low, out_grad, middle_low, pre_low, hidden_width // 256)
-    out_bias_total = jnp.sum(grad_in, axis=0)
-    residual_grad = grad_in + norm_back(rows_grad, hat_two, scale_two, vectors[2])
-    gain_two_grad = jnp.sum(rows_grad * hat_two, axis=0)
-    bias_two_grad = jnp.sum(rows_grad, axis=0)
-    gain_post_grad = jnp.sum(residual_grad * hat_post, axis=0)
-    bias_post_grad = jnp.sum(residual_grad, axis=0)
-    proj_low = norm_back(residual_grad, hat_post, scale_post, vectors[1]).astype(BF16)
-    proj_bias_grad = jnp.sum(proj_low.astype(F32), axis=0)
-    out_weight_grad = jnp.einsum("td,te->de", mixed_low, proj_low, preferred_element_type=F32)
-    mixed_grad = jnp.einsum("te,de->td", proj_low, out_full, preferred_element_type=F32)
-    head_grad = jnp.sum((mixed_grad * attended).reshape(tokens_dev, heads_count, -1), axis=(0, 2))
-    attended_low = (mixed_grad * scales).astype(BF16)
-    delta = (
-        jnp.sum((attended_low.astype(F32) * attended).reshape(tokens_dev, heads_count, -1), axis=-1)
-        .transpose(1, 0)
-        .reshape(heads_count // 2, 2, tokens_dev)
-    )
-    query_grad, key_grad, value_grad = attend_back(
-        queries, keys_all, values_all, attended_low, log_totals, delta, starts, heads_count
-    )
-    query_bias_grad = jnp.sum(query_grad.astype(F32), axis=0)
-    value_bias_grad = jnp.sum(value_grad.astype(F32), axis=0)
-    query_part = jnp.einsum("td,te->de", normed_low[own], query_grad, preferred_element_type=F32)
-    key_part = jnp.einsum("td,te->de", normed_low, key_grad, preferred_element_type=F32)
-    value_part = jnp.einsum("td,te->de", normed_low, value_grad, preferred_element_type=F32)
-    normed_grad = jnp.einsum(
-        "te,de->td", key_grad, qkv_full[:, width : 2 * width], preferred_element_type=F32
-    ) + jnp.einsum("te,de->td", value_grad, qkv_full[:, 2 * width :], preferred_element_type=F32)
-    halo_grad = normed_grad[: 2 * tokens_dev]
-    own_grad = normed_grad[own] + jnp.einsum(
-        "te,de->td", query_grad, qkv_full[:, :width], preferred_element_type=F32
-    )
-    gain_in_grad = jnp.sum(halo_grad * hat_in[: 2 * tokens_dev], axis=0) + jnp.sum(
-        own_grad * hat_in[own], axis=0
-    )
-    bias_in_grad = jnp.sum(halo_grad, axis=0) + jnp.sum(own_grad, axis=0)
-    vector_grad = jnp.stack(
+    output, middle_low, pre_low, rows_low, proj_low, residual_grad, attended_low, delta, small_grad = (
+        middle_part(
+            mixed_low,
+            attended,
+            inputs,
+            out_grad,
+            out_full.reshape(width, width),
+            regroup(fc1_full, 256),
+            fc2_full,
+            vectors,
+            hidden_par,
+            scales,
+            heads_count,
+        )
+    )
+    fc1_grad, fc2_grad, out_weight_grad = weight_grads(
+        rows_low, out_grad, mixed_low, proj_low, middle_low, pre_low, hidden_width // 256
+    )
+    fc1_part, fc2_part, out_part, qkv_part, halo_back, own_grad, small_total, norm_tile = back(
         [
-            gain_in_grad,
-            gain_post_grad,
-            gain_two_grad,
-            bias_in_grad,
-            query_bias_grad,
-            value_bias_grad,
-            proj_bias_grad,
-            bias_post_grad,
-            bias_two_grad,
-            out_bias_total,
-        ]
-    )
-    small_grad = pack(
-        [
-            to_slabs(vector_grad, wide),
-            to_slabs(hidden_grad, wide),
-            jnp.broadcast_to(head_grad[None], (wide, heads_count)),
-        ]
-    )
-    counted = (vector_size + hidden_size) // 128
-    small_part, qkv_part, out_part, fc1_part, fc2_part, halo_back, norm_tile = reduce_all(
-        [
-            small_grad,
-            query_part.astype(BF16).reshape(wide, -1, width),
-            key_part.astype(BF16).reshape(wide, -1, width),
-            value_part.astype(BF16).reshape(wide, -1, width),
-            out_weight_grad.astype(BF16).reshape(wide, -1, width),
             ungroup(fc1_grad, fc1_weight.shape[1]),
             fc2_grad.reshape(wide, -1, width),
+            out_weight_grad.reshape(wide, -1, width),
         ],
-        halo_grad.astype(BF16).reshape(2, tokens_dev, width),
-        tuple(
-            (6, k * (fc2_rows // 4), fc2_rows // 4, fc2_rows // 16, fc2_rows // 4, 4, 0)
-            for k in range(4)
-        )
-        + tuple(
-            (5, k * (fc1_rows // 4), fc1_rows // 4, plane_share(fc1_rows // 4), fc1_rows // 4, 3, 0)
-            for k in range(4)
-        )
-        + (
-            (4, 0, out_rows, out_rows // 4, out_rows, 2, 0),
-            (0, 0, small_grad.shape[1], 0, counted, 0, 0),
-            (1, 0, qkv_rows, qkv_rows // 4, qkv_rows, 1, 0),
-            (2, 0, qkv_rows, qkv_rows // 4, qkv_rows, 1, width),
-            (3, 0, qkv_rows, qkv_rows // 4, qkv_rows, 1, 2 * width),
+        (
+            queries,
+            keys_all,
+            values_all,
+            attended_low,
+            normed_low,
+            hat_low.reshape(-1, width),
+            qkv_full.reshape(width, 3 * width),
         ),
+        small_grad,
+        starts,
+        (log_totals, delta.reshape(log_totals.shape)),
+        heads_count,
     )
     total_grad = own_grad + halo_back[0].astype(F32) + halo_back[1].astype(F32)
-    input_grad = residual_grad + norm_back(total_grad, hat_in[own], scale_in[own], vectors[0])
-    flat = small_part.reshape(-1)
-    vector_part = flat[:vector_size].reshape(model_vectors.shape)
-    hidden_part = flat[vector_size : vector_size + hidden_size].reshape(hidden_vectors.shape)
-    head_total = flat[vector_size + hidden_size :][:heads_count]
-    grad_norm = jnp.sqrt(jnp.sum(norm_tile) + jnp.sum(head_total * head_total))
+    _, hat_in, scale_in = layer_norm(inputs.astype(F32), vectors[0], vectors[3])
+    input_grad = residual_grad + grad_through_norm(total_grad, hat_in, scale_in, vectors[0])
+    vector_rows = model_vectors.shape[0]
+    head_row = vector_rows + hidden_vectors.shape[0] * hidden_width // width
+    vector_total = small_total[:vector_rows]
+    hidden_total = small_total[vector_rows:head_row].reshape(hidden_vectors.shape[0], hidden_width)
+    head_total = jnp.sum(small_total[head_row].reshape(heads_count, head_size), axis=1)
+    place = lax.axis_index("wide")
+    vector_part = lax.dynamic_slice_in_dim(
+        vector_total, place * model_vectors.shape[1], model_vectors.shape[1], 1
+    )
+    hidden_part = lax.dynamic_slice_in_dim(
+        hidden_total, place * hidden_vectors.shape[1], hidden_vectors.shape[1], 1
+    )
+    small_square = jnp.sum(small_total[:head_row] ** 2) + jnp.sum(head_total**2)
+    grad_norm = jnp.sqrt(jnp.sum(norm_tile) + small_square)
     factor = jnp.minimum(1.0, clip_limit / (grad_norm + 1e-06))
     step = step_count[0].astype(F32)
     grads = (qkv_part, out_part, fc1_part, fc2_part, vector_part, hidden_part, head_total)

time: 534 us -> 457 us (0.86)
  matrix products: 37.9 us -> 0 us
  other arithmetic: 49.3 us -> 25.2 us
  local copies, waits for them, and re-layouts: 22.5 us -> 12.5 us
    dot_general x9 -> x0, matrix products: 37.9 us -> none  [the longest x1 5.88 us: body(): jnp.einsum('te,de->td', query_grad, qkv_full[:, :width], preferred_elemen...]
    reduce_sum x11 -> x5, other arithmetic: 16.6 us -> 4.45 us  [the longest x1 1.52 us: body(): jnp.sum(small_total[:head_row] ** 2) + jnp.sum(head_total ** 2)]
    pallas_call x4 -> x3, Pallas kernels: 266 us -> 263 us  [the longest x1 187 us: back(): pl.pallas_call(functools.partial(back_kernel, pieces, sets, width // head...]
    unnamed x101 -> x70, local copies, waits for them, and re-layouts: 11.1 us -> 7.56 us
where the time goes in v4:
time: 457 us; the launch traced here: 449 us
  Pallas kernels  406 us (89%)
  other arithmetic  25.2 us (6%)
  local copies, waits for them, and re-layouts  12.5 us (3%)
  between operations  5.3 us (1%)
    pallas_call x1, Pallas kernels, back(): pl.pallas_call(functools.partial(back_kernel, pieces, sets, width // head...  187 us
    pallas_call x1, Pallas kernels, front(): pl.pallas_call(functools.partial(front_kernel, thirds, width // heads), o...  143 us
    pallas_call x1, Pallas kernels, middle_part(): pl.pallas_call(functools.partial(middle_kernel, width // heads), grid=(ro...  57 us
    pallas_call x1, Pallas kernels, weight_grads(): pl.pallas_call(weights_kernel, grid=(blocks,), in_specs=[whole] * 4 + [bl...  18.5 us
    sub x7, other arithmetic, adam_step(): weight_new = weight - rate * (direction + decay * weight)  10.8 us

profile of v4, /device:TPU:0, one launch (start us, length us, event | category | flops | bytes accessed | tf_op | source)
XLA Modules:
  0.0 448.5 jit_solution(4831345185937792095)
XLA Ops:
  0.7 1.0 reduce_window_sum.11
  2.4 0.7 convert_element_type.44
  3.1 0.7 reshape_reshape.6.refs_7_.scale_ref
  3.8 2.1 convert_element_type.42.refs_3_
  5.9 0.9 convert_element_type.43.refs_4_
  6.8 0.8 convert_element_type.40.refs_1_
  7.6 0.7 convert_element_type.41.refs_2_
  8.9 143.1 %front.1 = (bf16[16,64,3072]{2,1,0:T(8,128)(2,1)}, bf16[16,64,1024]{2,1,0:T(8,128)(2,1)}, bf16[16,1024,256]{2,1,0:T(8,128)(2,1)}, bf16[16,256,1024]{2,1,0:T(8,12...) custom-call(bf16[16,128]{1,0:T(8,128)(2,1)} %fusion.17.refs_0_, ...), custom_call_target="tpu_custom_call" | custom-call | tf_op jit(solution)/shard_map/front/pallas_call | solution.py:609
  152.0 57.0 %middle_part.1 = (bf16[512,1024]{1,0:T(8,128)(2,1)}, bf16[512,4096]{1,0:T(8,128)(2,1)}, bf16[512,4096]{1,0:T(8,128)(2,1)}, bf16[512,1024]{1,0:T(8,128)(2,1)}, bf...) custom-call(bf16[512,1024]{1,0:T(8,128)(2,1)} %get-tuple-element.58., ...), custom_call_target="tpu_custom_call" | custom-call | tf_op jit(solution)/shard_map/middle_part/pallas_call | solution.py:1275
  209.0 2.2 copy-done
  211.2 1.2 copy-done.4
  212.4 1.2 copy-done.5
  213.6 18.5 %weight_grads.1 = (bf16[16,1024,256]{2,1,0:T(8,128)(2,1)}, bf16[16,256,1024]{2,1,0:T(8,128)(2,1)}, bf16[1024,1024]{1,0:T(8,128)(2,1)S(1)}) custom-call(bf16[512,1024]{1,0:T(8,128)(2,1)S(1)} %copy-done.4, bf16[512,1024]{1,0:T(8,128)(2,1)S(1)} %copy-done.1, bf16[512,1024]{1,0:T(8,128)(2,1)S(1)} %copy-done.2, bf16[512,1024]{1,0:T(8,128)(2,1)S(1)} %copy-done.5, ...), custom_call_target="tpu_custom_call" | custom-call | tf_op jit(solution)/shard_map/weight_grads/pallas_call | solution.py:1324
  232.2 1.3 copy-done.3
  233.5 0.6 reshape.138.refs_12_
  234.2 187.0 %back.1 = (f32[1024,256]{1,0:T(8,128)}, f32[256,1024]{1,0:T(8,128)}, f32[64,1024]{1,0:T(8,128)}, f32[64,3072]{1,0:T(8,128)}, bf16[2,512,1024]{2,1,0:T(8,128)(2,1...) custom-call(bf16[4,2,2,1024,256]{4,3,2,1,0:T(8,128)(2,1)} %bitcast.24, ...), custom_call_target="tpu_custom_call" | custom-call | tf_op jit(solution)/shard_map/back/pallas_call | solution.py:1068
  421.2 0.8 slice_reduce_fusion
  422.2 0.6 multiply_reduce_fusion.1
  422.8 1.5 multiply_reduce_fusion
  425.6 1.3 reduce_sum.76
  428.9 0.8 slice.27
  429.8 0.6 multiply_subtract_fusion.5
  430.4 0.8 slice.26
  431.3 0.7 multiply_subtract_fusion.4
  432.0 3.9 multiply_subtract_fusion
  436.0 2.2 multiply_subtract_fusion.1
  438.2 1.0 multiply_subtract_fusion.3
  439.9 1.8 multiply_subtract_fusion.2
  441.7 0.9 slice.23
  443.4 0.9 fusion.20
  444.4 0.7 copy-done.10
  445.0 2.0 fusion.7
  (83 shorter events, 3.8 us)
Async XLA Ops:
  0.7 5.2 %copy-start.7 = (f32[256,1024]{1,0:T(8,128)S(1)}, f32[256,1024]{1,0:T(8,128)}, u32[]{:S(2)}) copy-start(f32[256,1024]{1,0:T(8,128)} %param.38) | copy-start | bytes 3145732
  0.7 6.1 %copy-start.9 = (f32[64,3072]{1,0:T(8,128)S(1)}, f32[64,3072]{1,0:T(8,128)}, u32[]{:S(2)}) copy-start(f32[64,3072]{1,0:T(8,128)} %param.29) | copy-start | bytes 2359300
  3.8 3.8 copy-start.17
  3.8 4.5 copy-start.26
  3.8 4.5 copy-start.27
  152.0 57.0 %copy-start.1 = (bf16[512,1024]{1,0:T(8,128)(2,1)S(1)}, bf16[512,1024]{1,0:T(8,128)(2,1)}, u32[]{:S(2)}) copy-start(bf16[512,1024]{1,0:T(8,128)(2,1)} %gy_ref.3) | copy-start | bytes 3145732
  152.0 57.0 %copy-start.2 = (bf16[512,1024]{1,0:T(8,128)(2,1)S(1)}, bf16[512,1024]{1,0:T(8,128)(2,1)}, u32[]{:S(2)}) copy-start(bf16[512,1024]{1,0:T(8,128)(2,1)} %get-tuple-element.58.c_ref) | copy-start | bytes 3145732
  209.0 2.2 copy-start
  213.6 19.8 %copy-start.25 = (f32[16,512]{1,0:T(8,128)S(1)}, f32[16,512]{1,0:T(8,128)}, u32[]{:S(2)}) copy-start(f32[16,512]{1,0:T(8,128)} %get-tuple-element.82) | copy-start | bytes 98308
  234.1 194.2 %copy-start.32 = (f32[16]{0:T(128)S(1)}, f32[16]{0:T(128)}, u32[]{:S(2)}) copy-start(f32[16]{0:T(128)} %param.47) | copy-start | bytes 196
  234.1 194.2 %copy-start.33 = (f32[16]{0:T(128)S(1)}, f32[16]{0:T(128)}, u32[]{:S(2)}) copy-start(f32[16]{0:T(128)} %param.49) | copy-start | bytes 196
  234.1 194.2 %copy-start.34 = (f32[16]{0:T(128)S(1)}, f32[16]{0:T(128)}, u32[]{:S(2)}) copy-start(f32[16]{0:T(128)} %param.48) | copy-start | bytes 196
  234.1 195.7 %copy-start.30 = (f32[3,256]{1,0:T(4,128)S(1)}, f32[3,256]{1,0:T(4,128)}, u32[]{:S(2)}) copy-start(f32[3,256]{1,0:T(4,128)} %param.46) | copy-start | bytes 9220
  234.1 195.7 %copy-start.31 = (f32[3,256]{1,0:T(4,128)S(1)}, f32[3,256]{1,0:T(4,128)}, u32[]{:S(2)}) copy-start(f32[3,256]{1,0:T(4,128)} %param.45) | copy-start | bytes 9220
  234.2 197.1 %copy-start.28 = (f32[10,64]{1,0:T(8,128)S(1)}, f32[10,64]{1,0:T(8,128)}, u32[]{:S(2)}) copy-start(f32[10,64]{1,0:T(8,128)} %param.43) | copy-start | bytes 7684
  234.2 197.1 %copy-start.29 = (f32[10,64]{1,0:T(8,128)S(1)}, f32[10,64]{1,0:T(8,128)}, u32[]{:S(2)}) copy-start(f32[10,64]{1,0:T(8,128)} %param.42) | copy-start | bytes 7684
  234.2 197.8 %copy-start.13 = (f32[256,1024]{1,0:T(8,128)S(1)}, f32[256,1024]{1,0:T(8,128)}, u32[]{:S(2)}) copy-start(f32[256,1024]{1,0:T(8,128)} %param.40) | copy-start | bytes 3145732
  432.0 3.9 copy-start.8
  432.0 3.9 copy-start.14
  432.0 3.9 copy-start.15
  432.0 3.9 copy-start.16
  436.0 2.3 copy-start.18
  436.0 2.2 copy-start.22
  436.0 2.2 copy-start.23
  436.0 2.2 copy-start.24
  436.0 3.2 copy-start.21
  438.2 1.4 copy-start.19
  438.2 1.7 copy-start.20
  439.9 2.7 copy-start.6
  439.9 3.4 copy-start.12
  441.7 1.8 copy-start.11
  443.4 1.6 copy-start.10
  (3 other events, 3.8 us)
